TPU v7x, 768 devices: a whole 4x8x12 slice. The times are simulated.
768 devices in a mesh: gx: 4 (over x), gy: 16 (over y, core), gz: 12 (over z).
Axes of the slice: x: 4, y: 8, z: 12, core: 2. Of those that a mesh axis runs over, the one named last changes fastest.
Arguments:
- drops: float32 [96, 256, 128, 128], P('gz', 'gx', 'gy'), may hold values from 0 to 1
- capture_efficiency_matrix: float32 [128, 128], replicated, may hold values from 0 to 0.015625
- transfer: float32 [128, 128], replicated, may hold values from 0 to 0.015625
- courant_u: float32 [96], P('gz'), may hold values from -0.45 to 0.45
- courant_v: float32 [96], P('gz'), may hold values from -0.45 to 0.45
- fall_class: int32 [128], replicated, may hold values from 0 to 2, as said below
- cloud_mask: int32 [256, 128], P('gx', 'gy'), may hold values from 0 to 1, as said below
Outputs:
- drops_out: float32 [96, 256, 128, 128], P('gz', 'gx', 'gy')
Inputs may be any that keep to these rules, and one draw needn't show every extreme that they name: `fall_class`: nondecreasing in the bin index; the first bin has 0 and the last 2. `cloud_mask`: each aligned tile of 64 x 8 columns (one device's) holds at most 256 cloudy columns, and some tile holds exactly 256.
All inputs are finite; a program needn't handle non-finite values.
Results may differ from a plain program's by a relative error of at most 0.0001.
Values sent between devices are 32-bit elements; how exact they have to be, the bound alone decides.
No kernel may reach another device: no remote copies, remote signals or barrier semaphores. Data moves between devices by JAX's collectives and lax.ppermute only.
A program may use at most 32 MiB of HBM per device.

v0:
```python
import jax
import jax.numpy as jnp
from jax import lax
from jax.sharding import PartitionSpec as P

H_MAX = 2
STEPS = 2


def passed_along(block, axis, distance):
    devices = range(lax.axis_size(axis))
    route = [(i - distance, i) for i in devices if i - distance in devices]
    return lax.ppermute(block, axis, route)


def with_halo(value, sides, width):
    edges = {}
    for axis, dim in sides:
        devices, length = (lax.axis_size(axis), value.shape[dim])
        up = [(i, (i + 1) % devices) for i in range(devices)]
        last = lax.slice_in_dim(value, length - width, length, axis=dim)
        leading = lax.slice_in_dim(value, 0, width, axis=dim)
        edges[dim] = (
            lax.ppermute(last, axis, up),
            lax.ppermute(leading, axis, [(b, a) for a, b in up]),
        )
    done = []
    for _, dim in sides:
        low, high = edges[dim]
        around = [(width, width) if d in done else (0, 0) for d in range(value.ndim)]
        value = jnp.concatenate([jnp.pad(low, around), value, jnp.pad(high, around)], axis=dim)
        done.append(dim)
    return value


def collide(particle_distribution, capture_efficiency_matrix, transfer, cloudy):
    merger_speed = jnp.einsum(
        "ugcr,mr->ugcm",
        particle_distribution,
        capture_efficiency_matrix,
        precision=lax.Precision.HIGHEST,
    )
    water_removed = particle_distribution * merger_speed
    mass_gain = jnp.einsum(
        "zxyi,ik->zxyk", water_removed, transfer, precision=lax.Precision.HIGHEST
    )
    return particle_distribution + cloudy[None, :, :, None] * (mass_gain - water_removed)


def advect(with_edges, courant_u, courant_v):
    centre = with_edges[:, 1:-1, 1:-1]
    west_side = with_edges[:, :-2, 1:-1]
    east_side = with_edges[:, 2:, 1:-1]
    south_side = with_edges[:, 1:-1, :-2]
    north_side = with_edges[:, 1:-1, 2:]
    x_plus = jnp.maximum(courant_u, 0.0)[:, None, None, None]
    x_minus = jnp.minimum(courant_u, 0.0)[:, None, None, None]
    northward_neighbor = jnp.maximum(courant_v, 0.0)[:, None, None, None]
    y_minus = jnp.minimum(courant_v, 0.0)[:, None, None, None]
    result = centre - x_plus * (centre - west_side) - x_minus * (east_side - centre)
    return result - northward_neighbor * (centre - south_side) - y_minus * (north_side - centre)


def sediment(padded, fall_class, levels):
    result = padded[:levels]
    for fall_depth in range(1, H_MAX + 1):
        result = jnp.where(
            (fall_class == fall_depth)[None, None, None, :],
            padded[fall_depth : fall_depth + levels],
            result,
        )
    return result


def on_device(
    drops, capture_efficiency_matrix, transfer, courant_u, courant_v, fall_class, cloud_mask
):
    cloudy = cloud_mask.astype(jnp.float32)
    reach = STEPS * H_MAX
    from_above, upper_u, upper_v = passed_along(
        (drops[:reach], courant_u[:reach], courant_v[:reach]), "gz", -1
    )
    particle_distribution = jnp.concatenate([drops, from_above], axis=0)
    column_u = jnp.concatenate([courant_u, upper_u], axis=0)
    column_v = jnp.concatenate([courant_v, upper_v], axis=0)
    for repeat in range(STEPS):
        current = particle_distribution.shape[0]
        coalesced_drops = collide(
            particle_distribution, capture_efficiency_matrix, transfer, cloudy
        )
        with_edges = with_halo(coalesced_drops, (("gx", 1), ("gy", 2)), 1)
        advected = advect(with_edges, column_u[:current], column_v[:current])
        particle_distribution = sediment(advected, fall_class, current - H_MAX)
    return particle_distribution


def solution(mesh):
    in_specs = (P("gz", "gx", "gy", None), P(), P(), P("gz"), P("gz"), P(), P("gx", "gy"))
    out_specs = P("gz", "gx", "gy", None)
    return jax.shard_map(
        on_device, mesh=mesh, in_specs=in_specs, out_specs=out_specs, check_vma=False
    )
```

profile of v0, /device:TPU:223, one launch (start us, length us, event | category | flops | bytes accessed | tf_op | source)
XLA Modules:
  0.0 73.9 jit_solution(2936493543115283079)
XLA Ops:
  0.0 2.4 %slice.89 = f32[4,64,8,128]{3,2,1,0:T(8,128)} slice(f32[8,64,8,128]{3,2,1,0:T(8,128)} %param.7), slice={[0:4], [0:64], [0:8], [0:128]} | slice | bytes 2097152 | tf_op jit(solution)/shard_map/slice | solution.py:81
  2.4 2.0 %collective-permute-start = (f32[4,64,8,128]{3,2,1,0:T(8,128)}, f32[4,64,8,128]{3,2,1,0:T(8,128)S(1)}, u32[]{:S(2)}, u32[]{:S(2)}) collective-permute-start(f32[4,64,8,128]{3,2,1,0:T(8,128)} %slice.89), channel_id=1, source_target_pairs={{1,0},{2,1},{3,2},{4,3},{5,4},{6,5},{7,6},{8,7},{9,8},{10,9},{11,1... | collective-permute-start | bytes 3145736 | tf_op jit(solution)/shard_map/ppermute | solution.py:13
  4.5 1.9 %collective-permute-start.4 = (f32[4]{0:T(128)}, f32[4]{0:T(128)S(1)}, u32[]{:S(2)}, u32[]{:S(2)}) collective-permute-start(f32[4]{0:T(128)} %bitcast.18), channel_id=1, source_target_pairs={{1,0},{2,1},{3,2},{4,3},{5,4},{6,5},{7,6},{8,7},{9,8},{10,9},{11,1... | collective-permute-start | bytes 56 | tf_op jit(solution)/shard_map/ppermute | solution.py:13
  6.4 1.9 %collective-permute-start.1 = (f32[4]{0:T(128)}, f32[4]{0:T(128)S(1)}, u32[]{:S(2)}, u32[]{:S(2)}) collective-permute-start(f32[4]{0:T(128)} %bitcast.19), channel_id=1, source_target_pairs={{1,0},{2,1},{3,2},{4,3},{5,4},{6,5},{7,6},{8,7},{9,8},{10,9},{11,1... | collective-permute-start | bytes 56 | tf_op jit(solution)/shard_map/ppermute | solution.py:13
  8.3 0.7 convert_element_type.9
  9.0 0.1 copy.8
  9.1 0.1 constant_dynamic-update-slice_fusion.1
  9.3 21.6 %collective-permute-done.4 = f32[4]{0:T(128)S(1)} collective-permute-done((f32[4]{0:T(128)}, f32[4]{0:T(128)S(1)}, u32[]{:S(2)}, u32[]{:S(2)}) %collective-permute-start.4) | collective-permute-done | bytes 48 | tf_op jit(solution)/shard_map/ppermute | solution.py:13
  30.8 0.1 broadcast_maximum_fusion
  30.9 0.0 collective-permute-done.1
  30.9 0.1 broadcast_maximum_fusion.1
  31.0 0.1 constant_dynamic-update-slice_fusion
  31.1 0.0 copy-start.2
  31.1 2.7 %fusion.36 = f32[12,64,8,128]{3,2,1,0:T(8,128)S(1)} fusion(f32[12,64,8,128]{3,2,1,0:T(8,128)S(1)} %constant_dynamic-update-slice_fusion, f32[128,128]{1,0:T(8,128)S(1)} %copy-done), kind=kOutput, calls=%fused_computation.60 | convolution fusion | flops 1207959552 | bytes 6356992 | tf_op jit(solution)/shard_map/ugcr,mr->ugcm/dot_general | solution.py:37
  33.9 3.1 %multiply_add_fusion = f32[12,64,8,128]{3,2,1,0:T(8,128)S(1)} fusion(f32[12,64,8,128]{3,2,1,0:T(8,128)S(1)} %constant_dynamic-update-slice_fusion, f32[12,64,8,128]{3,2,1,0:T(8,128)S(1)} %fusion.36, f32[64,8]{1,0:T(8,128)S(1)} %copy.8, f32[128,128]{1,0:T(8,128)S(1)} %copy-done.2), kind=kOutput, calls=%fused_computation.24 | convolution fusion | flops 1211105280 | bytes 9504768 | tf_op jit(solution)/shard_map/zxyi,ik->zxyk/dot_general | solution.py:44
  37.0 0.7 fusion.38
  37.7 3.7 %collective-permute-start.5 = (f32[12,64,1,128]{3,2,1,0:T(1,128)S(1)}, f32[12,64,1,128]{3,2,1,0:T(1,128)S(1)}, u32[]{:S(2)}, u32[]{:S(2)}) collective-permute-start(f32[12,64,1,128]{3,2,1,0:T(1,128)S(1)} %get-tuple-element.9), channel_id=1, source_target_pairs={{0,12},{12,24},{24,36},{36,48},{48,60},{60,72},{72,84},{84,96},{96... | collective-permute-start | bytes 1179656 | tf_op jit(solution)/shard_map/ppermute | solution.py:24
  41.4 2.1 %collective-permute-start.2 = (f32[12,1,8,128]{3,2,1,0:T(8,128)S(1)}, f32[12,1,8,128]{3,2,1,0:T(8,128)S(1)}, u32[]{:S(2)}, u32[]{:S(2)}) collective-permute-start(f32[12,1,8,128]{3,2,1,0:T(8,128)S(1)} %get-tuple-element.11), channel_id=1, source_target_pairs={{0,192},{192,384},{384,576},{576,0},{1,193},{193,385},{385,577},{5... | collective-permute-start | bytes 147464 | tf_op jit(solution)/shard_map/ppermute | solution.py:24
  43.5 3.4 %collective-permute-start.3 = (f32[12,1,8,128]{3,2,1,0:T(8,128)S(1)}, f32[12,1,8,128]{3,2,1,0:T(8,128)S(1)}, u32[]{:S(2)}, u32[]{:S(2)}) collective-permute-start(f32[12,1,8,128]{3,2,1,0:T(8,128)S(1)} %get-tuple-element.12), channel_id=1, source_target_pairs={{192,0},{384,192},{576,384},{0,576},{193,1},{385,193},{577,385},{1... | collective-permute-start | bytes 147464 | tf_op jit(solution)/shard_map/ppermute | solution.py:25
  46.9 3.4 %collective-permute-done.3 = f32[12,1,8,128]{3,2,1,0:T(8,128)S(1)} collective-permute-done((f32[12,1,8,128]{3,2,1,0:T(8,128)S(1)}, f32[12,1,8,128]{3,2,1,0:T(8,128)S(1)}, u32[]{:S(2)}, u32[]{:S(2)}) %collective-permute-start.3) | collective-permute-done | bytes 49184 | tf_op jit(solution)/shard_map/ppermute | solution.py:25
  50.3 2.7 %fusion.3 = f32[12,64,8,128]{3,2,1,0:T(8,128)S(1)} fusion(f32[12,64,8,128]{3,2,1,0:T(8,128)S(1)} %multiply_add_fusion, f32[12,64,1,128]{3,2,1,0:T(1,128)S(1)} %collective-permute-done.6, f32[12,1,8,128]{3,2,1,0:T(8,128)S(1)} %collective-permute-done.3, f32[12,1,8,128]{3,2,1,0:T(8,128)S(1)} %collective-permute-done.2, ...), kind=kLoop, calls=%fused_computation.4 | loop fusion | flops 20447232 | bytes 7176384 | tf_op jit(solution)/shard_map/sub | solution.py:61
  53.0 0.2 fusion.28
  53.3 2.2 %fusion.34 = f32[10,64,8,128]{3,2,1,0:T(8,128)S(1)} fusion(f32[10,64,8,128]{3,2,1,0:T(8,128)S(1)} %fusion.28, f32[128,128]{1,0:T(8,128)S(1)} %copy-done), kind=kOutput, calls=%fused_computation.58 | convolution fusion | flops 1006632960 | bytes 5308416 | tf_op jit(solution)/shard_map/ugcr,mr->ugcm/dot_general | solution.py:37
  55.5 2.5 %multiply_add_fusion.1 = f32[10,64,8,128]{3,2,1,0:T(8,128)S(1)} fusion(f32[10,64,8,128]{3,2,1,0:T(8,128)S(1)} %fusion.28, f32[10,64,8,128]{3,2,1,0:T(8,128)S(1)} %fusion.34, f32[64,8]{1,0:T(8,128)S(1)} %copy.8, f32[128,128]{1,0:T(8,128)S(1)} %copy-done.2), kind=kOutput, calls=%fused_computation.51 | convolution fusion | flops 1009254400 | bytes 7931904 | tf_op jit(solution)/shard_map/zxyi,ik->zxyk/dot_general | solution.py:44
  58.0 0.5 fusion.40
  58.5 0.5 collective-permute-start.10
  59.0 3.2 %collective-permute-start.9 = (f32[10,64,1,128]{3,2,1,0:T(1,128)S(1)}, f32[10,64,1,128]{3,2,1,0:T(1,128)S(1)}, u32[]{:S(2)}, u32[]{:S(2)}) collective-permute-start(f32[10,64,1,128]{3,2,1,0:T(1,128)S(1)} %get-tuple-element.13), channel_id=1, source_target_pairs={{0,12},{12,24},{24,36},{36,48},{48,60},{60,72},{72,84},{84,96},{96... | collective-permute-start | bytes 983048 | tf_op jit(solution)/shard_map/ppermute | solution.py:24
  62.2 1.9 %collective-permute-start.7 = (f32[10,1,8,128]{3,2,1,0:T(8,128)S(1)}, f32[10,1,8,128]{3,2,1,0:T(8,128)S(1)}, u32[]{:S(2)}, u32[]{:S(2)}) collective-permute-start(f32[10,1,8,128]{3,2,1,0:T(8,128)S(1)} %get-tuple-element.15), channel_id=1, source_target_pairs={{0,192},{192,384},{384,576},{576,0},{1,193},{193,385},{385,577},{5... | collective-permute-start | bytes 122888 | tf_op jit(solution)/shard_map/ppermute | solution.py:24
  64.1 3.4 %collective-permute-start.8 = (f32[10,1,8,128]{3,2,1,0:T(8,128)S(1)}, f32[10,1,8,128]{3,2,1,0:T(8,128)S(1)}, u32[]{:S(2)}, u32[]{:S(2)}) collective-permute-start(f32[10,1,8,128]{3,2,1,0:T(8,128)S(1)} %get-tuple-element.16), channel_id=1, source_target_pairs={{192,0},{384,192},{576,384},{0,576},{193,1},{385,193},{577,385},{1... | collective-permute-start | bytes 122888 | tf_op jit(solution)/shard_map/ppermute | solution.py:25
  67.5 2.6 %collective-permute-done.8 = f32[10,1,8,128]{3,2,1,0:T(8,128)S(1)} collective-permute-done((f32[10,1,8,128]{3,2,1,0:T(8,128)S(1)}, f32[10,1,8,128]{3,2,1,0:T(8,128)S(1)}, u32[]{:S(2)}, u32[]{:S(2)}) %collective-permute-start.8) | collective-permute-done | bytes 40992 | tf_op jit(solution)/shard_map/ppermute | solution.py:25
  70.1 2.3 %fusion.17 = f32[10,64,8,128]{3,2,1,0:T(8,128)S(1)} fusion(f32[10,64,8,128]{3,2,1,0:T(8,128)S(1)} %multiply_add_fusion.1, f32[10,64,1,128]{3,2,1,0:T(1,128)S(1)} %collective-permute-done.10, f32[10,1,8,128]{3,2,1,0:T(8,128)S(1)} %collective-permute-done.8, f32[10,1,8,128]{3,2,1,0:T(8,128)S(1)} %collective-permute-done.7, ...), kind=kLoop, calls=%fused_computation.29 | loop fusion | flops 17039360 | bytes 5980320 | tf_op jit(solution)/shard_map/sub | solution.py:61
  72.4 1.5 %fusion.30 = f32[8,64,8,128]{3,2,1,0:T(8,128)} fusion(f32[10,64,8,128]{3,2,1,0:T(8,128)S(1)} %fusion.17, pred[128]{0:T(512)(128)(4,1)S(1)} %get-tuple-element.22, pred[128]{0:T(512)(128)(4,1)S(1)} %get-tuple-element.21), kind=kLoop, calls=%fused_computation.54 | loop fusion | flops 1048576 | bytes 8388864 | tf_op jit(solution)/shard_map/jit(_where)/select_n | solution.py:67
  (25 shorter events, 0.1 us)
Async XLA Ops:
  0.0 31.1 %copy-start = (f32[128,128]{1,0:T(8,128)S(1)}, f32[128,128]{1,0:T(8,128)}, u32[]{:S(2)}) copy-start(f32[128,128]{1,0:T(8,128)} %param.8) | copy-start | bytes 196612
  0.0 9.1 %copy-start.1 = (f32[8,64,8,128]{3,2,1,0:T(8,128)S(1)}, f32[8,64,8,128]{3,2,1,0:T(8,128)}, u32[]{:S(2)}) copy-start(f32[8,64,8,128]{3,2,1,0:T(8,128)} %param.7) | copy-start | bytes 6291460
  2.4 6.8 %copy-start.5 = (s32[128]{0:T(128)S(1)}, s32[128]{0:T(128)}, u32[]{:S(2)}) copy-start(s32[128]{0:T(128)} %param.12) | copy-start | bytes 1540
  2.4 28.4 %copy-start.3 = (f32[8]{0:T(128)S(1)}, f32[8]{0:T(128)}, u32[]{:S(2)}) copy-start(f32[8]{0:T(128)} %param.11) | copy-start | bytes 100
  2.4 28.5 %copy-start.4 = (f32[8]{0:T(128)S(1)}, f32[8]{0:T(128)}, u32[]{:S(2)}) copy-start(f32[8]{0:T(128)} %param.10) | copy-start | bytes 100
  2.4 28.6 %collective-permute-start = (f32[4,64,8,128]{3,2,1,0:T(8,128)}, f32[4,64,8,128]{3,2,1,0:T(8,128)S(1)}, u32[]{:S(2)}, u32[]{:S(2)}) collective-permute-start(f32[4,64,8,128]{3,2,1,0:T(8,128)} %slice.89), channel_id=1, source_target_pairs={{1,0},{2,1},{3,2},{4,3},{5,4},{6,5},{7,6},{8,7},{9,8},{10,9},{11,1... | collective-permute-start | bytes 3145736 | tf_op jit(solution)/shard_map/ppermute | solution.py:13
  4.5 26.4 %collective-permute-start.4 = (f32[4]{0:T(128)}, f32[4]{0:T(128)S(1)}, u32[]{:S(2)}, u32[]{:S(2)}) collective-permute-start(f32[4]{0:T(128)} %bitcast.18), channel_id=1, source_target_pairs={{1,0},{2,1},{3,2},{4,3},{5,4},{6,5},{7,6},{8,7},{9,8},{10,9},{11,1... | collective-permute-start | bytes 56 | tf_op jit(solution)/shard_map/ppermute | solution.py:13
  6.4 24.5 %collective-permute-start.1 = (f32[4]{0:T(128)}, f32[4]{0:T(128)S(1)}, u32[]{:S(2)}, u32[]{:S(2)}) collective-permute-start(f32[4]{0:T(128)} %bitcast.19), channel_id=1, source_target_pairs={{1,0},{2,1},{3,2},{4,3},{5,4},{6,5},{7,6},{8,7},{9,8},{10,9},{11,1... | collective-permute-start | bytes 56 | tf_op jit(solution)/shard_map/ppermute | solution.py:13
  31.1 2.8 %copy-start.2 = (f32[128,128]{1,0:T(8,128)S(1)}, f32[128,128]{1,0:T(8,128)}, u32[]{:S(2)}) copy-start(f32[128,128]{1,0:T(8,128)} %param.9) | copy-start | bytes 196612
  37.7 12.6 %collective-permute-start.5 = (f32[12,64,1,128]{3,2,1,0:T(1,128)S(1)}, f32[12,64,1,128]{3,2,1,0:T(1,128)S(1)}, u32[]{:S(2)}, u32[]{:S(2)}) collective-permute-start(f32[12,64,1,128]{3,2,1,0:T(1,128)S(1)} %get-tuple-element.9), channel_id=1, source_target_pairs={{0,12},{12,24},{24,36},{36,48},{48,60},{60,72},{72,84},{84,96},{96... | collective-permute-start | bytes 1179656 | tf_op jit(solution)/shard_map/ppermute | solution.py:24
  41.4 8.9 %collective-permute-start.6 = (f32[12,64,1,128]{3,2,1,0:T(1,128)S(1)}, f32[12,64,1,128]{3,2,1,0:T(1,128)S(1)}, u32[]{:S(2)}, u32[]{:S(2)}) collective-permute-start(f32[12,64,1,128]{3,2,1,0:T(1,128)S(1)} %get-tuple-element.10), channel_id=1, source_target_pairs={{12,0},{24,12},{36,24},{48,36},{60,48},{72,60},{84,72},{96,84},{10... | collective-permute-start | bytes 1179656 | tf_op jit(solution)/shard_map/ppermute | solution.py:25
  41.4 5.5 %collective-permute-start.2 = (f32[12,1,8,128]{3,2,1,0:T(8,128)S(1)}, f32[12,1,8,128]{3,2,1,0:T(8,128)S(1)}, u32[]{:S(2)}, u32[]{:S(2)}) collective-permute-start(f32[12,1,8,128]{3,2,1,0:T(8,128)S(1)} %get-tuple-element.11), channel_id=1, source_target_pairs={{0,192},{192,384},{384,576},{576,0},{1,193},{193,385},{385,577},{5... | collective-permute-start | bytes 147464 | tf_op jit(solution)/shard_map/ppermute | solution.py:24
  43.5 6.8 %collective-permute-start.3 = (f32[12,1,8,128]{3,2,1,0:T(8,128)S(1)}, f32[12,1,8,128]{3,2,1,0:T(8,128)S(1)}, u32[]{:S(2)}, u32[]{:S(2)}) collective-permute-start(f32[12,1,8,128]{3,2,1,0:T(8,128)S(1)} %get-tuple-element.12), channel_id=1, source_target_pairs={{192,0},{384,192},{576,384},{0,576},{193,1},{385,193},{577,385},{1... | collective-permute-start | bytes 147464 | tf_op jit(solution)/shard_map/ppermute | solution.py:25
  58.5 11.6 %collective-permute-start.10 = (f32[10,64,1,128]{3,2,1,0:T(1,128)S(1)}, f32[10,64,1,128]{3,2,1,0:T(1,128)S(1)}, u32[]{:S(2)}, u32[]{:S(2)}) collective-permute-start(f32[10,64,1,128]{3,2,1,0:T(1,128)S(1)} %get-tuple-element.14), channel_id=1, source_target_pairs={{12,0},{24,12},{36,24},{48,36},{60,48},{72,60},{84,72},{96,84},{10... | collective-permute-start | bytes 983048 | tf_op jit(solution)/shard_map/ppermute | solution.py:25
  59.0 11.1 %collective-permute-start.9 = (f32[10,64,1,128]{3,2,1,0:T(1,128)S(1)}, f32[10,64,1,128]{3,2,1,0:T(1,128)S(1)}, u32[]{:S(2)}, u32[]{:S(2)}) collective-permute-start(f32[10,64,1,128]{3,2,1,0:T(1,128)S(1)} %get-tuple-element.13), channel_id=1, source_target_pairs={{0,12},{12,24},{24,36},{36,48},{48,60},{60,72},{72,84},{84,96},{96... | collective-permute-start | bytes 983048 | tf_op jit(solution)/shard_map/ppermute | solution.py:24
  62.2 5.3 %collective-permute-start.7 = (f32[10,1,8,128]{3,2,1,0:T(8,128)S(1)}, f32[10,1,8,128]{3,2,1,0:T(8,128)S(1)}, u32[]{:S(2)}, u32[]{:S(2)}) collective-permute-start(f32[10,1,8,128]{3,2,1,0:T(8,128)S(1)} %get-tuple-element.15), channel_id=1, source_target_pairs={{0,192},{192,384},{384,576},{576,0},{1,193},{193,385},{385,577},{5... | collective-permute-start | bytes 122888 | tf_op jit(solution)/shard_map/ppermute | solution.py:24
  64.1 6.0 %collective-permute-start.8 = (f32[10,1,8,128]{3,2,1,0:T(8,128)S(1)}, f32[10,1,8,128]{3,2,1,0:T(8,128)S(1)}, u32[]{:S(2)}, u32[]{:S(2)}) collective-permute-start(f32[10,1,8,128]{3,2,1,0:T(8,128)S(1)} %get-tuple-element.16), channel_id=1, source_target_pairs={{192,0},{384,192},{576,384},{0,576},{193,1},{385,193},{577,385},{1... | collective-permute-start | bytes 122888 | tf_op jit(solution)/shard_map/ppermute | solution.py:25
where the time goes:
time: 74.2 us; the launch traced here: 73.9 us
  waiting for transfers between devices  27.5 us (37%)
  starting transfers between devices  24 us (32%)
  matrix products  10.5 us (14%)
  other arithmetic  7.62 us (10%)
  local copies, waits for them, and re-layouts  3.99 us (5%)
    ppermute x3, waiting for transfers between devices, passed_along(): return lax.ppermute(block, axis, route)  21.6 us
    ppermute x4, starting transfers between devices, with_halo(): lax.ppermute(last, axis, up)  10.9 us
    ppermute x4, starting transfers between devices, with_halo(): lax.ppermute(leading, axis, [(b, a) for a, b in up])  7.21 us
    ppermute x4, waiting for transfers between devices, with_halo(): lax.ppermute(leading, axis, [(b, a) for a, b in up])  5.96 us
    ppermute x3, starting transfers between devices, passed_along(): return lax.ppermute(block, axis, route)  5.88 us
    dot_general x2, matrix products, collide(): jnp.einsum('zxyi,ik->zxyk', water_removed, transfer, precision=lax.Precis...  5.55 us
    sub x2, other arithmetic, advect(): result - northward_neighbor * (centre - south_side)  5 us
    dot_general x2, matrix products, collide(): jnp.einsum('ugcr,mr->ugcm', particle_distribution, capture_efficiency_mat...  4.94 us
  transfers between devices with their start and end apart: 11, of which 3 were waited for; matrix products, arithmetic and copies ran while one was open for 1% of the time, Pallas kernels for 0%

commit v1 on v0

v1 whole, which is shorter than its diff:
```python
import functools

import jax
import jax.numpy as jnp
from jax import lax
from jax.experimental import pallas as pl
from jax.experimental.pallas import tpu as pltpu
from jax.sharding import PartitionSpec as P

H_MAX = 2
Z, X, Y, B = 8, 64, 8, 128
T = 8
XW = X + 4
XA = X + 2
HALO = 2 * X * Z
XROWS = 2 * Z * Y
F32, BF16 = jnp.float32, jnp.bfloat16

VMEM = pl.BlockSpec(memory_space=pltpu.VMEM)
SMEM = pl.BlockSpec(memory_space=pltpu.SMEM)
ANY = pl.BlockSpec(memory_space=pl.ANY)


def rows(start, n=T):
    return pl.ds(start if isinstance(start, int) else pl.multiple_of(start, T), n)


def call(body, outs, args, specs, scratch=(), cost=(0, 0), out_specs=None, aliases=None):
    shapes = [pltpu.VMEM(s, d) if m else jax.ShapeDtypeStruct(s, d) for s, d, m in outs]
    args = [
        pltpu.with_memory_space_constraint(a, pltpu.VMEM) if s is VMEM else a
        for a, s in zip(args, specs)
    ]
    return pl.pallas_call(
        body,
        out_shape=shapes,
        in_specs=list(specs),
        out_specs=out_specs or [VMEM] * len(outs),
        scratch_shapes=list(scratch),
        input_output_aliases=aliases or {},
        cost_estimate=pl.CostEstimate(flops=cost[0], bytes_accessed=cost[1], transcendentals=0),
        compiler_params=pltpu.CompilerParams(vmem_limit_bytes=40 << 20),
    )(*args)


def split(x):
    high = x.astype(BF16)
    return high, (x - high.astype(F32)).astype(BF16)


def product(x, weights):
    out = jnp.dot(jnp.concatenate(split(x), axis=1), weights, preferred_element_type=F32)
    return out[:, :B] + out[:, B:]


def collide(s, cloudy, capture, transfer):
    loss = s * product(s, capture)
    return s + cloudy * (product(loss, transfer) - loss)


def eightfold(ref, row):
    return ref[pl.ds(row, T, stride=0), :]


def repeated(ref, start, n):
    return jnp.concatenate([eightfold(ref, start + i) for i in range(n)], axis=0)


def classes(sc_ref):
    lane = lax.broadcasted_iota(jnp.int32, (T, B), 1)
    return lane < sc_ref[0], lane >= sc_ref[1]


def fall(c0, c2, a, b, c):
    return jnp.where(c0, a, jnp.where(c2, c, b))


def edges_body(drops, cloudy, k_ref, t_ref, own, xm, xp, ym, yp, kk, tt, sem):
    copy = pltpu.make_async_copy(drops, own, sem)
    copy.start()
    for ref, out, turned in ((k_ref, kk, True), (t_ref, tt, False)):
        w = ref[...].T if turned else ref[...]
        high, low = split(w)
        half = jnp.concatenate([high, low], axis=1)
        out[...] = jnp.concatenate([half, half], axis=0)
    for out, cols in ((xm, (0, 1)), (xp, (X - 1, X - 2))):
        for d, x in enumerate(cols):
            out[XROWS + d * Y : XROWS + d * Y + Y] = cloudy[x * Y : x * Y + Y]
    for out, ys in ((ym, (0, 1)), (yp, (Y - 1, Y - 2))):
        for d, y in enumerate(ys):
            out[HALO + d * X : HALO + d * X + X] = cloudy[pl.ds(y, X, stride=Y), :]
    copy.wait()
    for out, cols in ((xm, (0, 1)), (xp, (X - 1, X - 2))):
        for d, x in enumerate(cols):
            for z in range(Z):
                at = (z * X + x) * Y
                out[(d * Z + z) * Y : (d * Z + z + 1) * Y] = own[at : at + Y]
    for out, ys in ((ym, (0, 1)), (yp, (Y - 1, Y - 2))):
        for d, y in enumerate(ys):
            for x in range(X):
                at = (d * X + x) * Z
                out[at : at + Z] = own[pl.ds(x * Y + y, Z, stride=X * Y), :]


def corners_body(left, right, up, down):
    for out, y in ((up, Y - 1), (down, 0)):
        out[...] = jnp.zeros_like(out)
        for i, ref in enumerate((left, right)):
            out[i * Z : (i + 1) * Z] = ref[pl.ds(y, Z, stride=Y), :]
            out[2 * Z + i : 2 * Z + i + 1] = ref[XROWS + y : XROWS + y + 1]


def cy_at(side, d, x):
    return ((side * 2 + d) * XA + x + 1) * Z


def first_body(own, cloudy, left, right, south, north, kk, tt, c1, cy, m1, my):
    k, t = kk[...], tt[...]

    def level(z, _):
        c1[rows((z * XW + 2) * Y, X * Y)] = collide(own[rows(z * X * Y, X * Y)], cloudy[...], k, t)
        return 0

    lax.fori_loop(0, Z, level, 0)
    m1[0:Y] = left[XROWS : XROWS + Y]
    m1[Y : Y + X * Y] = cloudy[...]
    m1[Y + X * Y :] = right[XROWS : XROWS + Y]
    for ref, at in ((left, (1, 0)), (right, (XW - 2, XW - 1))):
        mask = jnp.concatenate(
            [ref[XROWS + d * Y : XROWS + d * Y + Y] for d in range(2) for _ in range(Z)], axis=0
        )
        c = collide(ref[0:XROWS], mask, k, t)
        for d in range(2):
            for z in range(Z):
                to = (z * XW + at[d]) * Y
                c1[to : to + Y] = c[(d * Z + z) * Y : (d * Z + z + 1) * Y]
    for side, ref in enumerate((south, north)):
        for d in range(2):
            mask = repeated(ref, HALO + d * X, X)
            if d == 0:
                my[side * X * Z : (side + 1) * X * Z] = mask
            at = cy_at(side, d, 0)
            cy[at : at + X * Z] = collide(ref[d * X * Z : (d + 1) * X * Z], mask, k, t)


def advect_level(z, c_ref, width, first, count, out_ref, out_width, edge, u_ref, v_ref):
    u, v = u_ref[z], v_ref[z]
    au, av = jnp.abs(u), jnp.abs(v)
    shift = jnp.where(v > 0, 1, T - 1)
    side = jnp.where(v > 0, 0, 1)
    at_edge = lax.broadcasted_iota(jnp.int32, (T, B), 0) == jnp.where(v > 0, 0, T - 1)
    base = (z * width + first) * Y
    base_x = base + jnp.where(u > 0, -Y, Y)
    base_out = z * out_width * Y
    edge_ref, edge_at, edge_stride = edge(side)
    for i in range(count):
        c = c_ref[rows(base + i * Y)]
        x = c_ref[rows(base_x + i * Y)]
        e = eightfold(edge_ref, edge_at + i * edge_stride)
        y = jnp.where(at_edge, e, pltpu.roll(c, shift, 0))
        out_ref[rows(base_out + i * Y)] = c - au * (c - x) - av * (c - y)


def second_body(
    sc, u_ref, v_ref, ub, vb, c1_in, cy_in, cs, cn, kk, tt, m1, my, a1, a1y, c2, c2y, a2, pay, cy
):
    k, t = kk[...], tt[...]
    c0, cc2 = classes(sc)
    cy[...] = cy_in[...]
    for side, ref in enumerate((cs, cn)):
        mask = repeated(ref, 2 * Z, 2)
        c = collide(ref[0 : 2 * Z], mask, k, t)
        for i, x in enumerate((-1, X)):
            at = cy_at(side, 0, x)
            cy[at : at + Z] = c[i * Z : (i + 1) * Z]

    def edge1(z):
        return lambda side: (cy, side * (2 * XA * Z) + z, Z)

    def adv1(z, _):
        advect_level(z, c1_in, XW, 1, XA, a1, XA, edge1(z), u_ref, v_ref)
        return 0

    lax.fori_loop(0, 4, adv1, 0)
    au, av = jnp.abs(ub[...]), jnp.abs(vb[...])
    upos, vpos = ub[...] > 0, vb[...] > 0
    for side in range(2):
        for x in range(X):
            at = cy_at(side, 0, x)
            far = cy_at(side, 1, x)
            c = cy[at : at + Z]
            xx = jnp.where(upos, cy[at - Z : at], cy[at + Z : at + 2 * Z])
            outer = cy[far : far + Z]
            inner = c1_in[pl.ds((x + 2) * Y + (Y - 1) * side, Z, stride=XW * Y), :]
            yy = jnp.where(vpos, *((outer, inner) if side == 0 else (inner, outer)))
            a = c - au * (c - xx) - av * (c - yy)
            to = (side * X + x) * Z
            a1y[to : to + Z] = a
            c2y[to : to + Z] = fall(c0, cc2, a, pltpu.roll(a, Z - 1, 0), pltpu.roll(a, Z - 2, 0))
    for i in range(2):
        at = rows(i * X * Z, X * Z)
        c2y[at] = collide(c2y[at], my[at], k, t)
    settle_collide(0, 2, c0, cc2, a1, m1, c2, k, t)

    def adv2(z, _):
        advect_level(z, c2, XA, 1, X, a2, X, lambda side: (c2y, side * (X * Z) + z, Z), u_ref, v_ref)
        return 0

    lax.fori_loop(0, 2, adv2, 0)
    for i in range(XA):
        l0, l1 = a1[i * T : (i + 1) * T], a1[(XA + i) * T : (XA + i + 1) * T]
        pay[i * T : (i + 1) * T] = fall(c0, cc2, l0, l0, l1)
        pay[(NT + i) * T : (NT + i + 1) * T] = l0
    for i in range(2 * X // T):
        at = i * T * Z
        l0, l1 = a1y[pl.ds(at, T, stride=Z), :], a1y[pl.ds(at + 1, T, stride=Z), :]
        j = XA + i
        pay[j * T : (j + 1) * T] = fall(c0, cc2, l0, l0, l1)
        pay[(NT + j) * T : (NT + j + 1) * T] = l0
    for i in range(X):
        l0, l1 = a2[i * T : (i + 1) * T], a2[(X + i) * T : (X + i + 1) * T]
        j = XA + 2 * X // T + i
        pay[j * T : (j + 1) * T] = fall(c0, cc2, l0, l0, l1)
        pay[(NT + j) * T : (NT + j + 1) * T] = l0


NT = XA + 2 * X // T + X


def settle_collide(lo, hi, c0, cc2, a1, m1, c2, k, t):
    def level(z, _):
        for i in range(XA):
            at = (z * XA + i) * T
            c2[rows(at)] = fall(
                c0, cc2, a1[rows(at)], a1[rows(at + XA * T)], a1[rows(at + 2 * XA * T)]
            )
        at = rows(z * XA * T, XA * T)
        c2[at] = collide(c2[at], m1[...], k, t)
        return 0

    lax.fori_loop(lo, hi, level, 0)


def third_body(sc, u_ref, v_ref, c1, cy, a1_in, c2_in, c2y, a2_in, kk, tt, m1, a1_hi, a2_hi, out, a1, c2, a2, c2b, sem):
    k, t = kk[...], tt[...]
    c0, cc2 = classes(sc)
    a1[0 : 4 * XA * T] = a1_in[...]
    c2[0 : 2 * XA * T] = c2_in[...]
    a2[0 : 2 * X * T] = a2_in[...]

    def adv1(z, _):
        advect_level(
            z, c1, XW, 1, XA, a1, XA, lambda side: (cy, side * (2 * XA * Z) + z, Z), u_ref, v_ref
        )
        return 0

    lax.fori_loop(4, 8, adv1, 0)
    settle_collide(2, 6, c0, cc2, a1, m1, c2, k, t)

    def adv2(z, _):
        advect_level(z, c2, XA, 1, X, a2, X, lambda side: (c2y, side * (X * Z) + z, Z), u_ref, v_ref)
        return 0

    lax.fori_loop(2, 6, adv2, 0)

    def done(z, _):
        for i in range(X):
            at = (z * X + i) * T
            c2b[rows(at)] = fall(
                c0, cc2, a2[rows(at)], a2[rows(at + X * T)], a2[rows(at + 2 * X * T)]
            )
        return 0

    lax.fori_loop(0, 4, done, 0)
    copy = pltpu.make_async_copy(c2b, out.at[pl.ds(0, 4 * X * T)], sem)
    copy.start()
    a1_hi[...] = a1[6 * XA * T : 8 * XA * T]
    a2_hi[...] = a2[4 * X * T : 6 * X * T]
    copy.wait()


def last_body(sc, u_ref, v_ref, a1_hi, a1y, a2_hi, south, north, kk, tt, m1, pay, out_in, out, c2, c2y, a2, res, sem):
    k, t = kk[...], tt[...]
    c0, cc2 = classes(sc)
    c0w = lax.broadcasted_iota(jnp.int32, (T, B), 1) < sc[0]
    for i in range(XA):
        p7 = pay[i * T : (i + 1) * T]
        p6 = pay[(NT + i) * T : (NT + i + 1) * T]
        x6, x7 = a1_hi[i * T : (i + 1) * T], a1_hi[(XA + i) * T : (XA + i + 1) * T]
        c2[i * T : (i + 1) * T] = fall(c0, cc2, x6, x7, p6)
        c2[(XA + i) * T : (XA + i + 1) * T] = jnp.where(c0w, x7, p7)
    for i in range(2 * X // T):
        j = XA + i
        p7 = pay[j * T : (j + 1) * T]
        p6 = pay[(NT + j) * T : (NT + j + 1) * T]
        at = i * T * Z
        x6, x7 = a1y[pl.ds(at + 6, T, stride=Z), :], a1y[pl.ds(at + 7, T, stride=Z), :]
        c2y[i * T : (i + 1) * T] = fall(c0, cc2, x6, x7, p6)
        c2y[2 * X + i * T : 2 * X + (i + 1) * T] = jnp.where(c0w, x7, p7)
    mask = jnp.concatenate([south[HALO : HALO + X], north[HALO : HALO + X]] * 2, axis=0)
    c2y[...] = collide(c2y[...], mask, k, t)
    for z in range(2):
        at = slice(z * XA * T, (z + 1) * XA * T)
        c2[at] = collide(c2[at], m1[...], k, t)
    a2[0 : 2 * X * T] = a2_hi[...]
    for z in (6, 7):
        advect_one(z, c2, a2, c2y, u_ref, v_ref)
    for i in range(X):
        j = XA + 2 * X // T + i
        p7 = pay[j * T : (j + 1) * T]
        p6 = pay[(NT + j) * T : (NT + j + 1) * T]
        x = [a2[(z * X + i) * T : (z * X + i + 1) * T] for z in range(4)]
        for z, v in enumerate(
            (
                fall(c0, cc2, x[0], x[1], x[2]),
                fall(c0, cc2, x[1], x[2], x[3]),
                fall(c0, cc2, x[2], x[3], p6),
                jnp.where(c0w, x[3], p7),
            )
        ):
            res[(z * X + i) * T : (z * X + i + 1) * T] = v
    copy = pltpu.make_async_copy(res, out.at[pl.ds(4 * X * T, 4 * X * T)], sem)
    copy.start()
    copy.wait()


def advect_one(z, c2, a2, c2y, u_ref, v_ref):
    u, v = u_ref[z], v_ref[z]
    au, av = jnp.abs(u), jnp.abs(v)
    shift = jnp.where(v > 0, 1, T - 1)
    at_edge = lax.broadcasted_iota(jnp.int32, (T, B), 0) == jnp.where(v > 0, 0, T - 1)
    base = ((z - 6) * XA + 1) * Y
    base_x = base + jnp.where(u > 0, -Y, Y)
    base_e = (z - 6) * 2 * X + jnp.where(v > 0, 0, X)
    for i in range(X):
        c = c2[rows(base + i * Y)]
        x = c2[rows(base_x + i * Y)]
        e = eightfold(c2y, base_e + i)
        y = jnp.where(at_edge, e, pltpu.roll(c, shift, 0))
        a2[((z - 4) * X + i) * T : ((z - 4) * X + i + 1) * T] = c - au * (c - x) - av * (c - y)


def ring(axis, step):
    n = lax.axis_size(axis)
    return [(i, (i + step) % n) for i in range(n)]


def on_device(drops, capture, transfer, courant_u, courant_v, fall_class, cloud_mask):
    drops = drops.reshape(Z * X * Y, B)
    cloudy = jnp.broadcast_to(cloud_mask.astype(F32)[:, :, None], (X, Y, B)).reshape(X * Y, B)
    n0 = jnp.sum((fall_class == 0).astype(jnp.int32))
    n2 = jnp.sum((fall_class == H_MAX).astype(jnp.int32))
    sc = jnp.stack([n0, B - n2])
    ub = jnp.broadcast_to(courant_u[:, None], (Z, B))
    vb = jnp.broadcast_to(courant_v[:, None], (Z, B))
    v = lambda n, d=F32: ((n, B), d, True)
    own, xm, xp, ym, yp, kk, tt = call(
        edges_body,
        [v(Z * X * Y), v(XROWS + 16), v(XROWS + 16), v(HALO + 128), v(HALO + 128)]
        + [((2 * B, 2 * B), BF16, True)] * 2,
        [drops, cloudy, capture, transfer],
        [ANY, VMEM, VMEM, VMEM],
        [pltpu.SemaphoreType.DMA],
        cost=(1000, 4 << 20),
    )
    south = lax.ppermute(yp, "gy", ring("gy", 1))
    north = lax.ppermute(ym, "gy", ring("gy", -1))
    left = lax.ppermute(xp, "gx", ring("gx", 1))
    right = lax.ppermute(xm, "gx", ring("gx", -1))
    up, down = call(corners_body, [v(3 * T), v(3 * T)], [left, right], [VMEM] * 2, cost=(1000, 1 << 18))
    cs = lax.ppermute(up, "gy", ring("gy", 1))
    cn = lax.ppermute(down, "gy", ring("gy", -1))
    c1, cy, m1, my = call(
        first_body,
        [v(Z * XW * Y), v(4 * XA * Z), v(XA * Y), v(2 * X * Z)],
        [own, cloudy, left, right, south, north, kk, tt],
        [VMEM] * 8,
        cost=(3 << 30, 8 << 20),
    )
    a1, a1y, c2, c2y, a2, pay, cy = call(
        second_body,
        [v(4 * XA * T), v(2 * X * Z), v(2 * XA * T), v(2 * X * Z), v(2 * X * T), v(2 * NT * T), v(4 * XA * Z)],
        [sc, courant_u, courant_v, ub, vb, c1, cy, cs, cn, kk, tt, m1, my],
        [SMEM] * 3 + [VMEM] * 10,
        cost=(3 << 30, 8 << 20),
    )
    n = lax.axis_size("gz")
    above = lax.ppermute(pay, "gz", [(i, i - 1) for i in range(1, n)])
    a1_hi, a2_hi, out = call(
        third_body,
        [v(2 * XA * T), v(2 * X * T), ((Z * X * Y, B), F32, False)],
        [sc, courant_u, courant_v, c1, cy, a1, c2, c2y, a2, kk, tt, m1],
        [SMEM] * 3 + [VMEM] * 9,
        [
            pltpu.VMEM((8 * XA * T, B), F32),
            pltpu.VMEM((6 * XA * T, B), F32),
            pltpu.VMEM((6 * X * T, B), F32),
            pltpu.VMEM((4 * X * T, B), F32),
            pltpu.SemaphoreType.DMA,
        ],
        cost=(3 << 30, 8 << 20),
        out_specs=[VMEM, VMEM, ANY],
    )
    (out,) = call(
        last_body,
        [((Z * X * Y, B), F32, False)],
        [sc, courant_u, courant_v, a1_hi, a1y, a2_hi, south, north, kk, tt, m1, above, out],
        [SMEM] * 3 + [VMEM] * 9 + [ANY],
        [
            pltpu.VMEM((2 * XA * T, B), F32),
            pltpu.VMEM((4 * X, B), F32),
            pltpu.VMEM((4 * X * T, B), F32),
            pltpu.VMEM((4 * X * T, B), F32),
            pltpu.SemaphoreType.DMA,
        ],
        cost=(3 << 30, 8 << 20),
        out_specs=[ANY],
        aliases={12: 0},
    )
    return out.reshape(Z, X, Y, B)


def solution(mesh):
    in_specs = (P("gz", "gx", "gy", None), P(), P(), P("gz"), P("gz"), P(), P("gx", "gy"))
    out_specs = P("gz", "gx", "gy", None)
    return jax.shard_map(
        on_device, mesh=mesh, in_specs=in_specs, out_specs=out_specs, check_vma=False
    )
```

time: 74.2 us -> 70.8 us (0.954)
  the two profiles are of different devices: /device:TPU:223 before, /device:TPU:6 now
where the time goes in v1:
time: 70.8 us; the launch traced here: 70.3 us
  waiting for transfers between devices  25.7 us (36%)
  starting transfers between devices  20.5 us (29%)
  Pallas kernels  17.6 us (25%)
  local copies, waits for them, and re-layouts  3.72 us (5%)
  other arithmetic  2.02 us (3%)
  between operations  0.81 us (1%)
    ppermute x1, waiting for transfers between devices, on_device(): above = lax.ppermute(pay, 'gz', [(i, i - 1) for i in range(1, n)])  22.1 us
    pallas_call x6, Pallas kernels, call(): pl.pallas_call(body, out_shape=shapes, in_specs=list(specs), out_specs=ou...  17.6 us
    ppermute x1, starting transfers between devices, on_device(): left = lax.ppermute(xp, 'gx', ring('gx', 1))  11.4 us
    ppermute x1, waiting for transfers between devices, on_device(): right = lax.ppermute(xm, 'gx', ring('gx', -1))  3.52 us
    unnamed x12, local copies, waits for them, and re-layouts  3.28 us
    ppermute x1, starting transfers between devices, on_device(): cn = lax.ppermute(down, 'gy', ring('gy', -1))  2.95 us
    ppermute x1, starting transfers between devices, on_device(): north = lax.ppermute(ym, 'gy', ring('gy', -1))  2.94 us
    ppermute x1, starting transfers between devices, on_device(): right = lax.ppermute(xm, 'gx', ring('gx', -1))  1.92 us
  transfers between devices with their start and end apart: 7, of which 2 were waited for; matrix products, arithmetic and copies ran while one was open for 2% of the time, Pallas kernels for 14%

profile of v1, /device:TPU:6, one launch (start us, length us, event | category | flops | bytes accessed | tf_op | source)
XLA Modules:
  0.0 70.3 jit_solution(571067991441407024)
XLA Ops:
  0.0 0.7 convert_element_type.11
  0.7 0.1 copy.9
  0.8 0.1 broadcast_in_dim.8
  0.9 0.1 broadcast_in_dim.9.cloudy
  1.0 0.0 copy-start
  1.0 1.6 %copy-done = f32[8,64,8,128]{3,2,1,0:T(8,128)S(1)} copy-done((f32[8,64,8,128]{3,2,1,0:T(8,128)S(1)}, f32[8,64,8,128]{3,2,1,0:T(8,128)}, u32[]{:S(2)}) %copy-start) | copy-done | bytes 2097176
  2.6 0.8 %copy-done.1 = f32[128,128]{1,0:T(8,128)S(1)} copy-done((f32[128,128]{1,0:T(8,128)S(1)}, f32[128,128]{1,0:T(8,128)}, u32[]{:S(2)}) %copy-start.1) | copy-done | bytes 65560
  3.5 0.8 %copy-done.2 = f32[128,128]{1,0:T(8,128)S(1)} copy-done((f32[128,128]{1,0:T(8,128)S(1)}, f32[128,128]{1,0:T(8,128)}, u32[]{:S(2)}) %copy-start.2) | copy-done | bytes 65560
  4.3 1.9 %shard_map.73 = (f32[4096,128]{1,0:T(8,128)S(1)}, f32[144,128]{1,0:T(8,128)S(1)}, f32[144,128]{1,0:T(8,128)S(1)}, f32[1152,128]{1,0:T(8,128)}, f32[1152,128]{1,0...) custom-call(f32[4096,128]{1,0:T(8,128)S(1)} %bitcast.4, f32[512,128]{1,0:T(8,128)S(1)} %broadcast_in_dim.9.cloudy, ...), custom_call_target="tpu_custom_call" | custom-call | flops 1000 | bytes 4194304 | tf_op jit(solution)/shard_map/pallas_call | solution.py:34
  6.2 0.0 collective-permute-start.2
  6.2 2.9 %collective-permute-start.3 = (f32[1152,128]{1,0:T(8,128)}, f32[1152,128]{1,0:T(8,128)}, u32[]{:S(2)}, u32[]{:S(2)}) collective-permute-start(f32[1152,128]{1,0:T(8,128)} %get-tuple-element.32), channel_id=1, source_target_pairs={{0,180},{12,0},{24,12},{36,24},{48,36},{60,48},{72,60},{84,72},{96... | collective-permute-start | bytes 1769480 | tf_op jit(solution)/shard_map/ppermute | solution.py:367
  9.2 11.4 %collective-permute-start = (f32[144,128]{1,0:T(8,128)S(1)}, f32[144,128]{1,0:T(8,128)S(1)}, u32[]{:S(2)}, u32[]{:S(2)}) collective-permute-start(f32[144,128]{1,0:T(8,128)S(1)} %get-tuple-element.29), channel_id=1, source_target_pairs={{0,192},{192,384},{384,576},{576,0},{1,193},{193,385},{385,577},{5... | collective-permute-start | bytes 221192 | tf_op jit(solution)/shard_map/ppermute | solution.py:368
  20.5 1.9 %collective-permute-start.1 = (f32[144,128]{1,0:T(8,128)S(1)}, f32[144,128]{1,0:T(8,128)S(1)}, u32[]{:S(2)}, u32[]{:S(2)}) collective-permute-start(f32[144,128]{1,0:T(8,128)S(1)} %get-tuple-element.30), channel_id=1, source_target_pairs={{0,576},{192,0},{384,192},{576,384},{1,577},{193,1},{385,193},{577... | collective-permute-start | bytes 221192 | tf_op jit(solution)/shard_map/ppermute | solution.py:369
  22.5 0.7 fusion
  23.9 0.6 pad_add_fusion.sc
  24.5 0.0 collective-permute-done.left
  24.5 3.5 %collective-permute-done.1.right = f32[144,128]{1,0:T(8,128)S(1)} collective-permute-done((f32[144,128]{1,0:T(8,128)S(1)}, f32[144,128]{1,0:T(8,128)S(1)}, u32[]{:S(2)}, u32[]{:S(2)}) %collective-permute-start.1) | collective-permute-done | bytes 73760 | tf_op jit(solution)/shard_map/ppermute | solution.py:369
  28.0 0.0 collective-permute-start.4
  28.0 2.9 %collective-permute-start.5 = (f32[24,128]{1,0:T(8,128)S(1)}, f32[24,128]{1,0:T(8,128)S(1)}, u32[]{:S(2)}, u32[]{:S(2)}) collective-permute-start(f32[24,128]{1,0:T(8,128)S(1)} %get-tuple-element.38), channel_id=1, source_target_pairs={{0,180},{12,0},{24,12},{36,24},{48,36},{60,48},{72,60},{84,72},{96... | collective-permute-start | bytes 36872 | tf_op jit(solution)/shard_map/ppermute | solution.py:372
  31.0 0.0 collective-permute-done.2.south
  31.0 0.0 collective-permute-done.3.north
  31.0 0.0 copy-start.4
  31.0 5.4 %shard_map.74 = (f32[4352,128]{1,0:T(8,128)S(1)}, f32[2112,128]{1,0:T(8,128)S(1)}, f32[528,128]{1,0:T(8,128)S(1)}, f32[1024,128]{1,0:T(8,128)S(1)}) custom-call(f32[4096,128]{1,0:T(8,128)S(1)} %get-tuple-element.28.own, f32[512,128]{1,0:T(8,128)S(1)} %broadcast_in_dim.9.cloudy, f32[144,128]{1,0:T(8,128)S(1)} %collective-permute-done.left, ...), custom_call_target="tpu_custom_call" | custom-call | flops 3221225472 | bytes 8388608 | tf_op jit(solution)/shard_map/pallas_call | solution.py:34
  36.4 0.0 collective-permute-done.4.cs
  36.4 0.0 collective-permute-done.5.cn
  36.4 0.1 broadcast_in_dim.10.ub
  36.5 0.1 broadcast_in_dim.11.vb
  36.6 3.2 %shard_map.76 = (f32[2112,128]{1,0:T(8,128)S(1)}, f32[1024,128]{1,0:T(8,128)S(1)}, f32[1056,128]{1,0:T(8,128)S(1)}, f32[1024,128]{1,0:T(8,128)S(1)}, f32[1024,12...) custom-call(s32[2]{0:T(128)S(1)} %pad_add_fusion.sc, f32[8]{0:T(128)S(1)} %copy-done.3, ...), custom_call_target="tpu_custom_call" | custom-call | flops 3221225472 | bytes 8388608 | tf_op jit(solution)/shard_map/pallas_call | solution.py:34
  39.8 1.3 %collective-permute-start.6 = (f32[2336,128]{1,0:T(8,128)S(1)}, f32[2336,128]{1,0:T(8,128)S(1)}, u32[]{:S(2)}, u32[]{:S(2)}) collective-permute-start(f32[2336,128]{1,0:T(8,128)S(1)} %get-tuple-element.49), channel_id=1, source_target_pairs={{1,0},{2,1},{3,2},{4,3},{5,4},{6,5},{7,6},{8,7},{9,8},{10,9},{11,1... | collective-permute-start | bytes 3588104 | tf_op jit(solution)/shard_map/ppermute | solution.py:388
  41.1 4.2 %shard_map.77 = (f32[1056,128]{1,0:T(8,128)S(1)}, f32[1024,128]{1,0:T(8,128)S(1)}, f32[4096,128]{1,0:T(8,128)}) custom-call(s32[2]{0:T(128)S(1)} %pad_add_fusion.sc, f32[8]{0:T(128)S(1)} %copy-done.3, f32[8]{0:T(128)S(1)} %copy-done.4, f32[4352,128]{1,0:T(8,128)S(1)} %get-tuple-element.35.c1_in.c1, f32[2112,128]{1,0:T(8,128)S(1)} %get-tuple-element.41.cy, ...), custom_call_target="tpu_custom_call" | custom-call | flops 3221225472 | bytes 8388608 | tf_op jit(solution)/shard_map/pallas_call | solution.py:34
  45.3 22.1 %collective-permute-done.6.pay = f32[2336,128]{1,0:T(8,128)S(1)} collective-permute-done((f32[2336,128]{1,0:T(8,128)S(1)}, f32[2336,128]{1,0:T(8,128)S(1)}, u32[]{:S(2)}, u32[]{:S(2)}) %collective-permute-start.6) | collective-permute-done | bytes 1196064 | tf_op jit(solution)/shard_map/ppermute | solution.py:388
  67.5 2.9 %shard_map.78 = f32[4096,128]{1,0:T(8,128)} custom-call(s32[2]{0:T(128)S(1)} %pad_add_fusion.sc, f32[8]{0:T(128)S(1)} %copy-done.3, f32[8]{0:T(128)S(1)} %copy-done.4, f32[1056,128]{1,0:T(8,128)S(1)} %get-tuple-element.46.a1_hi, f32[1024,128]{1,0:T(8,128)S(1)} %get-tuple-element.47.a1y, ...), custom_call_target="tpu_custom_call", output_to_operand_aliasing={{}: (12, {})} | custom-call | flops 3221225472 | bytes 8388608 | tf_op jit(solution)/shard_map/pallas_call | solution.py:34
  (8 shorter events, 0.0 us)
Async XLA Ops:
  0.0 22.5 %copy-start.5 = (s32[128]{0:T(128)S(1)}, s32[128]{0:T(128)}, u32[]{:S(2)}) copy-start(s32[128]{0:T(128)} %param.12) | copy-start | bytes 1540
  1.0 1.6 %copy-start = (f32[8,64,8,128]{3,2,1,0:T(8,128)S(1)}, f32[8,64,8,128]{3,2,1,0:T(8,128)}, u32[]{:S(2)}) copy-start(f32[8,64,8,128]{3,2,1,0:T(8,128)} %param.7) | copy-start | bytes 6291460
  2.6 0.8 %copy-start.1 = (f32[128,128]{1,0:T(8,128)S(1)}, f32[128,128]{1,0:T(8,128)}, u32[]{:S(2)}) copy-start(f32[128,128]{1,0:T(8,128)} %k_ref.1) | copy-start | bytes 196612
  3.5 0.8 %copy-start.2 = (f32[128,128]{1,0:T(8,128)S(1)}, f32[128,128]{1,0:T(8,128)}, u32[]{:S(2)}) copy-start(f32[128,128]{1,0:T(8,128)} %t_ref.1) | copy-start | bytes 196612
  6.2 24.8 %collective-permute-start.2 = (f32[1152,128]{1,0:T(8,128)}, f32[1152,128]{1,0:T(8,128)S(1)}, u32[]{:S(2)}, u32[]{:S(2)}) collective-permute-start(f32[1152,128]{1,0:T(8,128)} %get-tuple-element.31), channel_id=1, source_target_pairs={{0,12},{12,24},{24,36},{36,48},{48,60},{60,72},{72,84},{84,96},{96... | collective-permute-start | bytes 1769480 | tf_op jit(solution)/shard_map/ppermute | solution.py:366
  6.2 24.8 %collective-permute-start.3 = (f32[1152,128]{1,0:T(8,128)}, f32[1152,128]{1,0:T(8,128)}, u32[]{:S(2)}, u32[]{:S(2)}) collective-permute-start(f32[1152,128]{1,0:T(8,128)} %get-tuple-element.32), channel_id=1, source_target_pairs={{0,180},{12,0},{24,12},{36,24},{48,36},{60,48},{72,60},{84,72},{96... | collective-permute-start | bytes 1769480 | tf_op jit(solution)/shard_map/ppermute | solution.py:367
  9.2 15.3 %collective-permute-start = (f32[144,128]{1,0:T(8,128)S(1)}, f32[144,128]{1,0:T(8,128)S(1)}, u32[]{:S(2)}, u32[]{:S(2)}) collective-permute-start(f32[144,128]{1,0:T(8,128)S(1)} %get-tuple-element.29), channel_id=1, source_target_pairs={{0,192},{192,384},{384,576},{576,0},{1,193},{193,385},{385,577},{5... | collective-permute-start | bytes 221192 | tf_op jit(solution)/shard_map/ppermute | solution.py:368
  20.5 7.5 %collective-permute-start.1 = (f32[144,128]{1,0:T(8,128)S(1)}, f32[144,128]{1,0:T(8,128)S(1)}, u32[]{:S(2)}, u32[]{:S(2)}) collective-permute-start(f32[144,128]{1,0:T(8,128)S(1)} %get-tuple-element.30), channel_id=1, source_target_pairs={{0,576},{192,0},{384,192},{576,384},{1,577},{193,1},{385,193},{577... | collective-permute-start | bytes 221192 | tf_op jit(solution)/shard_map/ppermute | solution.py:369
  28.0 8.4 %collective-permute-start.4 = (f32[24,128]{1,0:T(8,128)S(1)}, f32[24,128]{1,0:T(8,128)S(1)}, u32[]{:S(2)}, u32[]{:S(2)}) collective-permute-start(f32[24,128]{1,0:T(8,128)S(1)} %get-tuple-element.37), channel_id=1, source_target_pairs={{0,12},{12,24},{24,36},{36,48},{48,60},{60,72},{72,84},{84,96},{96... | collective-permute-start | bytes 36872 | tf_op jit(solution)/shard_map/ppermute | solution.py:371
  28.0 8.4 %collective-permute-start.5 = (f32[24,128]{1,0:T(8,128)S(1)}, f32[24,128]{1,0:T(8,128)S(1)}, u32[]{:S(2)}, u32[]{:S(2)}) collective-permute-start(f32[24,128]{1,0:T(8,128)S(1)} %get-tuple-element.38), channel_id=1, source_target_pairs={{0,180},{12,0},{24,12},{36,24},{48,36},{60,48},{72,60},{84,72},{96... | collective-permute-start | bytes 36872 | tf_op jit(solution)/shard_map/ppermute | solution.py:372
  31.0 5.4 %copy-start.3 = (f32[8]{0:T(128)S(1)}, f32[8]{0:T(128)}, u32[]{:S(2)}) copy-start(f32[8]{0:T(128)} %u_ref.5) | copy-start | bytes 100
  31.0 5.5 %copy-start.4 = (f32[8]{0:T(128)S(1)}, f32[8]{0:T(128)}, u32[]{:S(2)}) copy-start(f32[8]{0:T(128)} %v_ref.5) | copy-start | bytes 100
  39.8 27.7 %collective-permute-start.6 = (f32[2336,128]{1,0:T(8,128)S(1)}, f32[2336,128]{1,0:T(8,128)S(1)}, u32[]{:S(2)}, u32[]{:S(2)}) collective-permute-start(f32[2336,128]{1,0:T(8,128)S(1)} %get-tuple-element.49), channel_id=1, source_target_pairs={{1,0},{2,1},{3,2},{4,3},{5,4},{6,5},{7,6},{8,7},{9,8},{10,9},{11,1... | collective-permute-start | bytes 3588104 | tf_op jit(solution)/shard_map/ppermute | solution.py:388

commit v2 on v0

--- a/solution.py
+++ b/solution.py
@@ -1,10 +1,541 @@
+import functools
+
 import jax
 import jax.numpy as jnp
 from jax import lax
+from jax.experimental import pallas as pl
+from jax.experimental.pallas import tpu as pltpu
 from jax.sharding import PartitionSpec as P
 
 H_MAX = 2
 STEPS = 2
+Z, X, Y, B = 8, 64, 8, 128
+T = 8
+XW = X + 4
+XA = X + 2
+LOW = Z // 2
+HALF = 2 * LOW * X
+ENDS = HALF + 2 * X
+XROWS = 2 * Z * Y
+EARLY = (X - 2) + 2 * X // T + (X - 4)
+GROUPS = 4
+SPARE = B // GROUPS
+EXTRA = -(-EARLY // GROUPS)
+LATE = 4 + 1 + 4
+F32, BF16 = jnp.float32, jnp.bfloat16
+
+VMEM = pl.BlockSpec(memory_space=pltpu.VMEM)
+SMEM = pl.BlockSpec(memory_space=pltpu.SMEM)
+HBM = pl.BlockSpec(memory_space=pltpu.HBM)
+
+
+def rows(start, n=T):
+    return pl.ds(start if isinstance(start, int) else pl.multiple_of(start, T), n)
+
+
+def call(body, outs, args, specs, scratch=(), cost=(0, 0), out_specs=None, aliases=None):
+    shapes = [pltpu.VMEM(s, d) if m else jax.ShapeDtypeStruct(s, d) for s, d, m in outs]
+    args = [
+        a if s is SMEM else pltpu.with_memory_space_constraint(a, s.memory_space)
+        for a, s in zip(args, specs)
+    ]
+    return pl.pallas_call(
+        body,
+        out_shape=shapes,
+        in_specs=list(specs),
+        out_specs=out_specs or [VMEM] * len(outs),
+        scratch_shapes=list(scratch),
+        input_output_aliases=aliases or {},
+        cost_estimate=pl.CostEstimate(flops=cost[0], bytes_accessed=cost[1], transcendentals=0),
+        compiler_params=pltpu.CompilerParams(vmem_limit_bytes=8 << 20),
+    )(*args)
+
+
+def split(x):
+    high = x.astype(BF16)
+    return high, (x - high.astype(F32)).astype(BF16)
+
+
+def product(x, weights):
+    out = jnp.dot(jnp.concatenate(split(x), axis=1), weights, preferred_element_type=F32)
+    return out[:, :B] + out[:, B:]
+
+
+def collide(s, cloudy, capture, transfer):
+    loss = s * product(s, capture)
+    return s + cloudy * (product(loss, transfer) - loss)
+
+
+def eightfold(ref, row):
+    return ref[pl.ds(row, T, stride=0), :]
+
+
+def repeated(ref, start, n):
+    return jnp.concatenate([eightfold(ref, start + i) for i in range(n)], axis=0)
+
+
+def classes(sc_ref):
+    lane = lax.broadcasted_iota(jnp.int32, (T, B), 1)
+    return lane < sc_ref[0], lane >= sc_ref[1]
+
+
+def fall(c0, c2, a, b, c):
+    return jnp.where(c0, a, jnp.where(c2, c, b))
+
+
+def edges_body(drops, cloud, k_in, t_in, own, m1, ym0, ym1, yp0, yp1, kk, tt, mask, k_ref, t_ref, sem):
+    copies = [
+        pltpu.make_async_copy(a, b, sem.at[i])
+        for i, (a, b) in enumerate(((drops, own), (cloud, mask), (k_in, k_ref), (t_in, t_ref)))
+    ]
+    for copy in copies[1:] + copies[:1]:
+        copy.start()
+    copies[1].wait()
+    columns = mask[...].astype(F32)
+    for x in range(X):
+        m1[(x + 1) * Y : (x + 2) * Y] = jnp.broadcast_to(columns[:, x : x + 1], (Y, B))
+    for i, (ref, out, turned) in enumerate(((k_ref, kk, True), (t_ref, tt, False))):
+        copies[2 + i].wait()
+        w = ref[...].T if turned else ref[...]
+        high, low = split(w)
+        half = jnp.concatenate([high, low], axis=1)
+        out[...] = jnp.concatenate([half, half], axis=0)
+    for out, ys in ((ym0, (0, 1)), (yp0, (Y - 1, Y - 2))):
+        for d, y in enumerate(ys):
+            out[HALF + d * X : HALF + (d + 1) * X] = m1[pl.ds(Y + y, X, stride=Y), :]
+    copies[0].wait()
+    for outs, ys in (((ym0, ym1), (0, 1)), ((yp0, yp1), (Y - 1, Y - 2))):
+        for part, out in enumerate(outs):
+            for d, y in enumerate(ys):
+                for z in range(LOW):
+                    at = (d * LOW + z) * X
+                    start = (part * LOW + z) * X * Y + y
+                    out[at : at + X] = own[pl.ds(start, X, stride=Y), :]
+        for i, x in enumerate((0, X - 1)):
+            at, start = ENDS + i * LOW, (LOW * X + x) * Y + ys[0]
+            outs[0][at : at + LOW] = own[pl.ds(start, LOW, stride=X * Y), :]
+
+
+def sides_body(own, m1, south, north, xm, xp):
+    for out, cols in ((xm, (0, 1)), (xp, (X - 1, X - 2))):
+        for d, x in enumerate(cols):
+            out[XROWS + d * Y : XROWS + (d + 1) * Y] = m1[(x + 1) * Y : (x + 2) * Y]
+            for z in range(Z):
+                at = (z * X + x) * Y
+                out[(d * Z + z) * Y : (d * Z + z + 1) * Y] = own[at : at + Y]
+        x = cols[0]
+        at = XROWS + 2 * Y
+        out[at + 2 * Z :] = jnp.zeros((T, B), F32)
+        for side, ref in enumerate((south, north)):
+            row = at + side * Z
+            end = ENDS + (LOW if x else 0)
+            out[row : row + LOW] = ref[pl.ds(x, LOW, stride=X), :]
+            out[row + LOW : row + Z] = ref[end : end + LOW]
+            row = at + 2 * Z + side
+            out[row : row + 1] = ref[HALF + x : HALF + x + 1]
+
+
+XMESSAGE = XROWS + 2 * Y + 2 * Z + T
+
+
+def own_body(own, m1, kk, tt, c1):
+    k, t, mask = kk[...], tt[...], m1[Y : Y + X * Y]
+
+    def level(z, _):
+        c1[rows((z * XW + 2) * Y, X * Y)] = collide(own[rows(z * X * Y, X * Y)], mask, k, t)
+        return 0
+
+    lax.fori_loop(0, Z, level, 0)
+
+
+def cy_at(side, d, x):
+    return ((side * 2 + d) * XA + x + 1) * Z
+
+
+def collide_rows(part, south, north, masks, cy, k, t):
+    for side, (ref, mask_ref) in enumerate(zip((south, north), masks)):
+        for d in range(2):
+            mask = jnp.concatenate([mask_ref[HALF + d * X : HALF + (d + 1) * X]] * LOW, axis=0)
+            c = collide(ref[d * LOW * X : (d + 1) * LOW * X], mask, k, t)
+            for z in range(LOW):
+                cy[pl.ds(cy_at(side, d, 0) + part * LOW + z, X, stride=Z), :] = c[z * X : (z + 1) * X]
+
+
+def upwind(z, u_ref, v_ref):
+    u, v = u_ref[z], v_ref[z]
+    at_edge = lax.broadcasted_iota(jnp.int32, (T, B), 0) == jnp.where(v > 0, 0, T - 1)
+    return (
+        jnp.abs(u),
+        jnp.abs(v),
+        jnp.where(u > 0, -Y, Y),
+        jnp.where(v > 0, 1, T - 1),
+        jnp.where(v > 0, 0, 1),
+        at_edge,
+    )
+
+
+def advect(z, columns, c_ref, width, first, out_ref, out_width, edge, u_ref, v_ref):
+    au, av, step, shift, side, at_edge = upwind(z, u_ref, v_ref)
+    base, base_out = (z * width + first) * Y, z * out_width * Y
+    edge_ref, edge_at, edge_stride = edge(z, side)
+    for i in columns:
+        c = c_ref[rows(base + i * Y)]
+        x = c_ref[rows(base + step + i * Y)]
+        e = eightfold(edge_ref, edge_at + i * edge_stride)
+        y = jnp.where(at_edge, e, pltpu.roll(c, shift, 0))
+        out_ref[rows(base_out + i * Y)] = c - au * (c - x) - av * (c - y)
+
+
+def advect_first(z, columns, c1, a1, cy, u_ref, v_ref):
+    edge = lambda z, side: (cy, side * (2 * XA * Z) + z, Z)
+    advect(z, columns, c1, XW, 1, a1, XA, edge, u_ref, v_ref)
+
+
+def advect_second(z, columns, c2, a2, c2y, u_ref, v_ref):
+    edge = lambda z, side: (c2y, (z * 2 + side) * X, 1)
+    advect(z, columns, c2, XA, 1, a2, X, edge, u_ref, v_ref)
+
+
+def advect_rows(columns, ub, vb, c1, cy, a1y):
+    au, av = jnp.abs(ub[...]), jnp.abs(vb[...])
+    upos, vpos = ub[...] > 0, vb[...] > 0
+    for side in range(2):
+        for x in columns:
+            at, far = cy_at(side, 0, x), cy_at(side, 1, x)
+            c = cy[at : at + Z]
+            xx = jnp.where(upos, cy[at - Z : at], cy[at + Z : at + 2 * Z])
+            outer = cy[far : far + Z]
+            inner = c1[pl.ds((x + 2) * Y + (Y - 1) * side, Z, stride=XW * Y), :]
+            yy = jnp.where(vpos, *((outer, inner) if side == 0 else (inner, outer)))
+            to = (side * X + x) * Z
+            a1y[to : to + Z] = c - au * (c - xx) - av * (c - yy)
+
+
+def settle(z, columns, c0, cc2, a1, c2):
+    for i in columns:
+        at = (z * XA + i) * T
+        step = XA * T
+        c2[rows(at)] = fall(c0, cc2, a1[rows(at)], a1[rows(at + step)], a1[rows(at + 2 * step)])
+
+
+def settle_level(z, c0, cc2, a1, m1, c2, k, t):
+    settle(z, range(XA), c0, cc2, a1, c2)
+    at = rows(z * XA * T, XA * T)
+    c2[at] = collide(c2[at], m1[...], k, t)
+
+
+def settle_rows(z, c0, cc2, a1y, masks, c2y, k, t):
+    for i in range(2 * X // T):
+        a = [a1y[pl.ds(i * T * Z + z + j, T, stride=Z), :] for j in range(H_MAX + 1)]
+        to = z * 2 * X + i * T
+        c2y[to : to + T] = fall(c0, cc2, *a)
+    at = slice(z * 2 * X, (z + 1) * 2 * X)
+    mask = jnp.concatenate([m[HALF : HALF + X] for m in masks], axis=0)
+    c2y[at] = collide(c2y[at], mask, k, t)
+
+
+def falling(a1, a1y, a2, tile):
+    if tile < X - 2:
+        at = (tile + 2) * T
+        return lambda z: a1[z * XA * T + at : z * XA * T + at + T]
+    tile -= X - 2
+    if tile < 2 * X // T:
+        return lambda z: a1y[pl.ds(tile * T * Z + z, T, stride=Z), :]
+    at = (tile - 2 * X // T + 2) * T
+    return lambda z: a2[z * X * T + at : z * X * T + at + T]
+
+
+def early_body(
+    sc, u_ref, v_ref, ub, vb, c1, south, north, kk, tt, m1, cy, a1, a1y, c2, c2y, a2, pay
+):
+    k, t = kk[...], tt[...]
+    c0, cc2 = classes(sc)
+    collide_rows(0, south, north, (south, north), cy, k, t)
+
+    def first(z, _):
+        advect_first(z, range(2, X), c1, a1, cy, u_ref, v_ref)
+        return 0
+
+    lax.fori_loop(0, 4, first, 0)
+    advect_rows(range(1, X - 1), ub, vb, c1, cy, a1y)
+
+    def second(z, _):
+        settle_level(z, c0, cc2, a1, m1, c2, k, t)
+        return 0
+
+    lax.fori_loop(0, 2, second, 0)
+    for z in range(2):
+        settle_rows(z, c0, cc2, a1y, (south, north), c2y, k, t)
+
+    def third(z, _):
+        advect_second(z, range(2, X - 2), c2, a2, c2y, u_ref, v_ref)
+        return 0
+
+    lax.fori_loop(0, 2, third, 0)
+    n0 = sc[0]
+    n2 = B - sc[1]
+    for tile in range(EARLY):
+        level = falling(a1, a1y, a2, tile)
+        l0 = level(0)
+        packed = fall(c0, cc2, pltpu.roll(l0, n2, 1), l0, level(1))
+        pay[tile * T : (tile + 1) * T] = packed
+    group = lax.broadcasted_iota(jnp.int32, (T, B), 1) // SPARE
+    for j in range(EXTRA):
+        out = jnp.zeros((T, B), F32)
+        for g in range(GROUPS):
+            if j + g * EXTRA < EARLY:
+                l0 = falling(a1, a1y, a2, j + g * EXTRA)(0)
+                turn = (n2 - n0 + g * SPARE + B) & (B - 1)
+                out = jnp.where(group == g, pltpu.roll(l0, turn, 1), out)
+        pay[(EARLY + j) * T : (EARLY + j + 1) * T] = out
+
+
+EDGE = (0, 1, XA - 2, XA - 1)
+
+
+def late_body(
+    sc, u_ref, v_ref, ub, vb, left, right, kk, tt, south, north,
+    c1_in, cy_in, m1_in, a1_in, a1y_in, c2_in, c2y_in, a2_in,
+    c1, cy, m1, a1, a1y, c2, c2y, a2, pay,
+):
+    k, t = kk[...], tt[...]
+    c0, cc2 = classes(sc)
+    m1[0:Y] = left[XROWS : XROWS + Y]
+    m1[Y + X * Y :] = right[XROWS : XROWS + Y]
+    at_mask = XROWS + 2 * Y
+    pieces, masks = [], []
+    for ref in (left, right):
+        pieces += [ref[0:XROWS], ref[at_mask : at_mask + 2 * Z]]
+        masks += [ref[XROWS + d * Y : XROWS + (d + 1) * Y] for d in range(2) for _ in range(Z)]
+        masks += [eightfold(ref, at_mask + 2 * Z + side) for side in range(2)]
+    c = collide(jnp.concatenate(pieces, axis=0), jnp.concatenate(masks, axis=0), k, t)
+    size = XROWS + 2 * Z
+    for i, (columns, x) in enumerate((((1, 0), -1), ((XW - 2, XW - 1), X))):
+        for d in range(2):
+            for z in range(Z):
+                at, to = i * size + (d * Z + z) * Y, (z * XW + columns[d]) * Y
+                c1[to : to + Y] = c[at : at + Y]
+        for side in range(2):
+            at, to = i * size + XROWS + side * Z, cy_at(side, 0, x)
+            cy[to : to + Z] = c[at : at + Z]
+
+    for z in range(4):
+        advect_first(z, EDGE, c1, a1, cy, u_ref, v_ref)
+    advect_rows((0, X - 1), ub, vb, c1, cy, a1y)
+    for z in range(2):
+        settle(z, EDGE, c0, cc2, a1, c2)
+    tiles = [(z * XA + i) * T for z in range(2) for i in EDGE]
+    c = collide(
+        jnp.concatenate([c2[at : at + T] for at in tiles], axis=0),
+        jnp.concatenate([m1[i * T : (i + 1) * T] for i in EDGE] * 2, axis=0),
+        k,
+        t,
+    )
+    for i, at in enumerate(tiles):
+        c2[at : at + T] = c[i * T : (i + 1) * T]
+    for z in range(2):
+        settle_rows(z, c0, cc2, a1y, (south, north), c2y, k, t)
+        advect_second(z, (0, 1, X - 2, X - 1), c2, a2, c2y, u_ref, v_ref)
+    for i, x in enumerate(EDGE):
+        l0, l1 = (a1[(z * XA + x) * T : (z * XA + x + 1) * T] for z in range(2))
+        pay[i * T : (i + 1) * T] = fall(c0, cc2, l0, l0, l1)
+        pay[(LATE + i) * T : (LATE + i + 1) * T] = l0
+    at = 4 * T
+    for i, row in enumerate((0, X - 1, X, 2 * X - 1)):
+        l0, l1 = (a1y[row * Z + z : row * Z + z + 1] for z in range(2))
+        pay[at + i : at + i + 1] = fall(c0[0:1], cc2[0:1], l0, l0, l1)
+        pay[at + LATE * T + i : at + LATE * T + i + 1] = l0
+    for first in (at + 4, at + LATE * T + 4):
+        pay[first : first + 4] = jnp.zeros((4, B), F32)
+    for i, x in enumerate((0, 1, X - 2, X - 1)):
+        l0, l1 = (a2[(z * X + x) * T : (z * X + x + 1) * T] for z in range(2))
+        to = at + (i + 1) * T
+        pay[to : to + T] = fall(c0, cc2, l0, l0, l1)
+        pay[to + LATE * T : to + LATE * T + T] = l0
+
+
+def rest_body(
+    sc, u_ref, v_ref, ub, vb, kk, tt, south0, south1, north0, north1, c1, m1,
+    cy_in, a1_in, a1y_in, c2_in, c2y_in, a2_in,
+    cy, a1, a1y, c2, c2y, a2, out, res, sem,
+):
+    k, t = kk[...], tt[...]
+    c0, cc2 = classes(sc)
+    collide_rows(1, south1, north1, (south0, north0), cy, k, t)
+
+    def first(z, _):
+        advect_first(z, range(XA), c1, a1, cy, u_ref, v_ref)
+        return 0
+
+    lax.fori_loop(4, 8, first, 0)
+    advect_rows(range(X), ub, vb, c1, cy, a1y)
+
+    def second(z, _):
+        settle_level(z, c0, cc2, a1, m1, c2, k, t)
+        return 0
+
+    lax.fori_loop(2, 6, second, 0)
+    for z in range(2, 6):
+        settle_rows(z, c0, cc2, a1y, (south0, north0), c2y, k, t)
+
+    def third(z, _):
+        advect_second(z, range(X), c2, a2, c2y, u_ref, v_ref)
+        return 0
+
+    lax.fori_loop(2, 6, third, 0)
+
+    def done(z, _):
+        for i in range(X):
+            at, step = (z * X + i) * T, X * T
+            res[rows(at)] = fall(c0, cc2, a2[rows(at)], a2[rows(at + step)], a2[rows(at + 2 * step)])
+        return 0
+
+    lax.fori_loop(0, 4, done, 0)
+    copy = pltpu.make_async_copy(res, out.at[pl.ds(0, 4 * X * T)], sem)
+    copy.start()
+    copy.wait()
+
+
+def last_body(
+    sc, u_ref, v_ref, kk, tt, south, north, m1, a1, a1y, c2_in, c2y_in, a2_in, early, late, out_in,
+    out, c2, c2y, a2, row7, row6, res, sem,
+):
+    k, t = kk[...], tt[...]
+    c0, cc2 = classes(sc)
+    n0, start2 = sc[0], sc[1]
+    lane = lax.broadcasted_iota(jnp.int32, (T, B), 1)
+    within = lane < start2 + n0
+    turns = [(n0 + start2 - g * SPARE + B) & (B - 1) for g in range(GROUPS)]
+
+    def from_above(tile):
+        m = early[tile * T : (tile + 1) * T]
+        g, j = tile // EXTRA, tile % EXTRA
+        spare = early[(EARLY + j) * T : (EARLY + j + 1) * T]
+        return m, jnp.where(within, pltpu.roll(m, start2, 1), pltpu.roll(spare, turns[g], 1))
+
+    def from_late(i):
+        return late[i * T : (i + 1) * T], late[(LATE + i) * T : (LATE + i + 1) * T]
+
+    for i in range(XA):
+        p7, p6 = from_late(EDGE.index(i)) if i in EDGE else from_above(i - 2)
+        x6, x7 = (a1[(z * XA + i) * T : (z * XA + i + 1) * T] for z in (6, 7))
+        c2[(6 * XA + i) * T : (6 * XA + i + 1) * T] = fall(c0, cc2, x6, x7, p6)
+        c2[(7 * XA + i) * T : (7 * XA + i + 1) * T] = jnp.where(c0, x7, p7)
+    for i in range(2 * X // T):
+        row7[i * T : (i + 1) * T], row6[i * T : (i + 1) * T] = from_above(X - 2 + i)
+    p7, p6 = from_late(4)
+    for i, row in enumerate((0, X - 1, X, 2 * X - 1)):
+        row7[row : row + 1], row6[row : row + 1] = p7[i : i + 1], p6[i : i + 1]
+    for i in range(2 * X // T):
+        x6, x7 = (a1y[pl.ds(i * T * Z + z, T, stride=Z), :] for z in (6, 7))
+        at = 6 * 2 * X + i * T
+        c2y[at : at + T] = fall(c0, cc2, x6, x7, row6[i * T : (i + 1) * T])
+        c2y[at + 2 * X : at + 2 * X + T] = jnp.where(c0, x7, row7[i * T : (i + 1) * T])
+    mask = jnp.concatenate([south[HALF : HALF + X], north[HALF : HALF + X]] * 2, axis=0)
+    at = slice(12 * X, 16 * X)
+    c2y[at] = collide(c2y[at], mask, k, t)
+    for z in (6, 7):
+        at = slice(z * XA * T, (z + 1) * XA * T)
+        c2[at] = collide(c2[at], m1[...], k, t)
+        advect_second(z, range(X), c2, a2, c2y, u_ref, v_ref)
+    for i in range(X):
+        ends = (0, 1, X - 2, X - 1)
+        tile = X - 2 + 2 * X // T + i - 2
+        p7, p6 = from_late(5 + ends.index(i)) if i in ends else from_above(tile)
+        x = [a2[(z * X + i) * T : (z * X + i + 1) * T] for z in range(4, 8)]
+        for z, v in enumerate(
+            (
+                fall(c0, cc2, x[0], x[1], x[2]),
+                fall(c0, cc2, x[1], x[2], x[3]),
+                fall(c0, cc2, x[2], x[3], p6),
+                jnp.where(c0, x[3], p7),
+            )
+        ):
+            res[(z * X + i) * T : (z * X + i + 1) * T] = v
+    copy = pltpu.make_async_copy(res, out.at[pl.ds(4 * X * T, 4 * X * T)], sem)
+    copy.start()
+    copy.wait()
+
+
+def ring(axis, step):
+    n = lax.axis_size(axis)
+    return [(i, (i + step) % n) for i in range(n)]
+
+
+def below(value):
+    return lax.ppermute(value, "gz", [(i, i - 1) for i in range(1, lax.axis_size("gz"))])
+
+
+def packed(n0, n2, drops, capture, transfer, courant_u, courant_v, fall_class, cloud_mask):
+    drops = drops.reshape(Z * X * Y, B)
+    sc = jnp.stack([n0, B - n2])
+    ub = jnp.broadcast_to(courant_u[:, None], (Z, B))
+    vb = jnp.broadcast_to(courant_v[:, None], (Z, B))
+    v = lambda n, d=F32: ((n, B), d, True)
+    weights = [((2 * B, 2 * B), BF16, True)] * 2
+    own, m1, ym0, ym1, yp0, yp1, kk, tt = call(
+        edges_body,
+        [v(Z * X * Y), v(XA * Y), v(ENDS + T), v(HALF), v(ENDS + T), v(HALF)] + weights,
+        [drops, cloud_mask.T, capture, transfer],
+        [HBM] * 4,
+        [pltpu.VMEM((Y, X), jnp.int32), pltpu.VMEM((B, B), F32), pltpu.VMEM((B, B), F32), pltpu.SemaphoreType.DMA((4,))],
+        cost=(1000, 4 << 20),
+    )
+    south0 = lax.ppermute(yp0, "gy", ring("gy", 1))
+    north0 = lax.ppermute(ym0, "gy", ring("gy", -1))
+    south1 = lax.ppermute(yp1, "gy", ring("gy", 1))
+    north1 = lax.ppermute(ym1, "gy", ring("gy", -1))
+    (c1,) = call(own_body, [v(Z * XW * Y)], [own, m1, kk, tt], [VMEM] * 4, cost=(3 << 30, 8 << 20))
+    shapes = [v(4 * XA * Z), v(Z * XA * T), v(2 * X * Z), v(Z * XA * T), v(Z * 2 * X), v(Z * X * T)]
+    scalars = [sc, courant_u, courant_v]
+    cy, a1, a1y, c2, c2y, a2, pay = call(
+        early_body,
+        shapes + [v((EARLY + EXTRA) * T)],
+        scalars + [ub, vb, c1, south0, north0, kk, tt, m1],
+        [SMEM] * 3 + [VMEM] * 8,
+        cost=(1 << 30, 4 << 20),
+    )
+    early = below(pay)
+    xm, xp = call(
+        sides_body,
+        [v(XMESSAGE)] * 2,
+        [own, m1, south0, north0],
+        [VMEM] * 4,
+        cost=(1000, 1 << 18),
+    )
+    left = lax.ppermute(xp, "gx", ring("gx", 1))
+    right = lax.ppermute(xm, "gx", ring("gx", -1))
+    c1, cy, m1, a1, a1y, c2, c2y, a2, pay = call(
+        late_body,
+        [v(Z * XW * Y), shapes[0], v(XA * Y)] + shapes[1:] + [v(2 * LATE * T)],
+        scalars + [ub, vb, left, right, kk, tt, south0, north0, c1, cy, m1, a1, a1y, c2, c2y, a2],
+        [SMEM] * 3 + [VMEM] * 16,
+        cost=(1 << 28, 1 << 20),
+        aliases={11 + i: i for i in range(8)},
+    )
+    late = below(pay)
+    *state, out = call(
+        rest_body,
+        shapes + [((Z * X * Y, B), F32, False)],
+        scalars + [ub, vb, kk, tt, south0, south1, north0, north1, c1, m1, cy, a1, a1y, c2, c2y, a2],
+        [SMEM] * 3 + [VMEM] * 16,
+        [pltpu.VMEM((4 * X * T, B), F32), pltpu.SemaphoreType.DMA],
+        cost=(3 << 30, 8 << 20),
+        out_specs=[VMEM] * 6 + [HBM],
+        aliases={13 + i: i for i in range(6)},
+    )
+    (cy, a1, a1y, c2, c2y, a2) = state
+    out, *_ = call(
+        last_body,
+        [((Z * X * Y, B), F32, False), shapes[3], shapes[4], shapes[5]],
+        scalars + [kk, tt, south0, north0, m1, a1, a1y, c2, c2y, a2, early, late, out],
+        [SMEM] * 3 + [VMEM] * 12 + [HBM],
+        [pltpu.VMEM((2 * X, B), F32), pltpu.VMEM((2 * X, B), F32), pltpu.VMEM((4 * X * T, B), F32), pltpu.SemaphoreType.DMA],
+        cost=(1 << 30, 8 << 20),
+        out_specs=[HBM] + [VMEM] * 3,
+        aliases={15: 0, 10: 1, 11: 2, 12: 3},
+    )
+    return out.reshape(Z, X, Y, B)
 
 
 def passed_along(block, axis, distance):
@@ -33,7 +564,7 @@
     return value
 
 
-def collide(particle_distribution, capture_efficiency_matrix, transfer, cloudy):
+def collide_plain(particle_distribution, capture_efficiency_matrix, transfer, cloudy):
     merger_speed = jnp.einsum(
         "ugcr,mr->ugcm",
         particle_distribution,
@@ -47,7 +578,7 @@
     return particle_distribution + cloudy[None, :, :, None] * (mass_gain - water_removed)
 
 
-def advect(with_edges, courant_u, courant_v):
+def advect_plain(with_edges, courant_u, courant_v):
     centre = with_edges[:, 1:-1, 1:-1]
     west_side = with_edges[:, :-2, 1:-1]
     east_side = with_edges[:, 2:, 1:-1]
@@ -72,7 +603,7 @@
     return result
 
 
-def on_device(
+def plain(
     drops, capture_efficiency_matrix, transfer, courant_u, courant_v, fall_class, cloud_mask
 ):
     cloudy = cloud_mask.astype(jnp.float32)
@@ -85,13 +616,22 @@
     column_v = jnp.concatenate([courant_v, upper_v], axis=0)
     for repeat in range(STEPS):
         current = particle_distribution.shape[0]
-        coalesced_drops = collide(
+        coalesced_drops = collide_plain(
             particle_distribution, capture_efficiency_matrix, transfer, cloudy
         )
         with_edges = with_halo(coalesced_drops, (("gx", 1), ("gy", 2)), 1)
-        advected = advect(with_edges, column_u[:current], column_v[:current])
+        advected = advect_plain(with_edges, column_u[:current], column_v[:current])
         particle_distribution = sediment(advected, fall_class, current - H_MAX)
     return particle_distribution
+
+
+def on_device(*args):
+    fall_class = args[5]
+    n0 = jnp.sum((fall_class == 0).astype(jnp.int32))
+    n2 = jnp.sum((fall_class == H_MAX).astype(jnp.int32))
+    return lax.cond(
+        n2 - n0 <= SPARE, lambda a: packed(*a), lambda a: plain(*a[2:]), (n0, n2, *args)
+    )
 
 
 def solution(mesh):

time: 74.2 us -> 53.2 us (0.72)
  the two profiles are of different devices: /device:TPU:223 before, /device:TPU:6 now
where the time goes in v2:
time: 53.2 us; the launch traced here: 52.1 us
  starting transfers between devices  21.9 us (41%)
  Pallas kernels  18.8 us (35%)
  waiting for transfers between devices  6 us (11%)
  other arithmetic  2.14 us (4%)
  between operations  1.51 us (3%)
  loops' own time  0.99 us (2%)
  local copies, waits for them, and re-layouts  0.86 us (2%)
    pallas_call x7, Pallas kernels, call(): pl.pallas_call(body, out_shape=shapes, in_specs=list(specs), out_specs=ou...  18.8 us
    ppermute x1, starting transfers between devices, packed(): left = lax.ppermute(xp, 'gx', ring('gx', 1))  11.4 us
    ppermute x1, waiting for transfers between devices, packed(): right = lax.ppermute(xm, 'gx', ring('gx', -1))  5.51 us
    ppermute x1, starting transfers between devices, packed(): north0 = lax.ppermute(ym0, 'gy', ring('gy', -1))  2.95 us
    ppermute x2, starting transfers between devices, below(): lax.ppermute(value, 'gz', [(i, i - 1) for i in range(1, lax.axis_size('gz...  2.58 us
    ppermute x1, starting transfers between devices, packed(): north1 = lax.ppermute(ym1, 'gy', ring('gy', -1))  2.5 us
    ppermute x1, starting transfers between devices, packed(): right = lax.ppermute(xm, 'gx', ring('gx', -1))  1.92 us
    reduce_sum x1, other arithmetic, on_device(): n0 = jnp.sum((fall_class == 0).astype(jnp.int32))  1.37 us
  transfers between devices with their start and end apart: 8, of which 4 were waited for; matrix products, arithmetic and copies ran while one was open for 1% of the time, Pallas kernels for 19%

profile of v2, /device:TPU:6, one launch (start us, length us, event | category | flops | bytes accessed | tf_op | source)
XLA Modules:
  0.0 52.1 jit_solution(5324985527377099246)
XLA Ops:
  0.0 1.4 %fusion.39 = (s32[]{:T(128)}, s32[]{:T(128)}) fusion(s32[128]{0:T(128)} %param.14), kind=kLoop, calls=%fused_computation.80 | loop fusion | flops 766 | bytes 520 | tf_op jit(solution)/shard_map/reduce_sum | solution.py:630
  2.7 49.3 %conditional.1 = (f32[8,64,8,128]{3,2,1,0:T(8,128)}) conditional(s32[]{:T(128)} %convert_element_type.20, (s32[128]{0:T(128)}, f32[8,64,8,128]{3,2,1,0:T(8,128)}, s32[64,8]{0,1:T(8,128)}, f32[128,128]{1,0:T(8,128)}, f32[128,128]{1,0:T(8,128)}, /*index=5*/f32[8]{0:T(128)}, f32[8]{0:T(128)}) %tuple.11, (s32[]{:T(128)}, s32[]{:T(128)}, ...), branch_computations={%region_2.3_spmd, %region_3.4_spmd} | conditional | flops 8858372096 | bytes 92374296 | solution.py:632
  2.9 2.8 %branch_1_fun.7 = (f32[4096,128]{1,0:T(8,128)S(1)}, f32[528,128]{1,0:T(8,128)S(1)}, f32[648,128]{1,0:T(8,128)}, f32[512,128]{1,0:T(8,128)S(1)}, f32[648,128]{1,0...) custom-call(f32[4096,128]{1,0:T(8,128)} %bitcast.23, ...), custom_call_target="tpu_custom_call" | custom-call | flops 1000 | bytes 4194304 | tf_op jit(solution)/shard_map/cond/branch_1_fun/pallas_call | solution.py:42
  5.7 0.0 copy-start
  5.7 0.7 %copy-done = f32[512,128]{1,0:T(8,128)} copy-done((f32[512,128]{1,0:T(8,128)}, f32[512,128]{1,0:T(8,128)S(1)}, u32[]{:S(2)}) %copy-start) | copy-done | bytes 262168 | tf_op jit(solution)/shard_map/cond
  6.4 0.0 collective-permute-start
  6.4 3.0 %collective-permute-start.1 = (f32[648,128]{1,0:T(8,128)}, f32[648,128]{1,0:T(8,128)S(1)}, u32[]{:S(2)}, u32[]{:S(2)}) collective-permute-start(f32[648,128]{1,0:T(8,128)} %get-tuple-element.56), channel_id=1, source_target_pairs={{0,180},{12,0},{24,12},{36,24},{48,36},{60,48},{72,60},{84,72},{96... | collective-permute-start | bytes 995336 | tf_op jit(solution)/shard_map/cond/branch_1_fun/ppermute | solution.py:485
  10.0 0.8 %pad_add_fusion.sc = s32[2]{0:T(128)S(1)} fusion(s32[1]{0:T(128)} %bitcast.7, s32[1]{0:T(128)} %bitcast.6), kind=kLoop, calls=%fused_computation.76 | loop fusion | flops 2 | bytes 16 | tf_op jit(solution)/shard_map/cond/branch_1_fun/stack | solution.py:471
  10.8 3.4 %branch_1_fun.9.c1.c1_in = f32[4352,128]{1,0:T(8,128)S(1)} custom-call(f32[4096,128]{1,0:T(8,128)S(1)} %get-tuple-element.57.own, f32[528,128]{1,0:T(8,128)S(1)} %get-tuple-element.58.m1.m1_in, bf16[256,256]{1,0:T(8,128)(2,1)S(1)} %get-tuple-element.53.kk, bf16[256,256]{1,0:T(8,128)(2,1)S(1)} %get-tuple-element.54.tt), custom_call_target="tpu_custom_call" | custom-call | flops 3221225472 | bytes 8388608 | tf_op jit(solution)/shard_map/cond/branch_1_fun/pallas_call | solution.py:42
  14.2 0.0 copy-start.1
  14.2 0.2 collective-permute-done.south.south0
  14.4 0.0 collective-permute-done.1.north.north0
  14.4 0.0 copy-done.6
  14.4 0.1 broadcast_in_dim.42.ub
  14.5 0.0 copy-done.8
  14.5 0.1 broadcast_in_dim.43.vb
  14.5 3.5 %branch_1_fun.10 = (f32[2112,128]{1,0:T(8,128)S(1)}, f32[4224,128]{1,0:T(8,128)S(1)}, f32[1024,128]{1,0:T(8,128)S(1)}, f32[4224,128]{1,0:T(8,128)S(1)}, f32[1024...) custom-call(s32[2]{0:T(128)S(1)} %pad_add_fusion.sc, f32[8]{0:T(128)S(1)} %copy-done.6, ...), custom_call_target="tpu_custom_call" | custom-call | flops 1073741824 | bytes 4194304 | tf_op jit(solution)/shard_map/cond/branch_1_fun/pallas_call | solution.py:42
  18.0 1.3 %collective-permute-start.6 = (f32[1384,128]{1,0:T(8,128)S(1)}, f32[1384,128]{1,0:T(8,128)S(1)}, u32[]{:S(2)}, u32[]{:S(2)}) collective-permute-start(f32[1384,128]{1,0:T(8,128)S(1)} %get-tuple-element.82), channel_id=1, source_target_pairs={{1,0},{2,1},{3,2},{4,3},{5,4},{6,5},{7,6},{8,7},{9,8},{10,9},{11,1... | collective-permute-start | bytes 2125832 | tf_op jit(solution)/shard_map/cond/branch_1_fun/ppermute | solution.py:466
  19.3 0.5 collective-permute-start.4
  19.8 2.5 %collective-permute-start.5 = (f32[512,128]{1,0:T(8,128)S(1)}, f32[512,128]{1,0:T(8,128)S(1)}, u32[]{:S(2)}, u32[]{:S(2)}) collective-permute-start(f32[512,128]{1,0:T(8,128)S(1)} %get-tuple-element.69), channel_id=1, source_target_pairs={{0,180},{12,0},{24,12},{36,24},{48,36},{60,48},{72,60},{84,72},{96... | collective-permute-start | bytes 786440 | tf_op jit(solution)/shard_map/cond/branch_1_fun/ppermute | solution.py:487
  22.4 11.4 %collective-permute-start.2 = (f32[168,128]{1,0:T(8,128)S(1)}, f32[168,128]{1,0:T(8,128)S(1)}, u32[]{:S(2)}, u32[]{:S(2)}) collective-permute-start(f32[168,128]{1,0:T(8,128)S(1)} %get-tuple-element.59), channel_id=1, source_target_pairs={{0,192},{192,384},{384,576},{576,0},{1,193},{193,385},{385,577},{5... | collective-permute-start | bytes 258056 | tf_op jit(solution)/shard_map/cond/branch_1_fun/ppermute | solution.py:506
  33.8 1.9 %collective-permute-start.3 = (f32[168,128]{1,0:T(8,128)S(1)}, f32[168,128]{1,0:T(8,128)S(1)}, u32[]{:S(2)}, u32[]{:S(2)}) collective-permute-start(f32[168,128]{1,0:T(8,128)S(1)} %get-tuple-element.60), channel_id=1, source_target_pairs={{0,576},{192,0},{384,192},{576,384},{1,577},{193,1},{385,193},{577... | collective-permute-start | bytes 258056 | tf_op jit(solution)/shard_map/cond/branch_1_fun/ppermute | solution.py:507
  35.7 0.1 collective-permute-done.2.left
  35.8 5.5 %collective-permute-done.3.right = f32[168,128]{1,0:T(8,128)S(1)} collective-permute-done((f32[168,128]{1,0:T(8,128)S(1)}, f32[168,128]{1,0:T(8,128)S(1)}, u32[]{:S(2)}, u32[]{:S(2)}) %collective-permute-start.3) | collective-permute-done | bytes 86048 | tf_op jit(solution)/shard_map/cond/branch_1_fun/ppermute | solution.py:507
  41.3 1.3 %branch_1_fun.11 = (f32[4352,128]{1,0:T(8,128)S(1)}, f32[2112,128]{1,0:T(8,128)S(1)}, f32[528,128]{1,0:T(8,128)S(1)}, f32[4224,128]{1,0:T(8,128)S(1)}, f32[1024,...) custom-call(s32[2]{0:T(128)S(1)} %pad_add_fusion.sc, ...), custom_call_target="tpu_custom_call", output_to_operand_aliasing={{0}: (11, {}), {1}: (12, {}), {2}: (13, {}), {3}: (14, {}),... | custom-call | flops 268435456 | bytes 1048576 | tf_op jit(solution)/shard_map/cond/branch_1_fun/pallas_call | solution.py:42
  42.6 1.3 %collective-permute-start.7 = (f32[144,128]{1,0:T(8,128)S(1)}, f32[144,128]{1,0:T(8,128)S(1)}, u32[]{:S(2)}, u32[]{:S(2)}) collective-permute-start(f32[144,128]{1,0:T(8,128)S(1)} %get-tuple-element.83), channel_id=1, source_target_pairs={{1,0},{2,1},{3,2},{4,3},{5,4},{6,5},{7,6},{8,7},{9,8},{10,9},{11,1... | collective-permute-start | bytes 221192 | tf_op jit(solution)/shard_map/cond/branch_1_fun/ppermute | solution.py:466
  43.9 0.0 collective-permute-done.4.south1
  43.9 0.0 collective-permute-done.5.north1
  43.9 5.4 %branch_1_fun.12 = (f32[2112,128]{1,0:T(8,128)S(1)}, f32[4224,128]{1,0:T(8,128)S(1)}, f32[1024,128]{1,0:T(8,128)S(1)}, f32[4224,128]{1,0:T(8,128)S(1)}, f32[1024...) custom-call(s32[2]{0:T(128)S(1)} %pad_add_fusion.sc, ...), custom_call_target="tpu_custom_call", output_to_operand_aliasing={{0}: (13, {}), {1}: (14, {}), {2}: (15, {}), {3}: (16, {}),... | custom-call | flops 3221225472 | bytes 8388608 | tf_op jit(solution)/shard_map/cond/branch_1_fun/pallas_call | solution.py:42
  49.3 0.1 collective-permute-done.7.late
  49.5 0.0 collective-permute-done.6.early
  49.5 2.5 %branch_1_fun.13 = (f32[4096,128]{1,0:T(8,128)}, f32[4224,128]{1,0:T(8,128)S(1)}, f32[1024,128]{1,0:T(8,128)S(1)}, f32[4096,128]{1,0:T(8,128)S(1)}) custom-call(s32[2]{0:T(128)S(1)} %pad_add_fusion.sc, f32[8]{0:T(128)S(1)} %copy-done.6, f32[8]{0:T(128)S(1)} %copy-done.8, ...), custom_call_target="tpu_custom_call", output_to_operand_aliasing={{0}: (15, {}), {1}: (10, {}), {2}: (11, {}), {3}: (12, {})} | custom-call | flops 1073741824 | bytes 8388608 | tf_op jit(solution)/shard_map/cond/branch_1_fun/pallas_call | solution.py:42
  (4 shorter events, 0.0 us)
Async XLA Ops:
  5.7 0.7 %copy-start = (f32[512,128]{1,0:T(8,128)}, f32[512,128]{1,0:T(8,128)S(1)}, u32[]{:S(2)}) copy-start(f32[512,128]{1,0:T(8,128)S(1)} %get-tuple-element.68) | copy-start | bytes 786436 | tf_op jit(solution)/shard_map/cond
  6.4 8.0 %collective-permute-start = (f32[648,128]{1,0:T(8,128)}, f32[648,128]{1,0:T(8,128)S(1)}, u32[]{:S(2)}, u32[]{:S(2)}) collective-permute-start(f32[648,128]{1,0:T(8,128)} %get-tuple-element.55), channel_id=1, source_target_pairs={{0,12},{12,24},{24,36},{36,48},{48,60},{60,72},{72,84},{84,96},{96... | collective-permute-start | bytes 995336 | tf_op jit(solution)/shard_map/cond/branch_1_fun/ppermute | solution.py:484
  6.4 8.0 %collective-permute-start.1 = (f32[648,128]{1,0:T(8,128)}, f32[648,128]{1,0:T(8,128)S(1)}, u32[]{:S(2)}, u32[]{:S(2)}) collective-permute-start(f32[648,128]{1,0:T(8,128)} %get-tuple-element.56), channel_id=1, source_target_pairs={{0,180},{12,0},{24,12},{36,24},{48,36},{60,48},{72,60},{84,72},{96... | collective-permute-start | bytes 995336 | tf_op jit(solution)/shard_map/cond/branch_1_fun/ppermute | solution.py:485
  10.8 3.6 %copy-start.6 = (f32[8]{0:T(128)S(1)}, f32[8]{0:T(128)}, u32[]{:S(2)}) copy-start(f32[8]{0:T(128)} %get-tuple-element.47.u_ref) | copy-start | bytes 100 | tf_op jit(solution)/shard_map/cond
  10.8 3.7 %copy-start.8 = (f32[8]{0:T(128)S(1)}, f32[8]{0:T(128)}, u32[]{:S(2)}) copy-start(f32[8]{0:T(128)} %get-tuple-element.48.v_ref) | copy-start | bytes 100 | tf_op jit(solution)/shard_map/cond
  14.2 5.1 %copy-start.1 = (f32[512,128]{1,0:T(8,128)S(1)}, f32[512,128]{1,0:T(8,128)}, u32[]{:S(2)}) copy-start(f32[512,128]{1,0:T(8,128)} %copy-done) | copy-start | bytes 786436 | tf_op jit(solution)/shard_map/cond
  18.0 31.5 %collective-permute-start.6 = (f32[1384,128]{1,0:T(8,128)S(1)}, f32[1384,128]{1,0:T(8,128)S(1)}, u32[]{:S(2)}, u32[]{:S(2)}) collective-permute-start(f32[1384,128]{1,0:T(8,128)S(1)} %get-tuple-element.82), channel_id=1, source_target_pairs={{1,0},{2,1},{3,2},{4,3},{5,4},{6,5},{7,6},{8,7},{9,8},{10,9},{11,1... | collective-permute-start | bytes 2125832 | tf_op jit(solution)/shard_map/cond/branch_1_fun/ppermute | solution.py:466
  19.3 24.6 %collective-permute-start.4 = (f32[512,128]{1,0:T(8,128)S(1)}, f32[512,128]{1,0:T(8,128)S(1)}, u32[]{:S(2)}, u32[]{:S(2)}) collective-permute-start(f32[512,128]{1,0:T(8,128)S(1)} %copy-done.1), channel_id=1, source_target_pairs={{0,12},{12,24},{24,36},{36,48},{48,60},{60,72},{72,84},{84,96},{96... | collective-permute-start | bytes 786440 | tf_op jit(solution)/shard_map/cond/branch_1_fun/ppermute | solution.py:486
  19.8 24.1 %collective-permute-start.5 = (f32[512,128]{1,0:T(8,128)S(1)}, f32[512,128]{1,0:T(8,128)S(1)}, u32[]{:S(2)}, u32[]{:S(2)}) collective-permute-start(f32[512,128]{1,0:T(8,128)S(1)} %get-tuple-element.69), channel_id=1, source_target_pairs={{0,180},{12,0},{24,12},{36,24},{48,36},{60,48},{72,60},{84,72},{96... | collective-permute-start | bytes 786440 | tf_op jit(solution)/shard_map/cond/branch_1_fun/ppermute | solution.py:487
  22.4 13.5 %collective-permute-start.2 = (f32[168,128]{1,0:T(8,128)S(1)}, f32[168,128]{1,0:T(8,128)S(1)}, u32[]{:S(2)}, u32[]{:S(2)}) collective-permute-start(f32[168,128]{1,0:T(8,128)S(1)} %get-tuple-element.59), channel_id=1, source_target_pairs={{0,192},{192,384},{384,576},{576,0},{1,193},{193,385},{385,577},{5... | collective-permute-start | bytes 258056 | tf_op jit(solution)/shard_map/cond/branch_1_fun/ppermute | solution.py:506
  33.8 7.6 %collective-permute-start.3 = (f32[168,128]{1,0:T(8,128)S(1)}, f32[168,128]{1,0:T(8,128)S(1)}, u32[]{:S(2)}, u32[]{:S(2)}) collective-permute-start(f32[168,128]{1,0:T(8,128)S(1)} %get-tuple-element.60), channel_id=1, source_target_pairs={{0,576},{192,0},{384,192},{576,384},{1,577},{193,1},{385,193},{577... | collective-permute-start | bytes 258056 | tf_op jit(solution)/shard_map/cond/branch_1_fun/ppermute | solution.py:507
  42.6 6.9 %collective-permute-start.7 = (f32[144,128]{1,0:T(8,128)S(1)}, f32[144,128]{1,0:T(8,128)S(1)}, u32[]{:S(2)}, u32[]{:S(2)}) collective-permute-start(f32[144,128]{1,0:T(8,128)S(1)} %get-tuple-element.83), channel_id=1, source_target_pairs={{1,0},{2,1},{3,2},{4,3},{5,4},{6,5},{7,6},{8,7},{9,8},{10,9},{11,1... | collective-permute-start | bytes 221192 | tf_op jit(solution)/shard_map/cond/branch_1_fun/ppermute | solution.py:466

commit v3 on v2

--- a/solution.py
+++ b/solution.py
@@ -13,9 +13,7 @@
 T = 8
 XW = X + 4
 XA = X + 2
-LOW = Z // 2
-HALF = 2 * LOW * X
-ENDS = HALF + 2 * X
+HALO = 2 * Z * X
 XROWS = 2 * Z * Y
 EARLY = (X - 2) + 2 * X // T + (X - 4)
 GROUPS = 4
@@ -83,7 +81,7 @@
     return jnp.where(c0, a, jnp.where(c2, c, b))
 
 
-def edges_body(drops, cloud, k_in, t_in, own, m1, ym0, ym1, yp0, yp1, kk, tt, mask, k_ref, t_ref, sem):
+def edges_body(drops, cloud, k_in, t_in, own, m1, ym, yp, kk, tt, mask, k_ref, t_ref, sem):
     copies = [
         pltpu.make_async_copy(a, b, sem.at[i])
         for i, (a, b) in enumerate(((drops, own), (cloud, mask), (k_in, k_ref), (t_in, t_ref)))
@@ -100,20 +98,15 @@
         high, low = split(w)
         half = jnp.concatenate([high, low], axis=1)
         out[...] = jnp.concatenate([half, half], axis=0)
-    for out, ys in ((ym0, (0, 1)), (yp0, (Y - 1, Y - 2))):
+    for out, ys in ((ym, (0, 1)), (yp, (Y - 1, Y - 2))):
         for d, y in enumerate(ys):
-            out[HALF + d * X : HALF + (d + 1) * X] = m1[pl.ds(Y + y, X, stride=Y), :]
+            out[HALO + d * X : HALO + (d + 1) * X] = m1[pl.ds(Y + y, X, stride=Y), :]
     copies[0].wait()
-    for outs, ys in (((ym0, ym1), (0, 1)), ((yp0, yp1), (Y - 1, Y - 2))):
-        for part, out in enumerate(outs):
-            for d, y in enumerate(ys):
-                for z in range(LOW):
-                    at = (d * LOW + z) * X
-                    start = (part * LOW + z) * X * Y + y
-                    out[at : at + X] = own[pl.ds(start, X, stride=Y), :]
-        for i, x in enumerate((0, X - 1)):
-            at, start = ENDS + i * LOW, (LOW * X + x) * Y + ys[0]
-            outs[0][at : at + LOW] = own[pl.ds(start, LOW, stride=X * Y), :]
+    for out, ys in ((ym, (0, 1)), (yp, (Y - 1, Y - 2))):
+        for d, y in enumerate(ys):
+            for z in range(Z):
+                at = (d * Z + z) * X
+                out[at : at + X] = own[pl.ds(z * X * Y + y, X, stride=Y), :]
 
 
 def sides_body(own, m1, south, north, xm, xp):
@@ -128,11 +121,9 @@
         out[at + 2 * Z :] = jnp.zeros((T, B), F32)
         for side, ref in enumerate((south, north)):
             row = at + side * Z
-            end = ENDS + (LOW if x else 0)
-            out[row : row + LOW] = ref[pl.ds(x, LOW, stride=X), :]
-            out[row + LOW : row + Z] = ref[end : end + LOW]
+            out[row : row + Z] = ref[pl.ds(x, Z, stride=X), :]
             row = at + 2 * Z + side
-            out[row : row + 1] = ref[HALF + x : HALF + x + 1]
+            out[row : row + 1] = ref[HALO + x : HALO + x + 1]
 
 
 XMESSAGE = XROWS + 2 * Y + 2 * Z + T
@@ -145,20 +136,20 @@
         c1[rows((z * XW + 2) * Y, X * Y)] = collide(own[rows(z * X * Y, X * Y)], mask, k, t)
         return 0
 
-    lax.fori_loop(0, Z, level, 0)
+    lax.fori_loop(0, Z, level, 0, unroll=4)
 
 
 def cy_at(side, d, x):
     return ((side * 2 + d) * XA + x + 1) * Z
 
 
-def collide_rows(part, south, north, masks, cy, k, t):
-    for side, (ref, mask_ref) in enumerate(zip((south, north), masks)):
+def collide_rows(south, north, cy, k, t):
+    for side, ref in enumerate((south, north)):
         for d in range(2):
-            mask = jnp.concatenate([mask_ref[HALF + d * X : HALF + (d + 1) * X]] * LOW, axis=0)
-            c = collide(ref[d * LOW * X : (d + 1) * LOW * X], mask, k, t)
-            for z in range(LOW):
-                cy[pl.ds(cy_at(side, d, 0) + part * LOW + z, X, stride=Z), :] = c[z * X : (z + 1) * X]
+            mask = jnp.concatenate([ref[HALO + d * X : HALO + (d + 1) * X]] * Z, axis=0)
+            c = collide(ref[d * Z * X : (d + 1) * Z * X], mask, k, t)
+            for z in range(Z):
+                cy[pl.ds(cy_at(side, d, 0) + z, X, stride=Z), :] = c[z * X : (z + 1) * X]
 
 
 def upwind(z, u_ref, v_ref):
@@ -230,7 +221,7 @@
         to = z * 2 * X + i * T
         c2y[to : to + T] = fall(c0, cc2, *a)
     at = slice(z * 2 * X, (z + 1) * 2 * X)
-    mask = jnp.concatenate([m[HALF : HALF + X] for m in masks], axis=0)
+    mask = jnp.concatenate([m[HALO : HALO + X] for m in masks], axis=0)
     c2y[at] = collide(c2y[at], mask, k, t)
 
 
@@ -250,7 +241,7 @@
 ):
     k, t = kk[...], tt[...]
     c0, cc2 = classes(sc)
-    collide_rows(0, south, north, (south, north), cy, k, t)
+    collide_rows(south, north, cy, k, t)
 
     def first(z, _):
         advect_first(z, range(2, X), c1, a1, cy, u_ref, v_ref)
@@ -263,7 +254,7 @@
         settle_level(z, c0, cc2, a1, m1, c2, k, t)
         return 0
 
-    lax.fori_loop(0, 2, second, 0)
+    lax.fori_loop(0, 2, second, 0, unroll=2)
     for z in range(2):
         settle_rows(z, c0, cc2, a1y, (south, north), c2y, k, t)
 
@@ -355,13 +346,12 @@
 
 
 def rest_body(
-    sc, u_ref, v_ref, ub, vb, kk, tt, south0, south1, north0, north1, c1, m1,
-    cy_in, a1_in, a1y_in, c2_in, c2y_in, a2_in,
-    cy, a1, a1y, c2, c2y, a2, out, res, sem,
+    sc, u_ref, v_ref, ub, vb, kk, tt, south, north, c1, m1, cy,
+    a1_in, a1y_in, c2_in, c2y_in, a2_in,
+    a1, a1y, c2, c2y, a2, out, res, sem,
 ):
     k, t = kk[...], tt[...]
     c0, cc2 = classes(sc)
-    collide_rows(1, south1, north1, (south0, north0), cy, k, t)
 
     def first(z, _):
         advect_first(z, range(XA), c1, a1, cy, u_ref, v_ref)
@@ -374,9 +364,9 @@
         settle_level(z, c0, cc2, a1, m1, c2, k, t)
         return 0
 
-    lax.fori_loop(2, 6, second, 0)
+    lax.fori_loop(2, 6, second, 0, unroll=4)
     for z in range(2, 6):
-        settle_rows(z, c0, cc2, a1y, (south0, north0), c2y, k, t)
+        settle_rows(z, c0, cc2, a1y, (south, north), c2y, k, t)
 
     def third(z, _):
         advect_second(z, range(X), c2, a2, c2y, u_ref, v_ref)
@@ -431,7 +421,7 @@
         at = 6 * 2 * X + i * T
         c2y[at : at + T] = fall(c0, cc2, x6, x7, row6[i * T : (i + 1) * T])
         c2y[at + 2 * X : at + 2 * X + T] = jnp.where(c0, x7, row7[i * T : (i + 1) * T])
-    mask = jnp.concatenate([south[HALF : HALF + X], north[HALF : HALF + X]] * 2, axis=0)
+    mask = jnp.concatenate([south[HALO : HALO + X], north[HALO : HALO + X]] * 2, axis=0)
     at = slice(12 * X, 16 * X)
     c2y[at] = collide(c2y[at], mask, k, t)
     for z in (6, 7):
@@ -473,25 +463,23 @@
     vb = jnp.broadcast_to(courant_v[:, None], (Z, B))
     v = lambda n, d=F32: ((n, B), d, True)
     weights = [((2 * B, 2 * B), BF16, True)] * 2
-    own, m1, ym0, ym1, yp0, yp1, kk, tt = call(
+    own, m1, ym, yp, kk, tt = call(
         edges_body,
-        [v(Z * X * Y), v(XA * Y), v(ENDS + T), v(HALF), v(ENDS + T), v(HALF)] + weights,
+        [v(Z * X * Y), v(XA * Y), v(HALO + 2 * X), v(HALO + 2 * X)] + weights,
         [drops, cloud_mask.T, capture, transfer],
         [HBM] * 4,
         [pltpu.VMEM((Y, X), jnp.int32), pltpu.VMEM((B, B), F32), pltpu.VMEM((B, B), F32), pltpu.SemaphoreType.DMA((4,))],
         cost=(1000, 4 << 20),
     )
-    south0 = lax.ppermute(yp0, "gy", ring("gy", 1))
-    north0 = lax.ppermute(ym0, "gy", ring("gy", -1))
-    south1 = lax.ppermute(yp1, "gy", ring("gy", 1))
-    north1 = lax.ppermute(ym1, "gy", ring("gy", -1))
+    south = lax.ppermute(yp, "gy", ring("gy", 1))
+    north = lax.ppermute(ym, "gy", ring("gy", -1))
     (c1,) = call(own_body, [v(Z * XW * Y)], [own, m1, kk, tt], [VMEM] * 4, cost=(3 << 30, 8 << 20))
     shapes = [v(4 * XA * Z), v(Z * XA * T), v(2 * X * Z), v(Z * XA * T), v(Z * 2 * X), v(Z * X * T)]
     scalars = [sc, courant_u, courant_v]
     cy, a1, a1y, c2, c2y, a2, pay = call(
         early_body,
         shapes + [v((EARLY + EXTRA) * T)],
-        scalars + [ub, vb, c1, south0, north0, kk, tt, m1],
+        scalars + [ub, vb, c1, south, north, kk, tt, m1],
         [SMEM] * 3 + [VMEM] * 8,
         cost=(1 << 30, 4 << 20),
     )
@@ -499,7 +487,7 @@
     xm, xp = call(
         sides_body,
         [v(XMESSAGE)] * 2,
-        [own, m1, south0, north0],
+        [own, m1, south, north],
         [VMEM] * 4,
         cost=(1000, 1 << 18),
     )
@@ -508,7 +496,7 @@
     c1, cy, m1, a1, a1y, c2, c2y, a2, pay = call(
         late_body,
         [v(Z * XW * Y), shapes[0], v(XA * Y)] + shapes[1:] + [v(2 * LATE * T)],
-        scalars + [ub, vb, left, right, kk, tt, south0, north0, c1, cy, m1, a1, a1y, c2, c2y, a2],
+        scalars + [ub, vb, left, right, kk, tt, south, north, c1, cy, m1, a1, a1y, c2, c2y, a2],
         [SMEM] * 3 + [VMEM] * 16,
         cost=(1 << 28, 1 << 20),
         aliases={11 + i: i for i in range(8)},
@@ -516,19 +504,19 @@
     late = below(pay)
     *state, out = call(
         rest_body,
-        shapes + [((Z * X * Y, B), F32, False)],
-        scalars + [ub, vb, kk, tt, south0, south1, north0, north1, c1, m1, cy, a1, a1y, c2, c2y, a2],
-        [SMEM] * 3 + [VMEM] * 16,
+        shapes[1:] + [((Z * X * Y, B), F32, False)],
+        scalars + [ub, vb, kk, tt, south, north, c1, m1, cy, a1, a1y, c2, c2y, a2],
+        [SMEM] * 3 + [VMEM] * 14,
         [pltpu.VMEM((4 * X * T, B), F32), pltpu.SemaphoreType.DMA],
         cost=(3 << 30, 8 << 20),
-        out_specs=[VMEM] * 6 + [HBM],
-        aliases={13 + i: i for i in range(6)},
-    )
-    (cy, a1, a1y, c2, c2y, a2) = state
+        out_specs=[VMEM] * 5 + [HBM],
+        aliases={12 + i: i for i in range(5)},
+    )
+    a1, a1y, c2, c2y, a2 = state
     out, *_ = call(
         last_body,
         [((Z * X * Y, B), F32, False), shapes[3], shapes[4], shapes[5]],
-        scalars + [kk, tt, south0, north0, m1, a1, a1y, c2, c2y, a2, early, late, out],
+        scalars + [kk, tt, south, north, m1, a1, a1y, c2, c2y, a2, early, late, out],
         [SMEM] * 3 + [VMEM] * 12 + [HBM],
         [pltpu.VMEM((2 * X, B), F32), pltpu.VMEM((2 * X, B), F32), pltpu.VMEM((4 * X * T, B), F32), pltpu.SemaphoreType.DMA],
         cost=(1 << 30, 8 << 20),

time: 53.2 us -> 52.7 us (level); the launches traced: 52.1 us -> 52.4 us
  waiting for transfers between devices: 6 us -> 10.2 us
  Pallas kernels: 18.8 us -> 15.6 us
  starting transfers between devices: 21.9 us -> 18.9 us
  local copies, waits for them, and re-layouts: 0.86 us -> 3.25 us
    pallas_call x7, Pallas kernels: 18.8 us -> 15.6 us  [call(): pl.pallas_call(body, out_shape=shapes, in_specs=list(specs), out_specs=ou...]
    ppermute x4 -> x2, starting transfers between devices: 5.95 us -> 2.96 us  [the longest x1 2.95 us: packed(): north = lax.ppermute(ym, 'gy', ring('gy', -1))]
    ppermute x4 -> x2, waiting for transfers between devices: 0.2 us -> 2.88 us  [the longest x1 2.88 us: packed(): south = lax.ppermute(yp, 'gy', ring('gy', 1))]
    cond x8 -> x16, local copies, waits for them, and re-layouts: 0.73 us -> 3.11 us
    ppermute x2, waiting for transfers between devices: 0.14 us -> 1.69 us  [below(): lax.ppermute(value, 'gz', [(i, i - 1) for i in range(1, lax.axis_size('gz...]
  transfers between devices with their start and end apart: 8 -> 6, of which waited for: 4 -> 4; matrix products, arithmetic and copies ran while one was open for 1% -> 1% of each run, Pallas kernels for 19% -> 13%
where the time goes in v3:
time: 52.7 us; the launch traced here: 52.4 us
  starting transfers between devices  18.9 us (36%)
  Pallas kernels  15.6 us (30%)
  waiting for transfers between devices  10.2 us (19%)
  local copies, waits for them, and re-layouts  3.25 us (6%)
  other arithmetic  2.04 us (4%)
  between operations  1.43 us (3%)
  loops' own time  0.97 us (2%)
    pallas_call x7, Pallas kernels, call(): pl.pallas_call(body, out_shape=shapes, in_specs=list(specs), out_specs=ou...  15.6 us
    ppermute x1, starting transfers between devices, packed(): left = lax.ppermute(xp, 'gx', ring('gx', 1))  11.4 us
    ppermute x1, waiting for transfers between devices, packed(): right = lax.ppermute(xm, 'gx', ring('gx', -1))  5.51 us
    cond x16, local copies, waits for them, and re-layouts  3.11 us
    ppermute x1, starting transfers between devices, packed(): north = lax.ppermute(ym, 'gy', ring('gy', -1))  2.95 us
    ppermute x1, waiting for transfers between devices, packed(): south = lax.ppermute(yp, 'gy', ring('gy', 1))  2.88 us
    ppermute x2, starting transfers between devices, below(): lax.ppermute(value, 'gz', [(i, i - 1) for i in range(1, lax.axis_size('gz...  2.58 us
    ppermute x1, starting transfers between devices, packed(): right = lax.ppermute(xm, 'gx', ring('gx', -1))  1.92 us
  transfers between devices with their start and end apart: 6, of which 4 were waited for; matrix products, arithmetic and copies ran while one was open for 1% of the time, Pallas kernels for 13%

profile of v3, /device:TPU:6, one launch (start us, length us, event | category | flops | bytes accessed | tf_op | source)
XLA Modules:
  0.0 52.4 jit_solution(1849891942434798180)
XLA Ops:
  0.0 1.4 %fusion.39 = (s32[]{:T(128)}, s32[]{:T(128)}) fusion(s32[128]{0:T(128)} %param.14), kind=kLoop, calls=%fused_computation.80 | loop fusion | flops 766 | bytes 520 | tf_op jit(solution)/shard_map/reduce_sum | solution.py:618
  2.6 49.6 %conditional.1 = (f32[8,64,8,128]{3,2,1,0:T(8,128)}) conditional(s32[]{:T(128)} %convert_element_type.20, (s32[128]{0:T(128)}, f32[8,64,8,128]{3,2,1,0:T(8,128)}, s32[64,8]{0,1:T(8,128)}, f32[128,128]{1,0:T(8,128)}, f32[128,128]{1,0:T(8,128)}, /*index=5*/f32[8]{0:T(128)}, f32[8]{0:T(128)}) %tuple.11, (s32[]{:T(128)}, s32[]{:T(128)}, ...), branch_computations={%region_2.3_spmd, %region_3.4_spmd} | conditional | flops 8858372096 | bytes 92374296 | solution.py:620
  2.9 3.0 %branch_1_fun.7 = (f32[4096,128]{1,0:T(8,128)S(1)}, f32[528,128]{1,0:T(8,128)S(1)}, f32[1152,128]{1,0:T(8,128)}, f32[1152,128]{1,0:T(8,128)}, bf16[256,256]{1,0:...) custom-call(f32[4096,128]{1,0:T(8,128)} %bitcast.23, s32[8,64]{1,0:T(8,128)} %bitcast.24, f32[128,128]{1,0:T(8,128)} %get-tuple-element.51.k_in, ...), custom_call_target="tpu_custom_call" | custom-call | flops 1000 | bytes 4194304 | tf_op jit(solution)/shard_map/cond/branch_1_fun/pallas_call | solution.py:40
  5.8 0.0 copy-start
  5.8 0.6 %copy-done = bf16[256,256]{1,0:T(8,128)(2,1)} copy-done((bf16[256,256]{1,0:T(8,128)(2,1)}, bf16[256,256]{1,0:T(8,128)(2,1)S(1)}, u32[]{:S(2)}) %copy-start) | copy-done | bytes 131096 | tf_op jit(solution)/shard_map/cond
  6.5 0.7 %copy-done.3 = bf16[256,256]{1,0:T(8,128)(2,1)} copy-done((bf16[256,256]{1,0:T(8,128)(2,1)}, bf16[256,256]{1,0:T(8,128)(2,1)S(1)}, u32[]{:S(2)}) %copy-start.3) | copy-done | bytes 131096 | tf_op jit(solution)/shard_map/cond
  7.1 0.0 collective-permute-start
  7.1 3.0 %collective-permute-start.1 = (f32[1152,128]{1,0:T(8,128)}, f32[1152,128]{1,0:T(8,128)S(1)}, u32[]{:S(2)}, u32[]{:S(2)}) collective-permute-start(f32[1152,128]{1,0:T(8,128)} %get-tuple-element.56), channel_id=1, source_target_pairs={{0,180},{12,0},{24,12},{36,24},{48,36},{60,48},{72,60},{84,72},{96... | collective-permute-start | bytes 1769480 | tf_op jit(solution)/shard_map/cond/branch_1_fun/ppermute | solution.py:475
  10.7 0.7 %pad_add_fusion.sc = s32[2]{0:T(128)S(1)} fusion(s32[1]{0:T(128)} %bitcast.7, s32[1]{0:T(128)} %bitcast.6), kind=kLoop, calls=%fused_computation.76 | loop fusion | flops 2 | bytes 16 | tf_op jit(solution)/shard_map/cond/branch_1_fun/stack | solution.py:461
  11.4 0.9 %copy-done.1 = bf16[256,256]{1,0:T(8,128)(2,1)S(1)} copy-done((bf16[256,256]{1,0:T(8,128)(2,1)S(1)}, bf16[256,256]{1,0:T(8,128)(2,1)}, u32[]{:S(2)}) %copy-start.1) | copy-done | bytes 131096 | tf_op jit(solution)/shard_map/cond
  12.3 0.9 %copy-done.4 = bf16[256,256]{1,0:T(8,128)(2,1)S(1)} copy-done((bf16[256,256]{1,0:T(8,128)(2,1)S(1)}, bf16[256,256]{1,0:T(8,128)(2,1)}, u32[]{:S(2)}) %copy-start.4) | copy-done | bytes 131096 | tf_op jit(solution)/shard_map/cond
  13.2 1.7 %branch_1_fun.9.c1.c1_in = f32[4352,128]{1,0:T(8,128)S(1)} custom-call(f32[4096,128]{1,0:T(8,128)S(1)} %get-tuple-element.57.own, f32[528,128]{1,0:T(8,128)S(1)} %get-tuple-element.58.m1.m1_in, bf16[256,256]{1,0:T(8,128)(2,1)S(1)} %copy-done.1, bf16[256,256]{1,0:T(8,128)(2,1)S(1)} %copy-done.4), custom_call_target="tpu_custom_call" | custom-call | flops 3221225472 | bytes 8388608 | tf_op jit(solution)/shard_map/cond/branch_1_fun/pallas_call | solution.py:40
  15.0 2.9 %collective-permute-done.south = f32[1152,128]{1,0:T(8,128)S(1)} collective-permute-done((f32[1152,128]{1,0:T(8,128)}, f32[1152,128]{1,0:T(8,128)S(1)}, u32[]{:S(2)}, u32[]{:S(2)}) %collective-permute-start) | collective-permute-done | bytes 589856 | tf_op jit(solution)/shard_map/cond/branch_1_fun/ppermute | solution.py:474
  17.9 0.0 collective-permute-done.1.north
  17.9 0.0 copy-done.10
  17.9 0.1 broadcast_in_dim.42.ub
  17.9 0.0 copy-done.12
  17.9 0.1 broadcast_in_dim.43.vb
  18.0 0.0 copy-done.2
  18.0 0.0 copy-done.5
  18.0 3.2 %branch_1_fun.10 = (f32[2112,128]{1,0:T(8,128)S(1)}, f32[4224,128]{1,0:T(8,128)S(1)}, f32[1024,128]{1,0:T(8,128)S(1)}, f32[4224,128]{1,0:T(8,128)S(1)}, f32[1024...) custom-call(s32[2]{0:T(128)S(1)} %pad_add_fusion.sc, f32[8]{0:T(128)S(1)} %copy-done.10, ...), custom_call_target="tpu_custom_call" | custom-call | flops 1073741824 | bytes 4194304 | tf_op jit(solution)/shard_map/cond/branch_1_fun/pallas_call | solution.py:40
  21.3 1.3 %collective-permute-start.4 = (f32[1384,128]{1,0:T(8,128)S(1)}, f32[1384,128]{1,0:T(8,128)S(1)}, u32[]{:S(2)}, u32[]{:S(2)}) collective-permute-start(f32[1384,128]{1,0:T(8,128)S(1)} %get-tuple-element.80), channel_id=1, source_target_pairs={{1,0},{2,1},{3,2},{4,3},{5,4},{6,5},{7,6},{8,7},{9,8},{10,9},{11,1... | collective-permute-start | bytes 2125832 | tf_op jit(solution)/shard_map/cond/branch_1_fun/ppermute | solution.py:456
  22.6 11.4 %collective-permute-start.2 = (f32[168,128]{1,0:T(8,128)S(1)}, f32[168,128]{1,0:T(8,128)S(1)}, u32[]{:S(2)}, u32[]{:S(2)}) collective-permute-start(f32[168,128]{1,0:T(8,128)S(1)} %get-tuple-element.59), channel_id=1, source_target_pairs={{0,192},{192,384},{384,576},{576,0},{1,193},{193,385},{385,577},{5... | collective-permute-start | bytes 258056 | tf_op jit(solution)/shard_map/cond/branch_1_fun/ppermute | solution.py:494
  34.0 1.9 %collective-permute-start.3 = (f32[168,128]{1,0:T(8,128)S(1)}, f32[168,128]{1,0:T(8,128)S(1)}, u32[]{:S(2)}, u32[]{:S(2)}) collective-permute-start(f32[168,128]{1,0:T(8,128)S(1)} %get-tuple-element.60), channel_id=1, source_target_pairs={{0,576},{192,0},{384,192},{576,384},{1,577},{193,1},{385,193},{577... | collective-permute-start | bytes 258056 | tf_op jit(solution)/shard_map/cond/branch_1_fun/ppermute | solution.py:495
  35.9 0.1 collective-permute-done.2.left
  36.1 5.5 %collective-permute-done.3.right = f32[168,128]{1,0:T(8,128)S(1)} collective-permute-done((f32[168,128]{1,0:T(8,128)S(1)}, f32[168,128]{1,0:T(8,128)S(1)}, u32[]{:S(2)}, u32[]{:S(2)}) %collective-permute-start.3) | collective-permute-done | bytes 86048 | tf_op jit(solution)/shard_map/cond/branch_1_fun/ppermute | solution.py:495
  41.6 1.3 %branch_1_fun.11 = (f32[4352,128]{1,0:T(8,128)S(1)}, f32[2112,128]{1,0:T(8,128)S(1)}, f32[528,128]{1,0:T(8,128)S(1)}, f32[4224,128]{1,0:T(8,128)S(1)}, f32[1024,...) custom-call(s32[2]{0:T(128)S(1)} %pad_add_fusion.sc, ...), custom_call_target="tpu_custom_call", output_to_operand_aliasing={{0}: (11, {}), {1}: (12, {}), {2}: (13, {}), {3}: (14, {}),... | custom-call | flops 268435456 | bytes 1048576 | tf_op jit(solution)/shard_map/cond/branch_1_fun/pallas_call | solution.py:40
  42.9 1.3 %collective-permute-start.5 = (f32[144,128]{1,0:T(8,128)S(1)}, f32[144,128]{1,0:T(8,128)S(1)}, u32[]{:S(2)}, u32[]{:S(2)}) collective-permute-start(f32[144,128]{1,0:T(8,128)S(1)} %get-tuple-element.81), channel_id=1, source_target_pairs={{1,0},{2,1},{3,2},{4,3},{5,4},{6,5},{7,6},{8,7},{9,8},{10,9},{11,1... | collective-permute-start | bytes 221192 | tf_op jit(solution)/shard_map/cond/branch_1_fun/ppermute | solution.py:456
  44.2 3.9 %branch_1_fun.12 = (f32[4224,128]{1,0:T(8,128)S(1)}, f32[1024,128]{1,0:T(8,128)S(1)}, f32[4224,128]{1,0:T(8,128)S(1)}, f32[1024,128]{1,0:T(8,128)S(1)}, f32[4096,128]{1,0:T(8,128)S(1)}, /*index=5*/f32[4096,128]{1,0:T(8,128)}) custom-call(s32[2]{0:T(128)S(1)} %pad_add_fusion.sc, ...), custom_call_target="tpu_custom_call", output_to_operand_aliasing={{0}: (12, {}), {1}: (13, {}), {2}: (14, {}), {3}: (15, {}),... | custom-call | flops 3221225472 | bytes 8388608 | tf_op jit(solution)/shard_map/cond/branch_1_fun/pallas_call | solution.py:40
  48.1 1.7 %collective-permute-done.5.late = f32[144,128]{1,0:T(8,128)S(1)} collective-permute-done((f32[144,128]{1,0:T(8,128)S(1)}, f32[144,128]{1,0:T(8,128)S(1)}, u32[]{:S(2)}, u32[]{:S(2)}) %collective-permute-start.5) | collective-permute-done | bytes 73760 | tf_op jit(solution)/shard_map/cond/branch_1_fun/ppermute | solution.py:456
  49.7 0.0 collective-permute-done.4.early
  49.8 2.5 %branch_1_fun.13 = (f32[4096,128]{1,0:T(8,128)}, f32[4224,128]{1,0:T(8,128)S(1)}, f32[1024,128]{1,0:T(8,128)S(1)}, f32[4096,128]{1,0:T(8,128)S(1)}) custom-call(s32[2]{0:T(128)S(1)} %pad_add_fusion.sc, f32[8]{0:T(128)S(1)} %copy-done.10, f32[8]{0:T(128)S(1)} %copy-done.12, ...), custom_call_target="tpu_custom_call", output_to_operand_aliasing={{0}: (15, {}), {1}: (10, {}), {2}: (11, {}), {3}: (12, {})} | custom-call | flops 1073741824 | bytes 8388608 | tf_op jit(solution)/shard_map/cond/branch_1_fun/pallas_call | solution.py:40
  (8 shorter events, 0.0 us)
Async XLA Ops:
  5.8 0.6 %copy-start = (bf16[256,256]{1,0:T(8,128)(2,1)}, bf16[256,256]{1,0:T(8,128)(2,1)S(1)}, u32[]{:S(2)}) copy-start(bf16[256,256]{1,0:T(8,128)(2,1)S(1)} %get-tuple-element.53.kk) | copy-start | bytes 393220 | tf_op jit(solution)/shard_map/cond
  6.5 0.7 %copy-start.3 = (bf16[256,256]{1,0:T(8,128)(2,1)}, bf16[256,256]{1,0:T(8,128)(2,1)S(1)}, u32[]{:S(2)}) copy-start(bf16[256,256]{1,0:T(8,128)(2,1)S(1)} %get-tuple-element.54.tt) | copy-start | bytes 393220 | tf_op jit(solution)/shard_map/cond
  7.1 10.7 %collective-permute-start = (f32[1152,128]{1,0:T(8,128)}, f32[1152,128]{1,0:T(8,128)S(1)}, u32[]{:S(2)}, u32[]{:S(2)}) collective-permute-start(f32[1152,128]{1,0:T(8,128)} %get-tuple-element.55), channel_id=1, source_target_pairs={{0,12},{12,24},{24,36},{36,48},{48,60},{60,72},{72,84},{84,96},{96... | collective-permute-start | bytes 1769480 | tf_op jit(solution)/shard_map/cond/branch_1_fun/ppermute | solution.py:474
  7.1 10.7 %collective-permute-start.1 = (f32[1152,128]{1,0:T(8,128)}, f32[1152,128]{1,0:T(8,128)S(1)}, u32[]{:S(2)}, u32[]{:S(2)}) collective-permute-start(f32[1152,128]{1,0:T(8,128)} %get-tuple-element.56), channel_id=1, source_target_pairs={{0,180},{12,0},{24,12},{36,24},{48,36},{60,48},{72,60},{84,72},{96... | collective-permute-start | bytes 1769480 | tf_op jit(solution)/shard_map/cond/branch_1_fun/ppermute | solution.py:475
  11.4 0.9 %copy-start.1 = (bf16[256,256]{1,0:T(8,128)(2,1)S(1)}, bf16[256,256]{1,0:T(8,128)(2,1)}, u32[]{:S(2)}) copy-start(bf16[256,256]{1,0:T(8,128)(2,1)} %copy-done) | copy-start | bytes 393220 | tf_op jit(solution)/shard_map/cond
  12.3 0.9 %copy-start.4 = (bf16[256,256]{1,0:T(8,128)(2,1)S(1)}, bf16[256,256]{1,0:T(8,128)(2,1)}, u32[]{:S(2)}) copy-start(bf16[256,256]{1,0:T(8,128)(2,1)} %copy-done.3) | copy-start | bytes 393220 | tf_op jit(solution)/shard_map/cond
  13.2 4.6 %copy-start.10 = (f32[8]{0:T(128)S(1)}, f32[8]{0:T(128)}, u32[]{:S(2)}) copy-start(f32[8]{0:T(128)} %get-tuple-element.47.u_ref) | copy-start | bytes 100 | tf_op jit(solution)/shard_map/cond
  13.2 4.7 %copy-start.12 = (f32[8]{0:T(128)S(1)}, f32[8]{0:T(128)}, u32[]{:S(2)}) copy-start(f32[8]{0:T(128)} %get-tuple-element.48.v_ref) | copy-start | bytes 100 | tf_op jit(solution)/shard_map/cond
  13.2 4.8 %copy-start.2 = (bf16[256,256]{1,0:T(8,128)(2,1)S(1)}, bf16[256,256]{1,0:T(8,128)(2,1)}, u32[]{:S(2)}) copy-start(bf16[256,256]{1,0:T(8,128)(2,1)} %copy-done) | copy-start | bytes 393220 | tf_op jit(solution)/shard_map/cond
  13.2 4.8 %copy-start.5 = (bf16[256,256]{1,0:T(8,128)(2,1)S(1)}, bf16[256,256]{1,0:T(8,128)(2,1)}, u32[]{:S(2)}) copy-start(bf16[256,256]{1,0:T(8,128)(2,1)} %copy-done.3) | copy-start | bytes 393220 | tf_op jit(solution)/shard_map/cond
  21.3 28.5 %collective-permute-start.4 = (f32[1384,128]{1,0:T(8,128)S(1)}, f32[1384,128]{1,0:T(8,128)S(1)}, u32[]{:S(2)}, u32[]{:S(2)}) collective-permute-start(f32[1384,128]{1,0:T(8,128)S(1)} %get-tuple-element.80), channel_id=1, source_target_pairs={{1,0},{2,1},{3,2},{4,3},{5,4},{6,5},{7,6},{8,7},{9,8},{10,9},{11,1... | collective-permute-start | bytes 2125832 | tf_op jit(solution)/shard_map/cond/branch_1_fun/ppermute | solution.py:456
  22.6 13.5 %collective-permute-start.2 = (f32[168,128]{1,0:T(8,128)S(1)}, f32[168,128]{1,0:T(8,128)S(1)}, u32[]{:S(2)}, u32[]{:S(2)}) collective-permute-start(f32[168,128]{1,0:T(8,128)S(1)} %get-tuple-element.59), channel_id=1, source_target_pairs={{0,192},{192,384},{384,576},{576,0},{1,193},{193,385},{385,577},{5... | collective-permute-start | bytes 258056 | tf_op jit(solution)/shard_map/cond/branch_1_fun/ppermute | solution.py:494
  34.0 7.6 %collective-permute-start.3 = (f32[168,128]{1,0:T(8,128)S(1)}, f32[168,128]{1,0:T(8,128)S(1)}, u32[]{:S(2)}, u32[]{:S(2)}) collective-permute-start(f32[168,128]{1,0:T(8,128)S(1)} %get-tuple-element.60), channel_id=1, source_target_pairs={{0,576},{192,0},{384,192},{576,384},{1,577},{193,1},{385,193},{577... | collective-permute-start | bytes 258056 | tf_op jit(solution)/shard_map/cond/branch_1_fun/ppermute | solution.py:495
  42.9 6.9 %collective-permute-start.5 = (f32[144,128]{1,0:T(8,128)S(1)}, f32[144,128]{1,0:T(8,128)S(1)}, u32[]{:S(2)}, u32[]{:S(2)}) collective-permute-start(f32[144,128]{1,0:T(8,128)S(1)} %get-tuple-element.81), channel_id=1, source_target_pairs={{1,0},{2,1},{3,2},{4,3},{5,4},{6,5},{7,6},{8,7},{9,8},{10,9},{11,1... | collective-permute-start | bytes 221192 | tf_op jit(solution)/shard_map/cond/branch_1_fun/ppermute | solution.py:456

commit v4 on v2

--- a/solution.py
+++ b/solution.py
@@ -33,19 +33,29 @@
     return pl.ds(start if isinstance(start, int) else pl.multiple_of(start, T), n)
 
 
-def call(body, outs, args, specs, scratch=(), cost=(0, 0), out_specs=None, aliases=None):
-    shapes = [pltpu.VMEM(s, d) if m else jax.ShapeDtypeStruct(s, d) for s, d, m in outs]
+def call(body, outs, args, specs, scratch=(), cost=(0, 0), out_specs=None, aliases=None, keep=()):
+    shapes = [
+        pltpu.VMEM(s, d) if m is True else m(s, d) if m else jax.ShapeDtypeStruct(s, d)
+        for s, d, m in outs
+    ]
+    shapes += [pltpu.VMEM(args[i].shape, args[i].dtype) for i in keep]
+    n_in, n_out = len(args), len(outs)
+    aliases = {**(aliases or {}), **{i: n_out + k for k, i in enumerate(keep)}}
+
+    def kernel(*refs):
+        body(*refs[: n_in + n_out], *refs[n_in + n_out + len(keep) :])
+
     args = [
-        a if s is SMEM else pltpu.with_memory_space_constraint(a, s.memory_space)
+        pltpu.with_memory_space_constraint(a, s.memory_space)
         for a, s in zip(args, specs)
     ]
     return pl.pallas_call(
-        body,
+        kernel,
         out_shape=shapes,
         in_specs=list(specs),
-        out_specs=out_specs or [VMEM] * len(outs),
+        out_specs=(out_specs or [VMEM] * len(outs)) + [VMEM] * len(keep),
         scratch_shapes=list(scratch),
-        input_output_aliases=aliases or {},
+        input_output_aliases=aliases,
         cost_estimate=pl.CostEstimate(flops=cost[0], bytes_accessed=cost[1], transcendentals=0),
         compiler_params=pltpu.CompilerParams(vmem_limit_bytes=8 << 20),
     )(*args)
@@ -83,19 +93,39 @@
     return jnp.where(c0, a, jnp.where(c2, c, b))
 
 
-def edges_body(drops, cloud, k_in, t_in, own, m1, ym0, ym1, yp0, yp1, kk, tt, mask, k_ref, t_ref, sem):
+def count_body(falls, u_in, v_in, out, u, v, ref, sem):
     copies = [
         pltpu.make_async_copy(a, b, sem.at[i])
-        for i, (a, b) in enumerate(((drops, own), (cloud, mask), (k_in, k_ref), (t_in, t_ref)))
+        for i, (a, b) in enumerate(((falls, ref), (u_in, u), (v_in, v)))
     ]
-    for copy in copies[1:] + copies[:1]:
+    for copy in copies:
         copy.start()
-    copies[1].wait()
+    for copy in copies:
+        copy.wait()
+    n0 = jnp.sum((ref[...] == 0).astype(jnp.int32))
+    n2 = jnp.sum((ref[...] == H_MAX).astype(jnp.int32))
+    out[0] = n0
+    out[1] = B - n2
+    out[2] = (n2 - n0 <= SPARE).astype(jnp.int32)
+
+
+def edges_body(drops, cloud, k_in, t_in, own, m1, ym0, ym1, yp0, yp1, kk, tt, mask, k_ref, t_ref, sem):
+    level = lambda z: pl.ds(z * X * Y, X * Y)
+    copies = [
+        pltpu.make_async_copy(a, b, sem.at[i])
+        for i, (a, b) in enumerate(
+            [(drops.at[level(z)], own.at[level(z)]) for z in range(Z)]
+            + [(cloud, mask), (k_in, k_ref), (t_in, t_ref)]
+        )
+    ]
+    for copy in copies[Z:] + copies[:Z]:
+        copy.start()
+    copies[Z].wait()
     columns = mask[...].astype(F32)
     for x in range(X):
         m1[(x + 1) * Y : (x + 2) * Y] = jnp.broadcast_to(columns[:, x : x + 1], (Y, B))
     for i, (ref, out, turned) in enumerate(((k_ref, kk, True), (t_ref, tt, False))):
-        copies[2 + i].wait()
+        copies[Z + 1 + i].wait()
         w = ref[...].T if turned else ref[...]
         high, low = split(w)
         half = jnp.concatenate([high, low], axis=1)
@@ -103,17 +133,16 @@
     for out, ys in ((ym0, (0, 1)), (yp0, (Y - 1, Y - 2))):
         for d, y in enumerate(ys):
             out[HALF + d * X : HALF + (d + 1) * X] = m1[pl.ds(Y + y, X, stride=Y), :]
-    copies[0].wait()
-    for outs, ys in (((ym0, ym1), (0, 1)), ((yp0, yp1), (Y - 1, Y - 2))):
-        for part, out in enumerate(outs):
+    for z in range(Z):
+        copies[z].wait()
+        for outs, ys in (((ym0, ym1), (0, 1)), ((yp0, yp1), (Y - 1, Y - 2))):
             for d, y in enumerate(ys):
-                for z in range(LOW):
-                    at = (d * LOW + z) * X
-                    start = (part * LOW + z) * X * Y + y
-                    out[at : at + X] = own[pl.ds(start, X, stride=Y), :]
+                at = (d * LOW + z % LOW) * X
+                outs[z // LOW][at : at + X] = own[pl.ds(z * X * Y + y, X, stride=Y), :]
+    for out, y in ((ym0, 0), (yp0, Y - 1)):
         for i, x in enumerate((0, X - 1)):
-            at, start = ENDS + i * LOW, (LOW * X + x) * Y + ys[0]
-            outs[0][at : at + LOW] = own[pl.ds(start, LOW, stride=X * Y), :]
+            at, start = ENDS + i * LOW, (LOW * X + x) * Y + y
+            out[at : at + LOW] = own[pl.ds(start, LOW, stride=X * Y), :]
 
 
 def sides_body(own, m1, south, north, xm, xp):
@@ -145,7 +174,7 @@
         c1[rows((z * XW + 2) * Y, X * Y)] = collide(own[rows(z * X * Y, X * Y)], mask, k, t)
         return 0
 
-    lax.fori_loop(0, Z, level, 0)
+    lax.fori_loop(0, Z, level, 0, unroll=4)
 
 
 def cy_at(side, d, x):
@@ -263,7 +292,7 @@
         settle_level(z, c0, cc2, a1, m1, c2, k, t)
         return 0
 
-    lax.fori_loop(0, 2, second, 0)
+    lax.fori_loop(0, 2, second, 0, unroll=2)
     for z in range(2):
         settle_rows(z, c0, cc2, a1y, (south, north), c2y, k, t)
 
@@ -374,7 +403,7 @@
         settle_level(z, c0, cc2, a1, m1, c2, k, t)
         return 0
 
-    lax.fori_loop(2, 6, second, 0)
+    lax.fori_loop(2, 6, second, 0, unroll=4)
     for z in range(2, 6):
         settle_rows(z, c0, cc2, a1y, (south0, north0), c2y, k, t)
 
@@ -384,16 +413,18 @@
 
     lax.fori_loop(2, 6, third, 0)
 
-    def done(z, _):
+    copies = []
+    for z in range(4):
         for i in range(X):
             at, step = (z * X + i) * T, X * T
-            res[rows(at)] = fall(c0, cc2, a2[rows(at)], a2[rows(at + step)], a2[rows(at + 2 * step)])
-        return 0
-
-    lax.fori_loop(0, 4, done, 0)
-    copy = pltpu.make_async_copy(res, out.at[pl.ds(0, 4 * X * T)], sem)
-    copy.start()
-    copy.wait()
+            res[at : at + T] = fall(
+                c0, cc2, *(a2[at + k * step : at + k * step + T] for k in range(H_MAX + 1))
+            )
+        level = pl.ds(z * X * T, X * T)
+        copies.append(pltpu.make_async_copy(res.at[level], out.at[level], sem.at[z]))
+        copies[-1].start()
+    for copy in copies:
+        copy.wait()
 
 
 def last_body(
@@ -438,23 +469,23 @@
         at = slice(z * XA * T, (z + 1) * XA * T)
         c2[at] = collide(c2[at], m1[...], k, t)
         advect_second(z, range(X), c2, a2, c2y, u_ref, v_ref)
-    for i in range(X):
-        ends = (0, 1, X - 2, X - 1)
-        tile = X - 2 + 2 * X // T + i - 2
-        p7, p6 = from_late(5 + ends.index(i)) if i in ends else from_above(tile)
-        x = [a2[(z * X + i) * T : (z * X + i + 1) * T] for z in range(4, 8)]
-        for z, v in enumerate(
-            (
-                fall(c0, cc2, x[0], x[1], x[2]),
-                fall(c0, cc2, x[1], x[2], x[3]),
-                fall(c0, cc2, x[2], x[3], p6),
-                jnp.where(c0, x[3], p7),
-            )
-        ):
-            res[(z * X + i) * T : (z * X + i + 1) * T] = v
-    copy = pltpu.make_async_copy(res, out.at[pl.ds(4 * X * T, 4 * X * T)], sem)
-    copy.start()
-    copy.wait()
+    ends = (0, 1, X - 2, X - 1)
+    copies = []
+    for z in range(4, 8):
+        for i in range(X):
+            x = [a2[(k * X + i) * T : (k * X + i + 1) * T] for k in range(z, min(z + 3, Z))]
+            if z > 5:
+                tile = X - 2 + 2 * X // T + i - 2
+                p7, p6 = from_late(5 + ends.index(i)) if i in ends else from_above(tile)
+                x = x + [p6] if z == 6 else x + [p7, p7]
+            res[((z - 4) * X + i) * T : ((z - 4) * X + i + 1) * T] = fall(c0, cc2, *x)
+        to = pl.ds(z * X * T, X * T)
+        copies.append(
+            pltpu.make_async_copy(res.at[pl.ds((z - 4) * X * T, X * T)], out.at[to], sem.at[z - 4])
+        )
+        copies[-1].start()
+    for copy in copies:
+        copy.wait()
 
 
 def ring(axis, step):
@@ -466,9 +497,8 @@
     return lax.ppermute(value, "gz", [(i, i - 1) for i in range(1, lax.axis_size("gz"))])
 
 
-def packed(n0, n2, drops, capture, transfer, courant_u, courant_v, fall_class, cloud_mask):
+def packed(scalars, drops, capture, transfer, courant_u, courant_v, fall_class, cloud_mask):
     drops = drops.reshape(Z * X * Y, B)
-    sc = jnp.stack([n0, B - n2])
     ub = jnp.broadcast_to(courant_u[:, None], (Z, B))
     vb = jnp.broadcast_to(courant_v[:, None], (Z, B))
     v = lambda n, d=F32: ((n, B), d, True)
@@ -478,23 +508,26 @@
         [v(Z * X * Y), v(XA * Y), v(ENDS + T), v(HALF), v(ENDS + T), v(HALF)] + weights,
         [drops, cloud_mask.T, capture, transfer],
         [HBM] * 4,
-        [pltpu.VMEM((Y, X), jnp.int32), pltpu.VMEM((B, B), F32), pltpu.VMEM((B, B), F32), pltpu.SemaphoreType.DMA((4,))],
+        [pltpu.VMEM((Y, X), jnp.int32), pltpu.VMEM((B, B), F32), pltpu.VMEM((B, B), F32), pltpu.SemaphoreType.DMA((Z + 3,))],
         cost=(1000, 4 << 20),
     )
     south0 = lax.ppermute(yp0, "gy", ring("gy", 1))
     north0 = lax.ppermute(ym0, "gy", ring("gy", -1))
     south1 = lax.ppermute(yp1, "gy", ring("gy", 1))
     north1 = lax.ppermute(ym1, "gy", ring("gy", -1))
-    (c1,) = call(own_body, [v(Z * XW * Y)], [own, m1, kk, tt], [VMEM] * 4, cost=(3 << 30, 8 << 20))
+    c1, kk, tt = call(
+        own_body, [v(Z * XW * Y)], [own, m1, kk, tt], [VMEM] * 4, cost=(3 << 30, 8 << 20), keep=(2, 3)
+    )
     shapes = [v(4 * XA * Z), v(Z * XA * T), v(2 * X * Z), v(Z * XA * T), v(Z * 2 * X), v(Z * X * T)]
-    scalars = [sc, courant_u, courant_v]
-    cy, a1, a1y, c2, c2y, a2, pay = call(
+    cy, a1, a1y, c2, c2y, a2, pay, kk, tt = call(
         early_body,
         shapes + [v((EARLY + EXTRA) * T)],
-        scalars + [ub, vb, c1, south0, north0, kk, tt, m1],
+        [*scalars, ub, vb, c1, south0, north0, kk, tt, m1],
         [SMEM] * 3 + [VMEM] * 8,
-        cost=(1 << 30, 4 << 20),
-    )
+        cost=(3 << 30, 8 << 20),
+        keep=(8, 9),
+    )
+    pay, south1, north1 = lax.optimization_barrier((pay, south1, north1))
     early = below(pay)
     xm, xp = call(
         sides_body,
@@ -505,32 +538,34 @@
     )
     left = lax.ppermute(xp, "gx", ring("gx", 1))
     right = lax.ppermute(xm, "gx", ring("gx", -1))
-    c1, cy, m1, a1, a1y, c2, c2y, a2, pay = call(
+    c1, cy, m1, a1, a1y, c2, c2y, a2, pay, kk, tt = call(
         late_body,
         [v(Z * XW * Y), shapes[0], v(XA * Y)] + shapes[1:] + [v(2 * LATE * T)],
-        scalars + [ub, vb, left, right, kk, tt, south0, north0, c1, cy, m1, a1, a1y, c2, c2y, a2],
+        [*scalars, ub, vb, left, right, kk, tt, south0, north0, c1, cy, m1, a1, a1y, c2, c2y, a2],
         [SMEM] * 3 + [VMEM] * 16,
         cost=(1 << 28, 1 << 20),
         aliases={11 + i: i for i in range(8)},
+        keep=(7, 8),
     )
     late = below(pay)
-    *state, out = call(
+    *state, out, kk, tt = call(
         rest_body,
         shapes + [((Z * X * Y, B), F32, False)],
-        scalars + [ub, vb, kk, tt, south0, south1, north0, north1, c1, m1, cy, a1, a1y, c2, c2y, a2],
+        [*scalars, ub, vb, kk, tt, south0, south1, north0, north1, c1, m1, cy, a1, a1y, c2, c2y, a2],
         [SMEM] * 3 + [VMEM] * 16,
-        [pltpu.VMEM((4 * X * T, B), F32), pltpu.SemaphoreType.DMA],
+        [pltpu.VMEM((4 * X * T, B), F32), pltpu.SemaphoreType.DMA((4,))],
         cost=(3 << 30, 8 << 20),
         out_specs=[VMEM] * 6 + [HBM],
         aliases={13 + i: i for i in range(6)},
+        keep=(5, 6),
     )
     (cy, a1, a1y, c2, c2y, a2) = state
     out, *_ = call(
         last_body,
         [((Z * X * Y, B), F32, False), shapes[3], shapes[4], shapes[5]],
-        scalars + [kk, tt, south0, north0, m1, a1, a1y, c2, c2y, a2, early, late, out],
+        [*scalars, kk, tt, south0, north0, m1, a1, a1y, c2, c2y, a2, early, late, out],
         [SMEM] * 3 + [VMEM] * 12 + [HBM],
-        [pltpu.VMEM((2 * X, B), F32), pltpu.VMEM((2 * X, B), F32), pltpu.VMEM((4 * X * T, B), F32), pltpu.SemaphoreType.DMA],
+        [pltpu.VMEM((2 * X, B), F32), pltpu.VMEM((2 * X, B), F32), pltpu.VMEM((4 * X * T, B), F32), pltpu.SemaphoreType.DMA((4,))],
         cost=(1 << 30, 8 << 20),
         out_specs=[HBM] + [VMEM] * 3,
         aliases={15: 0, 10: 1, 11: 2, 12: 3},
@@ -626,11 +661,16 @@
 
 
 def on_device(*args):
-    fall_class = args[5]
-    n0 = jnp.sum((fall_class == 0).astype(jnp.int32))
-    n2 = jnp.sum((fall_class == H_MAX).astype(jnp.int32))
+    scalars = call(
+        count_body,
+        [((3,), jnp.int32, pltpu.SMEM)] + [((Z,), F32, pltpu.SMEM)] * 2,
+        [args[5].reshape(1, B), args[3], args[4]],
+        [HBM] * 3,
+        [pltpu.VMEM((1, B), jnp.int32), pltpu.SemaphoreType.DMA((3,))],
+        out_specs=[SMEM] * 3,
+    )
     return lax.cond(
-        n2 - n0 <= SPARE, lambda a: packed(*a), lambda a: plain(*a[2:]), (n0, n2, *args)
+        scalars[0][2] > 0, lambda a: packed(*a), lambda a: plain(*a[1:]), (scalars, *args)
     )
 
 

time: 53.2 us -> 45 us (0.85); the launches traced: 52.1 us -> 44.8 us
  Pallas kernels: 18.8 us -> 13.3 us
  other arithmetic: 2.14 us -> 0 us
  waiting for transfers between devices: 6 us -> 7.78 us
  between operations: 1.51 us -> 0.84 us
  loops' own time: 0.99 us -> 0.32 us
    pallas_call x7 -> x8, Pallas kernels: 18.8 us -> 13.3 us  [call(): pl.pallas_call(kernel, out_shape=shapes, in_specs=list(specs), out_specs=...]
    ppermute x2, waiting for transfers between devices: 0.14 us -> 1.76 us  [below(): lax.ppermute(value, 'gz', [(i, i - 1) for i in range(1, lax.axis_size('gz...]
    reduce_sum x1 -> x0, other arithmetic: 1.37 us -> none  [on_device(): n0 = jnp.sum((fall_class == 0).astype(jnp.int32))]
    another operation x1 -> x0, other arithmetic: 0.76 us -> none  [packed(): sc = jnp.stack([n0, B - n2])]
    cond x8 -> x4, local copies, waits for them, and re-layouts: 0.73 us -> 0.01 us
    another operation x1, loops' own time: 0.99 us -> 0.32 us  [on_device(): lax.cond(scalars[0][2] > 0, lambda a: packed(*a), lambda a: plain(*a[1:])...]
    slice x0 -> x1, local copies, waits for them, and re-layouts: none -> 0.6 us  [on_device(): scalars[0][2] > 0]
  transfers between devices with their start and end apart: 8 -> 8, of which waited for: 4 -> 5; matrix products, arithmetic and copies ran while one was open for 1% -> 0% of each run, Pallas kernels for 19% -> 19%
where the time goes in v4:
time: 45 us; the launch traced here: 44.8 us
  starting transfers between devices  21.8 us (48%)
  Pallas kernels  13.3 us (30%)
  waiting for transfers between devices  7.78 us (17%)
  between operations  0.84 us (2%)
  local copies, waits for them, and re-layouts  0.74 us (2%)
    pallas_call x8, Pallas kernels, call(): pl.pallas_call(kernel, out_shape=shapes, in_specs=list(specs), out_specs=...  13.3 us
    ppermute x1, starting transfers between devices, packed(): left = lax.ppermute(xp, 'gx', ring('gx', 1))  11.4 us
    ppermute x1, waiting for transfers between devices, packed(): right = lax.ppermute(xm, 'gx', ring('gx', -1))  5.51 us
    ppermute x1, starting transfers between devices, packed(): north1 = lax.ppermute(ym1, 'gy', ring('gy', -1))  2.95 us
    ppermute x1, starting transfers between devices, packed(): north0 = lax.ppermute(ym0, 'gy', ring('gy', -1))  2.94 us
    ppermute x2, starting transfers between devices, below(): lax.ppermute(value, 'gz', [(i, i - 1) for i in range(1, lax.axis_size('gz...  2.57 us
    ppermute x1, starting transfers between devices, packed(): right = lax.ppermute(xm, 'gx', ring('gx', -1))  1.92 us
    ppermute x2, waiting for transfers between devices, below(): lax.ppermute(value, 'gz', [(i, i - 1) for i in range(1, lax.axis_size('gz...  1.76 us
  transfers between devices with their start and end apart: 8, of which 5 were waited for; matrix products, arithmetic and copies ran while one was open for 0% of the time, Pallas kernels for 19%

profile of v4, /device:TPU:6, one launch (start us, length us, event | category | flops | bytes accessed | tf_op | source)
XLA Modules:
  0.0 44.8 jit_solution(10661426862153604834)
XLA Ops:
  0.0 1.0 %shard_map.75 = (s32[3]{0:T(128)S(4)}, f32[8]{0:T(128)S(4)}, f32[8]{0:T(128)S(4)}) custom-call(s32[1,128]{1,0:T(1,128)} %bitcast.27, f32[8]{0:T(128)} %refs_1_.1, f32[8]{0:T(128)} %refs_2_.1), custom_call_target="tpu_custom_call" | custom-call | tf_op jit(solution)/shard_map/pallas_call | solution.py:52
  1.0 0.6 %slice.92 = s32[1]{0:T(128)} slice(s32[3]{0:T(128)S(4)} %get-tuple-element.104), slice={[2:3]} | slice | bytes 8 | tf_op jit(solution)/shard_map/slice | solution.py:673
  2.2 42.4 %conditional.1 = (f32[8,64,8,128]{3,2,1,0:T(8,128)}) conditional(s32[]{:T(128)} %bitcast.10, (s32[128]{0:T(128)}, f32[8,64,8,128]{3,2,1,0:T(8,128)}, s32[64,8]{0,1:T(8,128)}, f32[128,128]{1,0:T(8,128)}, f32[128,128]{1,0:T(8,128)}, /*index=5*/f32[8]{0:T(128)}, f32[8]{0:T(128)}) %tuple.12, (f32[8]{0:T(128)}, f32[8]{0:T(128)}, ...), branch_computations={%region_0.1_spmd, %region_1.2_spmd} | conditional | flops 11005855744 | bytes 92374296 | solution.py:672
  2.5 1.7 %branch_1_fun.7 = (f32[4096,128]{1,0:T(8,128)S(1)}, f32[528,128]{1,0:T(8,128)S(1)}, f32[648,128]{1,0:T(8,128)S(1)}, f32[512,128]{1,0:T(8,128)S(1)}, f32[648,128]...) custom-call(f32[4096,128]{1,0:T(8,128)} %bitcast.23, ...), custom_call_target="tpu_custom_call" | custom-call | flops 1000 | bytes 4194304 | tf_op jit(solution)/shard_map/cond/branch_1_fun/pallas_call | solution.py:52
  4.2 0.0 collective-permute-start
  4.2 2.9 %collective-permute-start.1 = (f32[648,128]{1,0:T(8,128)S(1)}, f32[648,128]{1,0:T(8,128)S(1)}, u32[]{:S(2)}, u32[]{:S(2)}) collective-permute-start(f32[648,128]{1,0:T(8,128)S(1)} %get-tuple-element.59), channel_id=1, source_target_pairs={{0,180},{12,0},{24,12},{36,24},{48,36},{60,48},{72,60},{84,72},{96... | collective-permute-start | bytes 995336 | tf_op jit(solution)/shard_map/cond/branch_1_fun/ppermute | solution.py:515
  7.2 0.0 collective-permute-start.4
  7.2 3.0 %collective-permute-start.5 = (f32[512,128]{1,0:T(8,128)S(1)}, f32[512,128]{1,0:T(8,128)S(1)}, u32[]{:S(2)}, u32[]{:S(2)}) collective-permute-start(f32[512,128]{1,0:T(8,128)S(1)} %get-tuple-element.79), channel_id=1, source_target_pairs={{0,180},{12,0},{24,12},{36,24},{48,36},{60,48},{72,60},{84,72},{96... | collective-permute-start | bytes 786440 | tf_op jit(solution)/shard_map/cond/branch_1_fun/ppermute | solution.py:517
  10.1 0.0 copy-start.4
  10.1 0.0 copy-start.6
  10.1 1.7 %branch_1_fun.9 = (f32[4352,128]{1,0:T(8,128)S(1)}, bf16[256,256]{1,0:T(8,128)(2,1)S(1)}, bf16[256,256]{1,0:T(8,128)(2,1)S(1)}) custom-call(f32[4096,128]{1,0:T(8,128)S(1)} %get-tuple-element.56.refs_0_, f32[528,128]{1,0:T(8,128)S(1)} %get-tuple-element.57.refs_1_.refs_10_.refs_13_, ...), custom_call_target="tpu_custom_call", output_to_operand_aliasing={{1}: (2, {}), {2}: (3, {})} | custom-call | flops 3221225472 | bytes 8388608 | tf_op jit(solution)/shard_map/cond/branch_1_fun/pallas_call | solution.py:52
  11.8 0.1 collective-permute-done.refs_2_.refs_6_.refs_9_.refs_7_.refs_5_
  12.0 0.0 collective-permute-done.1.refs_3_.refs_7_.refs_10_.refs_9_.refs_6_
  12.0 0.0 copy-done.4
  12.0 0.1 broadcast_in_dim.42.refs_3_
  12.0 0.0 copy-done.6
  12.0 0.1 broadcast_in_dim.43.refs_4_
  12.1 2.4 %branch_1_fun.10 = (f32[2112,128]{1,0:T(8,128)S(1)}, f32[4224,128]{1,0:T(8,128)S(1)}, f32[1024,128]{1,0:T(8,128)S(1)}, f32[4224,128]{1,0:T(8,128)S(1)}, f32[1024...) custom-call(s32[3]{0:T(128)S(4)} %get-tuple-element.47.refs_0_, ...), custom_call_target="tpu_custom_call", output_to_operand_aliasing={{7}: (8, {}), {8}: (9, {})} | custom-call | flops 3221225472 | bytes 8388608 | tf_op jit(solution)/shard_map/cond/branch_1_fun/pallas_call | solution.py:52
  14.5 0.2 collective-permute-done.4.refs_8_
  14.8 0.0 collective-permute-done.5.refs_10_
  14.8 1.3 %collective-permute-start.6 = (f32[1384,128]{1,0:T(8,128)S(1)}, f32[1384,128]{1,0:T(8,128)S(1)}, u32[]{:S(2)}, u32[]{:S(2)}) collective-permute-start(f32[1384,128]{1,0:T(8,128)S(1)} %get-tuple-element.97), channel_id=1, source_target_pairs={{1,0},{2,1},{3,2},{4,3},{5,4},{6,5},{7,6},{8,7},{9,8},{10,9},{11,1... | collective-permute-start | bytes 2125832 | tf_op jit(solution)/shard_map/cond/branch_1_fun/ppermute | solution.py:497
  16.1 11.4 %collective-permute-start.2 = (f32[168,128]{1,0:T(8,128)S(1)}, f32[168,128]{1,0:T(8,128)S(1)}, u32[]{:S(2)}, u32[]{:S(2)}) collective-permute-start(f32[168,128]{1,0:T(8,128)S(1)} %get-tuple-element.60), channel_id=1, source_target_pairs={{0,192},{192,384},{384,576},{576,0},{1,193},{193,385},{385,577},{5... | collective-permute-start | bytes 258056 | tf_op jit(solution)/shard_map/cond/branch_1_fun/ppermute | solution.py:539
  27.5 1.9 %collective-permute-start.3 = (f32[168,128]{1,0:T(8,128)S(1)}, f32[168,128]{1,0:T(8,128)S(1)}, u32[]{:S(2)}, u32[]{:S(2)}) collective-permute-start(f32[168,128]{1,0:T(8,128)S(1)} %get-tuple-element.61), channel_id=1, source_target_pairs={{0,576},{192,0},{384,192},{576,384},{1,577},{193,1},{385,193},{577... | collective-permute-start | bytes 258056 | tf_op jit(solution)/shard_map/cond/branch_1_fun/ppermute | solution.py:540
  29.4 0.1 collective-permute-done.2.refs_5_
  29.6 5.5 %collective-permute-done.3.refs_6_ = f32[168,128]{1,0:T(8,128)S(1)} collective-permute-done((f32[168,128]{1,0:T(8,128)S(1)}, f32[168,128]{1,0:T(8,128)S(1)}, u32[]{:S(2)}, u32[]{:S(2)}) %collective-permute-start.3) | collective-permute-done | bytes 86048 | tf_op jit(solution)/shard_map/cond/branch_1_fun/ppermute | solution.py:540
  35.1 0.7 %branch_1_fun.11 = (f32[4352,128]{1,0:T(8,128)S(1)}, f32[2112,128]{1,0:T(8,128)S(1)}, f32[528,128]{1,0:T(8,128)S(1)}, f32[4224,128]{1,0:T(8,128)S(1)}, f32[1024,...) custom-call(s32[3]{0:T(128)S(4)} %get-tuple-element.47.refs_0_, ...), custom_call_target="tpu_custom_call", output_to_operand_aliasing={{0}: (11, {}), {1}: (12, {}), {2}: (13, {}), {3}: (14, {}),... | custom-call | flops 268435456 | bytes 1048576 | tf_op jit(solution)/shard_map/cond/branch_1_fun/pallas_call | solution.py:52
  35.8 1.3 %collective-permute-start.7 = (f32[144,128]{1,0:T(8,128)S(1)}, f32[144,128]{1,0:T(8,128)S(1)}, u32[]{:S(2)}, u32[]{:S(2)}) collective-permute-start(f32[144,128]{1,0:T(8,128)S(1)} %get-tuple-element.98), channel_id=1, source_target_pairs={{1,0},{2,1},{3,2},{4,3},{5,4},{6,5},{7,6},{8,7},{9,8},{10,9},{11,1... | collective-permute-start | bytes 221192 | tf_op jit(solution)/shard_map/cond/branch_1_fun/ppermute | solution.py:497
  37.1 3.8 %branch_1_fun.12 = (f32[2112,128]{1,0:T(8,128)S(1)}, f32[4224,128]{1,0:T(8,128)S(1)}, f32[1024,128]{1,0:T(8,128)S(1)}, f32[4224,128]{1,0:T(8,128)S(1)}, f32[1024...) custom-call(s32[3]{0:T(128)S(4)} %get-tuple-element.47.refs_0_, ...), custom_call_target="tpu_custom_call", output_to_operand_aliasing={{0}: (13, {}), {1}: (14, {}), {2}: (15, {}), {3}: (16, {}),... | custom-call | flops 3221225472 | bytes 8388608 | tf_op jit(solution)/shard_map/cond/branch_1_fun/pallas_call | solution.py:52
  40.9 1.8 %collective-permute-done.7.refs_14_ = f32[144,128]{1,0:T(8,128)S(1)} collective-permute-done((f32[144,128]{1,0:T(8,128)S(1)}, f32[144,128]{1,0:T(8,128)S(1)}, u32[]{:S(2)}, u32[]{:S(2)}) %collective-permute-start.7) | collective-permute-done | bytes 73760 | tf_op jit(solution)/shard_map/cond/branch_1_fun/ppermute | solution.py:497
  42.7 0.0 collective-permute-done.6.refs_13_
  42.7 1.9 %branch_1_fun.13 = (f32[4096,128]{1,0:T(8,128)}, f32[4224,128]{1,0:T(8,128)S(1)}, f32[1024,128]{1,0:T(8,128)S(1)}, f32[4096,128]{1,0:T(8,128)S(1)}) custom-call(s32[3]{0:T(128)S(4)} %get-tuple-element.47.refs_0_, f32[8]{0:T(128)S(4)} %get-tuple-element.48.refs_1_, ...), custom_call_target="tpu_custom_call", output_to_operand_aliasing={{0}: (15, {}), {1}: (10, {}), {2}: (11, {}), {3}: (12, {})} | custom-call | flops 1073741824 | bytes 8388608 | tf_op jit(solution)/shard_map/cond/branch_1_fun/pallas_call | solution.py:52
  (1 shorter events, 0.0 us)
Async XLA Ops:
  4.2 7.8 %collective-permute-start = (f32[648,128]{1,0:T(8,128)S(1)}, f32[648,128]{1,0:T(8,128)S(1)}, u32[]{:S(2)}, u32[]{:S(2)}) collective-permute-start(f32[648,128]{1,0:T(8,128)S(1)} %get-tuple-element.58), channel_id=1, source_target_pairs={{0,12},{12,24},{24,36},{36,48},{48,60},{60,72},{72,84},{84,96},{96... | collective-permute-start | bytes 995336 | tf_op jit(solution)/shard_map/cond/branch_1_fun/ppermute | solution.py:514
  4.2 7.7 %collective-permute-start.1 = (f32[648,128]{1,0:T(8,128)S(1)}, f32[648,128]{1,0:T(8,128)S(1)}, u32[]{:S(2)}, u32[]{:S(2)}) collective-permute-start(f32[648,128]{1,0:T(8,128)S(1)} %get-tuple-element.59), channel_id=1, source_target_pairs={{0,180},{12,0},{24,12},{36,24},{48,36},{60,48},{72,60},{84,72},{96... | collective-permute-start | bytes 995336 | tf_op jit(solution)/shard_map/cond/branch_1_fun/ppermute | solution.py:515
  7.2 7.6 %collective-permute-start.4 = (f32[512,128]{1,0:T(8,128)S(1)}, f32[512,128]{1,0:T(8,128)S(1)}, u32[]{:S(2)}, u32[]{:S(2)}) collective-permute-start(f32[512,128]{1,0:T(8,128)S(1)} %get-tuple-element.78), channel_id=1, source_target_pairs={{0,12},{12,24},{24,36},{36,48},{48,60},{60,72},{72,84},{84,96},{96... | collective-permute-start | bytes 786440 | tf_op jit(solution)/shard_map/cond/branch_1_fun/ppermute | solution.py:516
  7.2 7.6 %collective-permute-start.5 = (f32[512,128]{1,0:T(8,128)S(1)}, f32[512,128]{1,0:T(8,128)S(1)}, u32[]{:S(2)}, u32[]{:S(2)}) collective-permute-start(f32[512,128]{1,0:T(8,128)S(1)} %get-tuple-element.79), channel_id=1, source_target_pairs={{0,180},{12,0},{24,12},{36,24},{48,36},{60,48},{72,60},{84,72},{96... | collective-permute-start | bytes 786440 | tf_op jit(solution)/shard_map/cond/branch_1_fun/ppermute | solution.py:517
  10.1 1.8 %copy-start.4 = (f32[8]{0:T(128)S(1)}, f32[8]{0:T(128)}, u32[]{:S(2)}) copy-start(f32[8]{0:T(128)} %get-tuple-element.50) | copy-start | bytes 100 | tf_op jit(solution)/shard_map/cond
  10.1 1.9 %copy-start.6 = (f32[8]{0:T(128)S(1)}, f32[8]{0:T(128)}, u32[]{:S(2)}) copy-start(f32[8]{0:T(128)} %get-tuple-element.51) | copy-start | bytes 100 | tf_op jit(solution)/shard_map/cond
  14.8 27.9 %collective-permute-start.6 = (f32[1384,128]{1,0:T(8,128)S(1)}, f32[1384,128]{1,0:T(8,128)S(1)}, u32[]{:S(2)}, u32[]{:S(2)}) collective-permute-start(f32[1384,128]{1,0:T(8,128)S(1)} %get-tuple-element.97), channel_id=1, source_target_pairs={{1,0},{2,1},{3,2},{4,3},{5,4},{6,5},{7,6},{8,7},{9,8},{10,9},{11,1... | collective-permute-start | bytes 2125832 | tf_op jit(solution)/shard_map/cond/branch_1_fun/ppermute | solution.py:497
  16.1 13.5 %collective-permute-start.2 = (f32[168,128]{1,0:T(8,128)S(1)}, f32[168,128]{1,0:T(8,128)S(1)}, u32[]{:S(2)}, u32[]{:S(2)}) collective-permute-start(f32[168,128]{1,0:T(8,128)S(1)} %get-tuple-element.60), channel_id=1, source_target_pairs={{0,192},{192,384},{384,576},{576,0},{1,193},{193,385},{385,577},{5... | collective-permute-start | bytes 258056 | tf_op jit(solution)/shard_map/cond/branch_1_fun/ppermute | solution.py:539
  27.5 7.6 %collective-permute-start.3 = (f32[168,128]{1,0:T(8,128)S(1)}, f32[168,128]{1,0:T(8,128)S(1)}, u32[]{:S(2)}, u32[]{:S(2)}) collective-permute-start(f32[168,128]{1,0:T(8,128)S(1)} %get-tuple-element.61), channel_id=1, source_target_pairs={{0,576},{192,0},{384,192},{576,384},{1,577},{193,1},{385,193},{577... | collective-permute-start | bytes 258056 | tf_op jit(solution)/shard_map/cond/branch_1_fun/ppermute | solution.py:540
  35.8 6.9 %collective-permute-start.7 = (f32[144,128]{1,0:T(8,128)S(1)}, f32[144,128]{1,0:T(8,128)S(1)}, u32[]{:S(2)}, u32[]{:S(2)}) collective-permute-start(f32[144,128]{1,0:T(8,128)S(1)} %get-tuple-element.98), channel_id=1, source_target_pairs={{1,0},{2,1},{3,2},{4,3},{5,4},{6,5},{7,6},{8,7},{9,8},{10,9},{11,1... | collective-permute-start | bytes 221192 | tf_op jit(solution)/shard_map/cond/branch_1_fun/ppermute | solution.py:497

commit v5 on v4

--- a/solution.py
+++ b/solution.py
@@ -22,6 +22,10 @@
 SPARE = B // GROUPS
 EXTRA = -(-EARLY // GROUPS)
 LATE = 4 + 1 + 4
+EDGE = (0, 1, XA - 2, XA - 1)
+ENDING = (0, 1, X - 2, X - 1)
+ROW_TILES = range(2 * X // T)
+ROW_EDGES = (0, X // T - 1, X // T, 2 * X // T - 1)
 F32, BF16 = jnp.float32, jnp.bfloat16
 
 VMEM = pl.BlockSpec(memory_space=pltpu.VMEM)
@@ -93,7 +97,7 @@
     return jnp.where(c0, a, jnp.where(c2, c, b))
 
 
-def count_body(falls, u_in, v_in, out, u, v, ref, sem):
+def count_body(falls, u_in, v_in, way, out, u, v, ref, sem):
     copies = [
         pltpu.make_async_copy(a, b, sem.at[i])
         for i, (a, b) in enumerate(((falls, ref), (u_in, u), (v_in, v)))
@@ -106,7 +110,7 @@
     n2 = jnp.sum((ref[...] == H_MAX).astype(jnp.int32))
     out[0] = n0
     out[1] = B - n2
-    out[2] = (n2 - n0 <= SPARE).astype(jnp.int32)
+    way[0] = (n2 - n0 <= SPARE).astype(jnp.int32) + (n2 <= n0).astype(jnp.int32)
 
 
 def edges_body(drops, cloud, k_in, t_in, own, m1, ym0, ym1, yp0, yp1, kk, tt, mask, k_ref, t_ref, sem):
@@ -253,14 +257,32 @@
     c2[at] = collide(c2[at], m1[...], k, t)
 
 
-def settle_rows(z, c0, cc2, a1y, masks, c2y, k, t):
-    for i in range(2 * X // T):
-        a = [a1y[pl.ds(i * T * Z + z + j, T, stride=Z), :] for j in range(H_MAX + 1)]
-        to = z * 2 * X + i * T
-        c2y[to : to + T] = fall(c0, cc2, *a)
-    at = slice(z * 2 * X, (z + 1) * 2 * X)
-    mask = jnp.concatenate([m[HALF : HALF + X] for m in masks], axis=0)
-    c2y[at] = collide(c2y[at], mask, k, t)
+def settle_rows(levels, tiles, c0, cc2, a1y, masks, c2y, k, t):
+    pieces, cloudy, where = [], [], []
+    for z in levels:
+        for i in tiles:
+            a = [a1y[pl.ds(i * T * Z + z + j, T, stride=Z), :] for j in range(H_MAX + 1)]
+            pieces.append(fall(c0, cc2, *a))
+            side, first = divmod(i * T, X)
+            cloudy.append(masks[side][HALF + first : HALF + first + T])
+            where.append(z * 2 * X + i * T)
+    c = collide(jnp.concatenate(pieces, axis=0), jnp.concatenate(cloudy, axis=0), k, t)
+    for i, to in enumerate(where):
+        c2y[to : to + T] = c[i * T : (i + 1) * T]
+
+
+def settle_edges(levels, c0, cc2, a1, m1, c2, k, t):
+    for z in levels:
+        settle(z, EDGE, c0, cc2, a1, c2)
+    tiles = [(z * XA + i) * T for z in levels for i in EDGE]
+    c = collide(
+        jnp.concatenate([c2[at : at + T] for at in tiles], axis=0),
+        jnp.concatenate([m1[i * T : (i + 1) * T] for i in EDGE] * len(levels), axis=0),
+        k,
+        t,
+    )
+    for i, at in enumerate(tiles):
+        c2[at : at + T] = c[i * T : (i + 1) * T]
 
 
 def falling(a1, a1y, a2, tile):
@@ -275,7 +297,7 @@
 
 
 def early_body(
-    sc, u_ref, v_ref, ub, vb, c1, south, north, kk, tt, m1, cy, a1, a1y, c2, c2y, a2, pay
+    extra, sc, u_ref, v_ref, ub, vb, c1, south, north, kk, tt, m1, cy, a1, a1y, c2, c2y, a2, pay
 ):
     k, t = kk[...], tt[...]
     c0, cc2 = classes(sc)
@@ -293,8 +315,7 @@
         return 0
 
     lax.fori_loop(0, 2, second, 0, unroll=2)
-    for z in range(2):
-        settle_rows(z, c0, cc2, a1y, (south, north), c2y, k, t)
+    settle_rows(range(2), ROW_TILES, c0, cc2, a1y, (south, north), c2y, k, t)
 
     def third(z, _):
         advect_second(z, range(2, X - 2), c2, a2, c2y, u_ref, v_ref)
@@ -309,7 +330,7 @@
         packed = fall(c0, cc2, pltpu.roll(l0, n2, 1), l0, level(1))
         pay[tile * T : (tile + 1) * T] = packed
     group = lax.broadcasted_iota(jnp.int32, (T, B), 1) // SPARE
-    for j in range(EXTRA):
+    for j in range(extra):
         out = jnp.zeros((T, B), F32)
         for g in range(GROUPS):
             if j + g * EXTRA < EARLY:
@@ -317,9 +338,6 @@
                 turn = (n2 - n0 + g * SPARE + B) & (B - 1)
                 out = jnp.where(group == g, pltpu.roll(l0, turn, 1), out)
         pay[(EARLY + j) * T : (EARLY + j + 1) * T] = out
-
-
-EDGE = (0, 1, XA - 2, XA - 1)
 
 
 def late_body(
@@ -351,20 +369,10 @@
     for z in range(4):
         advect_first(z, EDGE, c1, a1, cy, u_ref, v_ref)
     advect_rows((0, X - 1), ub, vb, c1, cy, a1y)
+    settle_edges(range(2), c0, cc2, a1, m1, c2, k, t)
+    settle_rows(range(2), ROW_EDGES, c0, cc2, a1y, (south, north), c2y, k, t)
     for z in range(2):
-        settle(z, EDGE, c0, cc2, a1, c2)
-    tiles = [(z * XA + i) * T for z in range(2) for i in EDGE]
-    c = collide(
-        jnp.concatenate([c2[at : at + T] for at in tiles], axis=0),
-        jnp.concatenate([m1[i * T : (i + 1) * T] for i in EDGE] * 2, axis=0),
-        k,
-        t,
-    )
-    for i, at in enumerate(tiles):
-        c2[at : at + T] = c[i * T : (i + 1) * T]
-    for z in range(2):
-        settle_rows(z, c0, cc2, a1y, (south, north), c2y, k, t)
-        advect_second(z, (0, 1, X - 2, X - 1), c2, a2, c2y, u_ref, v_ref)
+        advect_second(z, ENDING, c2, a2, c2y, u_ref, v_ref)
     for i, x in enumerate(EDGE):
         l0, l1 = (a1[(z * XA + x) * T : (z * XA + x + 1) * T] for z in range(2))
         pay[i * T : (i + 1) * T] = fall(c0, cc2, l0, l0, l1)
@@ -376,59 +384,75 @@
         pay[at + LATE * T + i : at + LATE * T + i + 1] = l0
     for first in (at + 4, at + LATE * T + 4):
         pay[first : first + 4] = jnp.zeros((4, B), F32)
-    for i, x in enumerate((0, 1, X - 2, X - 1)):
+    for i, x in enumerate(ENDING):
         l0, l1 = (a2[(z * X + x) * T : (z * X + x + 1) * T] for z in range(2))
         to = at + (i + 1) * T
         pay[to : to + T] = fall(c0, cc2, l0, l0, l1)
         pay[to + LATE * T : to + LATE * T + T] = l0
 
 
-def rest_body(
-    sc, u_ref, v_ref, ub, vb, kk, tt, south0, south1, north0, north1, c1, m1,
+def fall_out(z, columns, c0, cc2, a2, res):
+    for i in columns:
+        at, step = (z * X + i) * T, X * T
+        res[at : at + T] = fall(
+            c0, cc2, *(a2[at + k * step : at + k * step + T] for k in range(H_MAX + 1))
+        )
+
+
+def between_body(
+    sc, u_ref, v_ref, ub, vb, kk, tt, south, north, south1, north1, c1, m1,
     cy_in, a1_in, a1y_in, c2_in, c2y_in, a2_in,
-    cy, a1, a1y, c2, c2y, a2, out, res, sem,
+    cy, a1, a1y, c2, c2y, a2, res,
 ):
     k, t = kk[...], tt[...]
     c0, cc2 = classes(sc)
-    collide_rows(1, south1, north1, (south0, north0), cy, k, t)
+    collide_rows(1, south1, north1, (south, north), cy, k, t)
 
     def first(z, _):
-        advect_first(z, range(XA), c1, a1, cy, u_ref, v_ref)
+        advect_first(z, range(2, X), c1, a1, cy, u_ref, v_ref)
         return 0
 
     lax.fori_loop(4, 8, first, 0)
-    advect_rows(range(X), ub, vb, c1, cy, a1y)
+    advect_rows(range(1, X - 1), ub, vb, c1, cy, a1y)
 
     def second(z, _):
         settle_level(z, c0, cc2, a1, m1, c2, k, t)
         return 0
 
     lax.fori_loop(2, 6, second, 0, unroll=4)
+    settle_rows(range(2, 6), ROW_TILES, c0, cc2, a1y, (south, north), c2y, k, t)
+
+    def third(z, _):
+        advect_second(z, range(2, X - 2), c2, a2, c2y, u_ref, v_ref)
+        return 0
+
+    lax.fori_loop(2, 6, third, 0)
+    for z in range(4):
+        fall_out(z, range(2, X - 2), c0, cc2, a2, res)
+
+
+def rest_body(
+    sc, u_ref, v_ref, kk, tt, south, north, c1, m1, cy, a1y,
+    a1_in, c2_in, c2y_in, a2_in, res_in,
+    a1, c2, c2y, a2, res, out, sem,
+):
+    k, t = kk[...], tt[...]
+    c0, cc2 = classes(sc)
+    for z in range(4, 8):
+        advect_first(z, EDGE, c1, a1, cy, u_ref, v_ref)
+    settle_edges(range(2, 6), c0, cc2, a1, m1, c2, k, t)
+    settle_rows(range(2, 6), ROW_EDGES, c0, cc2, a1y, (south, north), c2y, k, t)
     for z in range(2, 6):
-        settle_rows(z, c0, cc2, a1y, (south0, north0), c2y, k, t)
-
-    def third(z, _):
-        advect_second(z, range(X), c2, a2, c2y, u_ref, v_ref)
-        return 0
-
-    lax.fori_loop(2, 6, third, 0)
-
-    copies = []
+        advect_second(z, ENDING, c2, a2, c2y, u_ref, v_ref)
     for z in range(4):
-        for i in range(X):
-            at, step = (z * X + i) * T, X * T
-            res[at : at + T] = fall(
-                c0, cc2, *(a2[at + k * step : at + k * step + T] for k in range(H_MAX + 1))
-            )
-        level = pl.ds(z * X * T, X * T)
-        copies.append(pltpu.make_async_copy(res.at[level], out.at[level], sem.at[z]))
-        copies[-1].start()
-    for copy in copies:
-        copy.wait()
+        fall_out(z, ENDING, c0, cc2, a2, res)
+    copy = pltpu.make_async_copy(res, out.at[pl.ds(0, 4 * X * T)], sem)
+    copy.start()
+    copy.wait()
 
 
 def last_body(
-    sc, u_ref, v_ref, kk, tt, south, north, m1, a1, a1y, c2_in, c2y_in, a2_in, early, late, out_in,
+    extra, sc, u_ref, v_ref, kk, tt, south, north, m1, a1, a1y, c2_in, c2y_in, a2_in, early, late, out_in,
     out, c2, c2y, a2, row7, row6, res, sem,
 ):
     k, t = kk[...], tt[...]
@@ -440,6 +464,8 @@
 
     def from_above(tile):
         m = early[tile * T : (tile + 1) * T]
+        if not extra:
+            return m, pltpu.roll(m, start2, 1)
         g, j = tile // EXTRA, tile % EXTRA
         spare = early[(EARLY + j) * T : (EARLY + j + 1) * T]
         return m, jnp.where(within, pltpu.roll(m, start2, 1), pltpu.roll(spare, turns[g], 1))
@@ -469,14 +495,13 @@
         at = slice(z * XA * T, (z + 1) * XA * T)
         c2[at] = collide(c2[at], m1[...], k, t)
         advect_second(z, range(X), c2, a2, c2y, u_ref, v_ref)
-    ends = (0, 1, X - 2, X - 1)
     copies = []
     for z in range(4, 8):
         for i in range(X):
             x = [a2[(k * X + i) * T : (k * X + i + 1) * T] for k in range(z, min(z + 3, Z))]
             if z > 5:
                 tile = X - 2 + 2 * X // T + i - 2
-                p7, p6 = from_late(5 + ends.index(i)) if i in ends else from_above(tile)
+                p7, p6 = from_late(5 + ENDING.index(i)) if i in ENDING else from_above(tile)
                 x = x + [p6] if z == 6 else x + [p7, p7]
             res[((z - 4) * X + i) * T : ((z - 4) * X + i + 1) * T] = fall(c0, cc2, *x)
         to = pl.ds(z * X * T, X * T)
@@ -497,7 +522,7 @@
     return lax.ppermute(value, "gz", [(i, i - 1) for i in range(1, lax.axis_size("gz"))])
 
 
-def packed(scalars, drops, capture, transfer, courant_u, courant_v, fall_class, cloud_mask):
+def packed(extra, scalars, drops, capture, transfer, courant_u, courant_v, fall_class, cloud_mask):
     drops = drops.reshape(Z * X * Y, B)
     ub = jnp.broadcast_to(courant_u[:, None], (Z, B))
     vb = jnp.broadcast_to(courant_v[:, None], (Z, B))
@@ -520,8 +545,8 @@
     )
     shapes = [v(4 * XA * Z), v(Z * XA * T), v(2 * X * Z), v(Z * XA * T), v(Z * 2 * X), v(Z * X * T)]
     cy, a1, a1y, c2, c2y, a2, pay, kk, tt = call(
-        early_body,
-        shapes + [v((EARLY + EXTRA) * T)],
+        functools.partial(early_body, extra),
+        shapes + [v((EARLY + extra) * T)],
         [*scalars, ub, vb, c1, south0, north0, kk, tt, m1],
         [SMEM] * 3 + [VMEM] * 8,
         cost=(3 << 30, 8 << 20),
@@ -538,6 +563,15 @@
     )
     left = lax.ppermute(xp, "gx", ring("gx", 1))
     right = lax.ppermute(xm, "gx", ring("gx", -1))
+    cy, a1, a1y, c2, c2y, a2, res, kk, tt = call(
+        between_body,
+        shapes + [v(4 * X * T)],
+        [*scalars, ub, vb, kk, tt, south0, north0, south1, north1, c1, m1, cy, a1, a1y, c2, c2y, a2],
+        [SMEM] * 3 + [VMEM] * 16,
+        cost=(3 << 30, 8 << 20),
+        aliases={13 + i: i for i in range(6)},
+        keep=(5, 6),
+    )
     c1, cy, m1, a1, a1y, c2, c2y, a2, pay, kk, tt = call(
         late_body,
         [v(Z * XW * Y), shapes[0], v(XA * Y)] + shapes[1:] + [v(2 * LATE * T)],
@@ -548,20 +582,19 @@
         keep=(7, 8),
     )
     late = below(pay)
-    *state, out, kk, tt = call(
+    a1, c2, c2y, a2, _, out, kk, tt = call(
         rest_body,
-        shapes + [((Z * X * Y, B), F32, False)],
-        [*scalars, ub, vb, kk, tt, south0, south1, north0, north1, c1, m1, cy, a1, a1y, c2, c2y, a2],
-        [SMEM] * 3 + [VMEM] * 16,
-        [pltpu.VMEM((4 * X * T, B), F32), pltpu.SemaphoreType.DMA((4,))],
-        cost=(3 << 30, 8 << 20),
-        out_specs=[VMEM] * 6 + [HBM],
-        aliases={13 + i: i for i in range(6)},
-        keep=(5, 6),
-    )
-    (cy, a1, a1y, c2, c2y, a2) = state
+        [shapes[1], *shapes[3:], v(4 * X * T), ((Z * X * Y, B), F32, False)],
+        [*scalars, kk, tt, south0, north0, c1, m1, cy, a1y, a1, c2, c2y, a2, res],
+        [SMEM] * 3 + [VMEM] * 13,
+        [pltpu.SemaphoreType.DMA],
+        cost=(1 << 28, 1 << 20),
+        out_specs=[VMEM] * 5 + [HBM],
+        aliases={11 + i: i for i in range(5)},
+        keep=(3, 4),
+    )
     out, *_ = call(
-        last_body,
+        functools.partial(last_body, extra),
         [((Z * X * Y, B), F32, False), shapes[3], shapes[4], shapes[5]],
         [*scalars, kk, tt, south0, north0, m1, a1, a1y, c2, c2y, a2, early, late, out],
         [SMEM] * 3 + [VMEM] * 12 + [HBM],
@@ -661,17 +694,20 @@
 
 
 def on_device(*args):
-    scalars = call(
+    way, *scalars = call(
         count_body,
-        [((3,), jnp.int32, pltpu.SMEM)] + [((Z,), F32, pltpu.SMEM)] * 2,
+        [((1,), jnp.int32, pltpu.SMEM), ((2,), jnp.int32, pltpu.SMEM)] + [((Z,), F32, pltpu.SMEM)] * 2,
         [args[5].reshape(1, B), args[3], args[4]],
         [HBM] * 3,
         [pltpu.VMEM((1, B), jnp.int32), pltpu.SemaphoreType.DMA((3,))],
-        out_specs=[SMEM] * 3,
-    )
-    return lax.cond(
-        scalars[0][2] > 0, lambda a: packed(*a), lambda a: plain(*a[1:]), (scalars, *args)
-    )
+        out_specs=[SMEM] * 4,
+    )
+    ways = (
+        lambda s, *a: plain(*a),
+        lambda s, *a: packed(EXTRA, s, *a),
+        lambda s, *a: packed(0, s, *a),
+    )
+    return lax.switch(way.reshape(()), ways, scalars, *args)
 
 
 def solution(mesh):

time: 45 us -> 44 us (0.978)
  between operations: 0.84 us -> 0.23 us
  local copies, waits for them, and re-layouts: 0.74 us -> 0.15 us
    ppermute x1, waiting for transfers between devices: 5.51 us -> 2.6 us  [packed(): right = lax.ppermute(xm, 'gx', ring('gx', -1))]
    ppermute x2, waiting for transfers between devices: 1.76 us -> 4.21 us  [below(): lax.ppermute(value, 'gz', [(i, i - 1) for i in range(1, lax.axis_size('gz...]
    slice x1 -> x0, local copies, waits for them, and re-layouts: 0.6 us -> none  [on_device(): scalars[0][2] > 0]
    pallas_call x8 -> x9, Pallas kernels: 13.3 us -> 13.3 us  [call(): pl.pallas_call(kernel, out_shape=shapes, in_specs=list(specs), out_specs=...]
  transfers between devices with their start and end apart: 8 -> 8, of which waited for: 5 -> 4; matrix products, arithmetic and copies ran while one was open for 0% -> 0% of each run, Pallas kernels for 19% -> 20%
where the time goes in v5:
time: 44 us; the launch traced here: 43.8 us
  starting transfers between devices  22.1 us (50%)
  Pallas kernels  13.3 us (30%)
  waiting for transfers between devices  7.35 us (17%)
  loops' own time  0.65 us (1%)
    pallas_call x9, Pallas kernels, call(): pl.pallas_call(kernel, out_shape=shapes, in_specs=list(specs), out_specs=...  13.3 us
    ppermute x1, starting transfers between devices, packed(): left = lax.ppermute(xp, 'gx', ring('gx', 1))  11.4 us
    ppermute x2, waiting for transfers between devices, below(): lax.ppermute(value, 'gz', [(i, i - 1) for i in range(1, lax.axis_size('gz...  4.21 us
    ppermute x1, starting transfers between devices, packed(): north1 = lax.ppermute(ym1, 'gy', ring('gy', -1))  2.95 us
    ppermute x1, starting transfers between devices, packed(): north0 = lax.ppermute(ym0, 'gy', ring('gy', -1))  2.94 us
    ppermute x1, waiting for transfers between devices, packed(): right = lax.ppermute(xm, 'gx', ring('gx', -1))  2.6 us
    ppermute x2, starting transfers between devices, below(): lax.ppermute(value, 'gz', [(i, i - 1) for i in range(1, lax.axis_size('gz...  2.57 us
    ppermute x1, starting transfers between devices, packed(): right = lax.ppermute(xm, 'gx', ring('gx', -1))  2.18 us
  transfers between devices with their start and end apart: 8, of which 4 were waited for; matrix products, arithmetic and copies ran while one was open for 0% of the time, Pallas kernels for 20%

profile of v5, /device:TPU:6, one launch (start us, length us, event | category | flops | bytes accessed | tf_op | source)
XLA Modules:
  0.0 43.8 jit_solution(15187807488432688501)
XLA Ops:
  0.0 1.0 %shard_map.76 = (s32[1]{0:T(128)S(4)}, s32[2]{0:T(128)S(4)}, f32[8]{0:T(128)S(4)}, f32[8]{0:T(128)S(4)}) custom-call(s32[1,128]{1,0:T(1,128)} %bitcast.32, f32[8]{0:T(128)} %refs_1_.1, f32[8]{0:T(128)} %refs_2_.1), custom_call_target="tpu_custom_call" | custom-call | tf_op jit(solution)/shard_map/pallas_call | solution.py:56
  1.0 42.6 %conditional.1 = (f32[8,64,8,128]{3,2,1,0:T(8,128)}) conditional(s32[]{:T(128)} %bitcast.13, (s32[128]{0:T(128)}, f32[8,64,8,128]{3,2,1,0:T(8,128)}, s32[64,8]{0,1:T(8,128)}, f32[128,128]{1,0:T(8,128)}, f32[128,128]{1,0:T(8,128)}, /*index=5*/f32[8]{0:T(128)}, f32[8]{0:T(128)}) %tuple.16, (f32[8]{0:T(128)}, f32[8]{0:T(128)}, ...), branch_computations={%region_0.1_spmd, %region_1.2_spmd, %region_2.3_spmd} | conditional | flops 11274291200 | bytes 92374296 | solution.py:710
  1.2 1.7 %branch_2_fun.8 = (f32[4096,128]{1,0:T(8,128)S(1)}, f32[528,128]{1,0:T(8,128)S(1)}, f32[648,128]{1,0:T(8,128)S(1)}, f32[512,128]{1,0:T(8,128)S(1)}, f32[648,128]...) custom-call(f32[4096,128]{1,0:T(8,128)} %bitcast.27, ...), custom_call_target="tpu_custom_call" | custom-call | flops 1000 | bytes 4194304 | tf_op jit(solution)/shard_map/cond/branch_2_fun/pallas_call | solution.py:56
  3.0 0.0 collective-permute-start.8
  3.0 2.9 %collective-permute-start.9 = (f32[648,128]{1,0:T(8,128)S(1)}, f32[648,128]{1,0:T(8,128)S(1)}, u32[]{:S(2)}, u32[]{:S(2)}) collective-permute-start(f32[648,128]{1,0:T(8,128)S(1)} %get-tuple-element.140), channel_id=1, source_target_pairs={{0,180},{12,0},{24,12},{36,24},{48,36},{60,48},{72,60},{84,72},{96... | collective-permute-start | bytes 995336 | tf_op jit(solution)/shard_map/cond/branch_2_fun/ppermute | solution.py:540
  5.9 0.0 collective-permute-start.12
  5.9 3.0 %collective-permute-start.13 = (f32[512,128]{1,0:T(8,128)S(1)}, f32[512,128]{1,0:T(8,128)S(1)}, u32[]{:S(2)}, u32[]{:S(2)}) collective-permute-start(f32[512,128]{1,0:T(8,128)S(1)} %get-tuple-element.152), channel_id=1, source_target_pairs={{0,180},{12,0},{24,12},{36,24},{48,36},{60,48},{72,60},{84,72},{96... | collective-permute-start | bytes 786440 | tf_op jit(solution)/shard_map/cond/branch_2_fun/ppermute | solution.py:542
  8.9 0.0 copy-start.5
  8.9 0.0 copy-start.8
  8.9 1.7 %branch_2_fun.10 = (f32[4352,128]{1,0:T(8,128)S(1)}, bf16[256,256]{1,0:T(8,128)(2,1)S(1)}, bf16[256,256]{1,0:T(8,128)(2,1)S(1)}) custom-call(f32[4096,128]{1,0:T(8,128)S(1)} %get-tuple-element.137.refs_0_, f32[528,128]{1,0:T(8,128)S(1)} %get-tuple-element.138.refs_1_.refs_10_.refs_12_.refs_13_, ...), custom_call_target="tpu_custom_call", output_to_operand_aliasing={{1}: (2, {}), {2}: (3, {})} | custom-call | flops 3221225472 | bytes 8388608 | tf_op jit(solution)/shard_map/cond/branch_2_fun/pallas_call | solution.py:56
  10.6 0.1 collective-permute-done.8.refs_2_.refs_6_.refs_7_.refs_9_.refs_5_
  10.7 0.0 collective-permute-done.9.refs_3_.refs_7_.refs_8_.refs_10_.refs_6_
  10.7 0.0 copy-done.5
  10.7 0.1 broadcast_in_dim.46.refs_3_
  10.8 0.0 copy-done.8
  10.8 0.1 broadcast_in_dim.47.refs_4_
  10.9 2.3 %branch_2_fun.11 = (f32[2112,128]{1,0:T(8,128)S(1)}, f32[4224,128]{1,0:T(8,128)S(1)}, f32[1024,128]{1,0:T(8,128)S(1)}, f32[4224,128]{1,0:T(8,128)S(1)}, f32[1024...) custom-call(s32[2]{0:T(128)S(4)} %get-tuple-element.128.refs_0_, ...), custom_call_target="tpu_custom_call", output_to_operand_aliasing={{7}: (8, {}), {8}: (9, {})} | custom-call | flops 3221225472 | bytes 8388608 | tf_op jit(solution)/shard_map/cond/branch_2_fun/pallas_call | solution.py:56
  13.1 0.4 collective-permute-done.12.refs_9_
  13.5 0.0 collective-permute-done.13.refs_10_
  13.5 1.3 %collective-permute-start.14 = (f32[1104,128]{1,0:T(8,128)S(1)}, f32[1104,128]{1,0:T(8,128)S(1)}, u32[]{:S(2)}, u32[]{:S(2)}) collective-permute-start(f32[1104,128]{1,0:T(8,128)S(1)} %get-tuple-element.186), channel_id=1, source_target_pairs={{1,0},{2,1},{3,2},{4,3},{5,4},{6,5},{7,6},{8,7},{9,8},{10,9},{11,1... | collective-permute-start | bytes 1695752 | tf_op jit(solution)/shard_map/cond/branch_2_fun/ppermute | solution.py:522
  14.9 11.4 %collective-permute-start.10 = (f32[168,128]{1,0:T(8,128)S(1)}, f32[168,128]{1,0:T(8,128)S(1)}, u32[]{:S(2)}, u32[]{:S(2)}) collective-permute-start(f32[168,128]{1,0:T(8,128)S(1)} %get-tuple-element.141), channel_id=1, source_target_pairs={{0,192},{192,384},{384,576},{576,0},{1,193},{193,385},{385,577},{5... | collective-permute-start | bytes 258056 | tf_op jit(solution)/shard_map/cond/branch_2_fun/ppermute | solution.py:564
  26.3 2.2 %collective-permute-start.11 = (f32[168,128]{1,0:T(8,128)S(1)}, f32[168,128]{1,0:T(8,128)S(1)}, u32[]{:S(2)}, u32[]{:S(2)}) collective-permute-start(f32[168,128]{1,0:T(8,128)S(1)} %get-tuple-element.142), channel_id=1, source_target_pairs={{0,576},{192,0},{384,192},{576,384},{1,577},{193,1},{385,193},{577... | collective-permute-start | bytes 258056 | tf_op jit(solution)/shard_map/cond/branch_2_fun/ppermute | solution.py:565
  28.4 2.8 %branch_2_fun.12 = (f32[2112,128]{1,0:T(8,128)S(1)}, f32[4224,128]{1,0:T(8,128)S(1)}, f32[1024,128]{1,0:T(8,128)S(1)}, f32[4224,128]{1,0:T(8,128)S(1)}, f32[1024...) custom-call(s32[2]{0:T(128)S(4)} %get-tuple-element.128.refs_0_, ...), custom_call_target="tpu_custom_call", output_to_operand_aliasing={{0}: (13, {}), {1}: (14, {}), {2}: (15, {}), {3}: (16, {}),... | custom-call | flops 3221225472 | bytes 8388608 | tf_op jit(solution)/shard_map/cond/branch_2_fun/pallas_call | solution.py:56
  31.2 0.0 collective-permute-done.10.refs_5_
  31.3 2.6 %collective-permute-done.11.refs_6_ = f32[168,128]{1,0:T(8,128)S(1)} collective-permute-done((f32[168,128]{1,0:T(8,128)S(1)}, f32[168,128]{1,0:T(8,128)S(1)}, u32[]{:S(2)}, u32[]{:S(2)}) %collective-permute-start.11) | collective-permute-done | bytes 86048 | tf_op jit(solution)/shard_map/cond/branch_2_fun/ppermute | solution.py:565
  33.8 0.7 %branch_2_fun.13 = (f32[4352,128]{1,0:T(8,128)S(1)}, f32[2112,128]{1,0:T(8,128)S(1)}, f32[528,128]{1,0:T(8,128)S(1)}, f32[4224,128]{1,0:T(8,128)S(1)}, f32[1024,...) custom-call(s32[2]{0:T(128)S(4)} %get-tuple-element.128.refs_0_, ...), custom_call_target="tpu_custom_call", output_to_operand_aliasing={{0}: (11, {}), {1}: (12, {}), {2}: (13, {}), {3}: (14, {}),... | custom-call | flops 268435456 | bytes 1048576 | tf_op jit(solution)/shard_map/cond/branch_2_fun/pallas_call | solution.py:56
  34.5 1.3 %collective-permute-start.15 = (f32[144,128]{1,0:T(8,128)S(1)}, f32[144,128]{1,0:T(8,128)S(1)}, u32[]{:S(2)}, u32[]{:S(2)}) collective-permute-start(f32[144,128]{1,0:T(8,128)S(1)} %get-tuple-element.187), channel_id=1, source_target_pairs={{1,0},{2,1},{3,2},{4,3},{5,4},{6,5},{7,6},{8,7},{9,8},{10,9},{11,1... | collective-permute-start | bytes 221192 | tf_op jit(solution)/shard_map/cond/branch_2_fun/ppermute | solution.py:522
  35.8 1.4 %branch_2_fun.14 = (f32[4224,128]{1,0:T(8,128)S(1)}, f32[4224,128]{1,0:T(8,128)S(1)}, f32[1024,128]{1,0:T(8,128)S(1)}, f32[4096,128]{1,0:T(8,128)S(1)}, f32[2048...) custom-call(s32[2]{0:T(128)S(4)} %get-tuple-element.128.refs_0_, ...), custom_call_target="tpu_custom_call", output_to_operand_aliasing={{0}: (11, {}), {1}: (12, {}), {2}: (13, {}), {3}: (14, {}),... | custom-call | flops 268435456 | bytes 1048576 | tf_op jit(solution)/shard_map/cond/branch_2_fun/pallas_call | solution.py:56
  37.2 4.2 %collective-permute-done.15.refs_14_ = f32[144,128]{1,0:T(8,128)S(1)} collective-permute-done((f32[144,128]{1,0:T(8,128)S(1)}, f32[144,128]{1,0:T(8,128)S(1)}, u32[]{:S(2)}, u32[]{:S(2)}) %collective-permute-start.15) | collective-permute-done | bytes 73760 | tf_op jit(solution)/shard_map/cond/branch_2_fun/ppermute | solution.py:522
  41.4 0.0 collective-permute-done.14.refs_13_
  41.4 1.8 %branch_2_fun.15 = (f32[4096,128]{1,0:T(8,128)}, f32[4224,128]{1,0:T(8,128)S(1)}, f32[1024,128]{1,0:T(8,128)S(1)}, f32[4096,128]{1,0:T(8,128)S(1)}) custom-call(s32[2]{0:T(128)S(4)} %get-tuple-element.128.refs_0_, f32[8]{0:T(128)S(4)} %get-tuple-element.129.refs_1_, ...), custom_call_target="tpu_custom_call", output_to_operand_aliasing={{0}: (15, {}), {1}: (10, {}), {2}: (11, {}), {3}: (12, {})} | custom-call | flops 1073741824 | bytes 8388608 | tf_op jit(solution)/shard_map/cond/branch_2_fun/pallas_call | solution.py:56
  (1 shorter events, 0.0 us)
Async XLA Ops:
  3.0 7.8 %collective-permute-start.8 = (f32[648,128]{1,0:T(8,128)S(1)}, f32[648,128]{1,0:T(8,128)S(1)}, u32[]{:S(2)}, u32[]{:S(2)}) collective-permute-start(f32[648,128]{1,0:T(8,128)S(1)} %get-tuple-element.139), channel_id=1, source_target_pairs={{0,12},{12,24},{24,36},{36,48},{48,60},{60,72},{72,84},{84,96},{96... | collective-permute-start | bytes 995336 | tf_op jit(solution)/shard_map/cond/branch_2_fun/ppermute | solution.py:539
  3.0 7.7 %collective-permute-start.9 = (f32[648,128]{1,0:T(8,128)S(1)}, f32[648,128]{1,0:T(8,128)S(1)}, u32[]{:S(2)}, u32[]{:S(2)}) collective-permute-start(f32[648,128]{1,0:T(8,128)S(1)} %get-tuple-element.140), channel_id=1, source_target_pairs={{0,180},{12,0},{24,12},{36,24},{48,36},{60,48},{72,60},{84,72},{96... | collective-permute-start | bytes 995336 | tf_op jit(solution)/shard_map/cond/branch_2_fun/ppermute | solution.py:540
  5.9 7.6 %collective-permute-start.12 = (f32[512,128]{1,0:T(8,128)S(1)}, f32[512,128]{1,0:T(8,128)S(1)}, u32[]{:S(2)}, u32[]{:S(2)}) collective-permute-start(f32[512,128]{1,0:T(8,128)S(1)} %get-tuple-element.151), channel_id=1, source_target_pairs={{0,12},{12,24},{24,36},{36,48},{48,60},{60,72},{72,84},{84,96},{96... | collective-permute-start | bytes 786440 | tf_op jit(solution)/shard_map/cond/branch_2_fun/ppermute | solution.py:541
  5.9 7.6 %collective-permute-start.13 = (f32[512,128]{1,0:T(8,128)S(1)}, f32[512,128]{1,0:T(8,128)S(1)}, u32[]{:S(2)}, u32[]{:S(2)}) collective-permute-start(f32[512,128]{1,0:T(8,128)S(1)} %get-tuple-element.152), channel_id=1, source_target_pairs={{0,180},{12,0},{24,12},{36,24},{48,36},{60,48},{72,60},{84,72},{96... | collective-permute-start | bytes 786440 | tf_op jit(solution)/shard_map/cond/branch_2_fun/ppermute | solution.py:542
  8.9 1.8 %copy-start.5 = (f32[8]{0:T(128)S(1)}, f32[8]{0:T(128)}, u32[]{:S(2)}) copy-start(f32[8]{0:T(128)} %get-tuple-element.131) | copy-start | bytes 100 | tf_op jit(solution)/shard_map/cond
  8.9 1.9 %copy-start.8 = (f32[8]{0:T(128)S(1)}, f32[8]{0:T(128)}, u32[]{:S(2)}) copy-start(f32[8]{0:T(128)} %get-tuple-element.132) | copy-start | bytes 100 | tf_op jit(solution)/shard_map/cond
  13.5 27.9 %collective-permute-start.14 = (f32[1104,128]{1,0:T(8,128)S(1)}, f32[1104,128]{1,0:T(8,128)S(1)}, u32[]{:S(2)}, u32[]{:S(2)}) collective-permute-start(f32[1104,128]{1,0:T(8,128)S(1)} %get-tuple-element.186), channel_id=1, source_target_pairs={{1,0},{2,1},{3,2},{4,3},{5,4},{6,5},{7,6},{8,7},{9,8},{10,9},{11,1... | collective-permute-start | bytes 1695752 | tf_op jit(solution)/shard_map/cond/branch_2_fun/ppermute | solution.py:522
  14.9 16.4 %collective-permute-start.10 = (f32[168,128]{1,0:T(8,128)S(1)}, f32[168,128]{1,0:T(8,128)S(1)}, u32[]{:S(2)}, u32[]{:S(2)}) collective-permute-start(f32[168,128]{1,0:T(8,128)S(1)} %get-tuple-element.141), channel_id=1, source_target_pairs={{0,192},{192,384},{384,576},{576,0},{1,193},{193,385},{385,577},{5... | collective-permute-start | bytes 258056 | tf_op jit(solution)/shard_map/cond/branch_2_fun/ppermute | solution.py:564
  26.3 7.6 %collective-permute-start.11 = (f32[168,128]{1,0:T(8,128)S(1)}, f32[168,128]{1,0:T(8,128)S(1)}, u32[]{:S(2)}, u32[]{:S(2)}) collective-permute-start(f32[168,128]{1,0:T(8,128)S(1)} %get-tuple-element.142), channel_id=1, source_target_pairs={{0,576},{192,0},{384,192},{576,384},{1,577},{193,1},{385,193},{577... | collective-permute-start | bytes 258056 | tf_op jit(solution)/shard_map/cond/branch_2_fun/ppermute | solution.py:565
  34.5 6.9 %collective-permute-start.15 = (f32[144,128]{1,0:T(8,128)S(1)}, f32[144,128]{1,0:T(8,128)S(1)}, u32[]{:S(2)}, u32[]{:S(2)}) collective-permute-start(f32[144,128]{1,0:T(8,128)S(1)} %get-tuple-element.187), channel_id=1, source_target_pairs={{1,0},{2,1},{3,2},{4,3},{5,4},{6,5},{7,6},{8,7},{9,8},{10,9},{11,1... | collective-permute-start | bytes 221192 | tf_op jit(solution)/shard_map/cond/branch_2_fun/ppermute | solution.py:522

commit v6 on v5

--- a/solution.py
+++ b/solution.py
@@ -341,7 +341,7 @@
 
 
 def late_body(
-    sc, u_ref, v_ref, ub, vb, left, right, kk, tt, south, north,
+    extra, sc, u_ref, v_ref, ub, vb, left, right, kk, tt, south, north,
     c1_in, cy_in, m1_in, a1_in, a1y_in, c2_in, c2y_in, a2_in,
     c1, cy, m1, a1, a1y, c2, c2y, a2, pay,
 ):
@@ -373,22 +373,23 @@
     settle_rows(range(2), ROW_EDGES, c0, cc2, a1y, (south, north), c2y, k, t)
     for z in range(2):
         advect_second(z, ENDING, c2, a2, c2y, u_ref, v_ref)
-    for i, x in enumerate(EDGE):
-        l0, l1 = (a1[(z * XA + x) * T : (z * XA + x + 1) * T] for z in range(2))
-        pay[i * T : (i + 1) * T] = fall(c0, cc2, l0, l0, l1)
-        pay[(LATE + i) * T : (LATE + i + 1) * T] = l0
-    at = 4 * T
-    for i, row in enumerate((0, X - 1, X, 2 * X - 1)):
-        l0, l1 = (a1y[row * Z + z : row * Z + z + 1] for z in range(2))
-        pay[at + i : at + i + 1] = fall(c0[0:1], cc2[0:1], l0, l0, l1)
-        pay[at + LATE * T + i : at + LATE * T + i + 1] = l0
-    for first in (at + 4, at + LATE * T + 4):
-        pay[first : first + 4] = jnp.zeros((4, B), F32)
-    for i, x in enumerate(ENDING):
-        l0, l1 = (a2[(z * X + x) * T : (z * X + x + 1) * T] for z in range(2))
-        to = at + (i + 1) * T
-        pay[to : to + T] = fall(c0, cc2, l0, l0, l1)
-        pay[to + LATE * T : to + LATE * T + T] = l0
+    tiles = [[a1[(z * XA + x) * T : (z * XA + x + 1) * T] for z in range(2)] for x in EDGE]
+    ends = (0, X - 1, X, 2 * X - 1)
+    tiles.append(
+        [
+            jnp.concatenate(
+                [a1y[row * Z + z : row * Z + z + 1] for row in ends] + [jnp.zeros((T - 4, B), F32)],
+                axis=0,
+            )
+            for z in range(2)
+        ]
+    )
+    tiles += [[a2[(z * X + x) * T : (z * X + x + 1) * T] for z in range(2)] for x in ENDING]
+    for i, (l0, l1) in enumerate(tiles):
+        own = l0 if extra else pltpu.roll(l0, B - sc[1], 1)
+        pay[i * T : (i + 1) * T] = fall(c0, cc2, own, l0, l1)
+        if extra:
+            pay[(LATE + i) * T : (LATE + i + 1) * T] = l0
 
 
 def fall_out(z, columns, c0, cc2, a2, res):
@@ -434,7 +435,7 @@
 def rest_body(
     sc, u_ref, v_ref, kk, tt, south, north, c1, m1, cy, a1y,
     a1_in, c2_in, c2y_in, a2_in, res_in,
-    a1, c2, c2y, a2, res, out, sem,
+    a1, c2, c2y, a2, res,
 ):
     k, t = kk[...], tt[...]
     c0, cc2 = classes(sc)
@@ -446,69 +447,142 @@
         advect_second(z, ENDING, c2, a2, c2y, u_ref, v_ref)
     for z in range(4):
         fall_out(z, ENDING, c0, cc2, a2, res)
-    copy = pltpu.make_async_copy(res, out.at[pl.ds(0, 4 * X * T)], sem)
-    copy.start()
-    copy.wait()
-
-
-def last_body(
-    extra, sc, u_ref, v_ref, kk, tt, south, north, m1, a1, a1y, c2_in, c2y_in, a2_in, early, late, out_in,
+
+
+def unpacking(extra, sc):
+    n0, start2 = sc[0], sc[1]
+    within = lax.broadcasted_iota(jnp.int32, (T, B), 1) < start2 + n0
+
+    def early(ref, tile):
+        m = ref[tile * T : (tile + 1) * T]
+        p6 = pltpu.roll(m, start2, 1)
+        if extra:
+            g, j = divmod(tile, EXTRA)
+            spare = ref[(EARLY + j) * T : (EARLY + j + 1) * T]
+            turn = (n0 + start2 - g * SPARE + B) & (B - 1)
+            p6 = jnp.where(within, p6, pltpu.roll(spare, turn, 1))
+        return m, p6
+
+    def late(ref, i):
+        m = ref[i * T : (i + 1) * T]
+        return m, ref[(LATE + i) * T : (LATE + i + 1) * T] if extra else pltpu.roll(m, start2, 1)
+
+    return early, late
+
+
+def settle_top(columns, above, c0, cc2, a1, c2):
+    for i in columns:
+        p7, p6 = above(i)
+        x6, x7 = (a1[(z * XA + i) * T : (z * XA + i + 1) * T] for z in (6, 7))
+        c2[(6 * XA + i) * T : (6 * XA + i + 1) * T] = fall(c0, cc2, x6, x7, p6)
+        c2[(7 * XA + i) * T : (7 * XA + i + 1) * T] = jnp.where(c0, x7, p7)
+
+
+def settle_top_rows(tiles, row7, row6, c0, cc2, a1y, c2y):
+    for i in tiles:
+        x6, x7 = (a1y[pl.ds(i * T * Z + z, T, stride=Z), :] for z in (6, 7))
+        at = 6 * 2 * X + i * T
+        c2y[at : at + T] = fall(c0, cc2, x6, x7, row6[i * T : (i + 1) * T])
+        c2y[at + 2 * X : at + 2 * X + T] = jnp.where(c0, x7, row7[i * T : (i + 1) * T])
+
+
+def fall_top(z, i, above, c0, cc2, a2):
+    x = [a2[(k * X + i) * T : (k * X + i + 1) * T] for k in range(z, min(z + 3, Z))]
+    if z > 5:
+        p7, p6 = above(i)
+        x = x + [p6] if z == 6 else x + [p7, p7]
+    return fall(c0, cc2, *x)
+
+
+def upper_body(
+    extra, sc, u_ref, v_ref, kk, tt, south, north, m1, a1, a1y, early, low, c2_in, c2y_in, a2_in,
     out, c2, c2y, a2, row7, row6, res, sem,
 ):
     k, t = kk[...], tt[...]
     c0, cc2 = classes(sc)
-    n0, start2 = sc[0], sc[1]
-    lane = lax.broadcasted_iota(jnp.int32, (T, B), 1)
-    within = lane < start2 + n0
-    turns = [(n0 + start2 - g * SPARE + B) & (B - 1) for g in range(GROUPS)]
-
-    def from_above(tile):
-        m = early[tile * T : (tile + 1) * T]
-        if not extra:
-            return m, pltpu.roll(m, start2, 1)
-        g, j = tile // EXTRA, tile % EXTRA
-        spare = early[(EARLY + j) * T : (EARLY + j + 1) * T]
-        return m, jnp.where(within, pltpu.roll(m, start2, 1), pltpu.roll(spare, turns[g], 1))
-
-    def from_late(i):
-        return late[i * T : (i + 1) * T], late[(LATE + i) * T : (LATE + i + 1) * T]
-
-    for i in range(XA):
-        p7, p6 = from_late(EDGE.index(i)) if i in EDGE else from_above(i - 2)
-        x6, x7 = (a1[(z * XA + i) * T : (z * XA + i + 1) * T] for z in (6, 7))
-        c2[(6 * XA + i) * T : (6 * XA + i + 1) * T] = fall(c0, cc2, x6, x7, p6)
-        c2[(7 * XA + i) * T : (7 * XA + i + 1) * T] = jnp.where(c0, x7, p7)
-    for i in range(2 * X // T):
-        row7[i * T : (i + 1) * T], row6[i * T : (i + 1) * T] = from_above(X - 2 + i)
-    p7, p6 = from_late(4)
-    for i, row in enumerate((0, X - 1, X, 2 * X - 1)):
-        row7[row : row + 1], row6[row : row + 1] = p7[i : i + 1], p6[i : i + 1]
-    for i in range(2 * X // T):
-        x6, x7 = (a1y[pl.ds(i * T * Z + z, T, stride=Z), :] for z in (6, 7))
-        at = 6 * 2 * X + i * T
-        c2y[at : at + T] = fall(c0, cc2, x6, x7, row6[i * T : (i + 1) * T])
-        c2y[at + 2 * X : at + 2 * X + T] = jnp.where(c0, x7, row7[i * T : (i + 1) * T])
+    copies = [pltpu.make_async_copy(low, out.at[pl.ds(0, 4 * X * T)], sem.at[4])]
+    copies[0].start()
+    unpack, _ = unpacking(extra, sc)
+    settle_top(range(2, X), lambda i: unpack(early, i - 2), c0, cc2, a1, c2)
+    for i in ROW_TILES:
+        row7[i * T : (i + 1) * T], row6[i * T : (i + 1) * T] = unpack(early, X - 2 + i)
+    settle_top_rows(ROW_TILES, row7, row6, c0, cc2, a1y, c2y)
     mask = jnp.concatenate([south[HALF : HALF + X], north[HALF : HALF + X]] * 2, axis=0)
     at = slice(12 * X, 16 * X)
     c2y[at] = collide(c2y[at], mask, k, t)
     for z in (6, 7):
-        at = slice(z * XA * T, (z + 1) * XA * T)
-        c2[at] = collide(c2[at], m1[...], k, t)
-        advect_second(z, range(X), c2, a2, c2y, u_ref, v_ref)
+        at = slice((z * XA + 2) * T, (z * XA + X) * T)
+        c2[at] = collide(c2[at], m1[2 * T : X * T], k, t)
+    columns = range(2, X - 2)
+    for z in (6, 7):
+        advect_second(z, columns, c2, a2, c2y, u_ref, v_ref)
+    above = lambda i: unpack(early, X - 2 + 2 * X // T + i - 2)
+    for z in range(4, 8):
+        for i in columns:
+            at = ((z - 4) * X + i) * T
+            res[at : at + T] = fall_top(z, i, above, c0, cc2, a2)
+        n = len(columns) * T
+        copies.append(
+            pltpu.make_async_copy(
+                res.at[pl.ds(((z - 4) * X + 2) * T, n)],
+                out.at[pl.ds((z * X + 2) * T, n)],
+                sem.at[z - 4],
+            )
+        )
+        copies[-1].start()
+    for copy in copies:
+        copy.wait()
+
+
+def last_body(
+    extra, sc, u_ref, v_ref, kk, tt, south, north, m1, a1, a1y, row7_in, row6_in, late, out_in,
+    c2_in, c2y_in, a2_in, out, c2, c2y, a2, res, sem,
+):
+    k, t = kk[...], tt[...]
+    c0, cc2 = classes(sc)
+    _, unpack = unpacking(extra, sc)
+    settle_top(EDGE, lambda i: unpack(late, EDGE.index(i)), c0, cc2, a1, c2)
+    p7, p6 = unpack(late, 4)
+    lane_row = lax.broadcasted_iota(jnp.int32, (T, B), 0)
+    fixed = {}
+    for i, tile in enumerate(ROW_EDGES):
+        row = lane_row == (T - 1 if i % 2 else 0)
+        fixed[tile] = [
+            jnp.where(row, p[i : i + 1], ref[tile * T : (tile + 1) * T])
+            for p, ref in ((p7, row7_in), (p6, row6_in))
+        ]
+    where, pieces, cloudy = [], [], []
+    for z in (6, 7):
+        for i in EDGE:
+            where.append((c2, (z * XA + i) * T))
+            pieces.append(c2[where[-1][1] : where[-1][1] + T])
+            cloudy.append(m1[i * T : (i + 1) * T])
+    for tile in ROW_EDGES:
+        x6, x7 = (a1y[pl.ds(tile * T * Z + z, T, stride=Z), :] for z in (6, 7))
+        side, first = divmod(tile * T, X)
+        mask = (south, north)[side][HALF + first : HALF + first + T]
+        for z, value in ((6, fall(c0, cc2, x6, x7, fixed[tile][1])), (7, jnp.where(c0, x7, fixed[tile][0]))):
+            where.append((c2y, z * 2 * X + tile * T))
+            pieces.append(value)
+            cloudy.append(mask)
+    c = collide(jnp.concatenate(pieces, axis=0), jnp.concatenate(cloudy, axis=0), k, t)
+    for i, (ref, to) in enumerate(where):
+        ref[to : to + T] = c[i * T : (i + 1) * T]
+    for z in (6, 7):
+        advect_second(z, ENDING, c2, a2, c2y, u_ref, v_ref)
+    above = lambda i: unpack(late, 5 + ENDING.index(i))
     copies = []
     for z in range(4, 8):
-        for i in range(X):
-            x = [a2[(k * X + i) * T : (k * X + i + 1) * T] for k in range(z, min(z + 3, Z))]
-            if z > 5:
-                tile = X - 2 + 2 * X // T + i - 2
-                p7, p6 = from_late(5 + ENDING.index(i)) if i in ENDING else from_above(tile)
-                x = x + [p6] if z == 6 else x + [p7, p7]
-            res[((z - 4) * X + i) * T : ((z - 4) * X + i + 1) * T] = fall(c0, cc2, *x)
-        to = pl.ds(z * X * T, X * T)
-        copies.append(
-            pltpu.make_async_copy(res.at[pl.ds((z - 4) * X * T, X * T)], out.at[to], sem.at[z - 4])
-        )
-        copies[-1].start()
+        for half in range(2):
+            at = ((z - 4) * 2 + half) * 2 * T
+            for j in range(2):
+                i = ENDING[half * 2 + j]
+                res[at + j * T : at + (j + 1) * T] = fall_top(z, i, above, c0, cc2, a2)
+            to = out.at[pl.ds((z * X + ENDING[half * 2]) * T, 2 * T)]
+            copies.append(
+                pltpu.make_async_copy(res.at[pl.ds(at, 2 * T)], to, sem.at[(z - 4) * 2 + half])
+            )
+            copies[-1].start()
     for copy in copies:
         copy.wait()
 
@@ -573,8 +647,8 @@
         keep=(5, 6),
     )
     c1, cy, m1, a1, a1y, c2, c2y, a2, pay, kk, tt = call(
-        late_body,
-        [v(Z * XW * Y), shapes[0], v(XA * Y)] + shapes[1:] + [v(2 * LATE * T)],
+        functools.partial(late_body, extra),
+        [v(Z * XW * Y), shapes[0], v(XA * Y)] + shapes[1:] + [v((2 if extra else 1) * LATE * T)],
         [*scalars, ub, vb, left, right, kk, tt, south0, north0, c1, cy, m1, a1, a1y, c2, c2y, a2],
         [SMEM] * 3 + [VMEM] * 16,
         cost=(1 << 28, 1 << 20),
@@ -582,26 +656,35 @@
         keep=(7, 8),
     )
     late = below(pay)
-    a1, c2, c2y, a2, _, out, kk, tt = call(
+    a1, c2, c2y, a2, res, kk, tt = call(
         rest_body,
-        [shapes[1], *shapes[3:], v(4 * X * T), ((Z * X * Y, B), F32, False)],
+        [shapes[1], *shapes[3:], v(4 * X * T)],
         [*scalars, kk, tt, south0, north0, c1, m1, cy, a1y, a1, c2, c2y, a2, res],
         [SMEM] * 3 + [VMEM] * 13,
-        [pltpu.SemaphoreType.DMA],
-        cost=(1 << 28, 1 << 20),
-        out_specs=[VMEM] * 5 + [HBM],
+        cost=(1 << 29, 1 << 20),
         aliases={11 + i: i for i in range(5)},
         keep=(3, 4),
     )
+    out, c2, c2y, a2, row7, row6, kk, tt = call(
+        functools.partial(upper_body, extra),
+        [((Z * X * Y, B), F32, False), *shapes[3:], v(2 * X), v(2 * X)],
+        [*scalars, kk, tt, south0, north0, m1, a1, a1y, early, res, c2, c2y, a2],
+        [SMEM] * 3 + [VMEM] * 12,
+        [pltpu.VMEM((4 * X * T, B), F32), pltpu.SemaphoreType.DMA((5,))],
+        cost=(3 << 30, 8 << 20),
+        out_specs=[HBM] + [VMEM] * 5,
+        aliases={12: 1, 13: 2, 14: 3},
+        keep=(3, 4),
+    )
     out, *_ = call(
         functools.partial(last_body, extra),
-        [((Z * X * Y, B), F32, False), shapes[3], shapes[4], shapes[5]],
-        [*scalars, kk, tt, south0, north0, m1, a1, a1y, c2, c2y, a2, early, late, out],
-        [SMEM] * 3 + [VMEM] * 12 + [HBM],
-        [pltpu.VMEM((2 * X, B), F32), pltpu.VMEM((2 * X, B), F32), pltpu.VMEM((4 * X * T, B), F32), pltpu.SemaphoreType.DMA((4,))],
-        cost=(1 << 30, 8 << 20),
+        [((Z * X * Y, B), F32, False), *shapes[3:]],
+        [*scalars, kk, tt, south0, north0, m1, a1, a1y, row7, row6, late, out, c2, c2y, a2],
+        [SMEM] * 3 + [VMEM] * 10 + [HBM] + [VMEM] * 3,
+        [pltpu.VMEM((4 * len(ENDING) * T, B), F32), pltpu.SemaphoreType.DMA((8,))],
+        cost=(1 << 28, 1 << 20),
         out_specs=[HBM] + [VMEM] * 3,
-        aliases={15: 0, 10: 1, 11: 2, 12: 3},
+        aliases={13: 0, 14: 1, 15: 2, 16: 3},
     )
     return out.reshape(Z, X, Y, B)
 

time: 44 us -> 42.9 us (0.975)
  waiting for transfers between devices: 7.35 us -> 6.08 us
    ppermute x2, waiting for transfers between devices: 4.21 us -> 3.03 us  [below(): lax.ppermute(value, 'gz', [(i, i - 1) for i in range(1, lax.axis_size('gz...]
    pallas_call x9 -> x10, Pallas kernels: 13.3 us -> 13.5 us  [call(): pl.pallas_call(kernel, out_shape=shapes, in_specs=list(specs), out_specs=...]
  transfers between devices with their start and end apart: 8 -> 8, of which waited for: 4 -> 4; matrix products, arithmetic and copies ran while one was open for 0% -> 0% of each run, Pallas kernels for 20% -> 23%
where the time goes in v6:
time: 42.9 us; the launch traced here: 42.7 us
  starting transfers between devices  22.1 us (52%)
  Pallas kernels  13.5 us (31%)
  waiting for transfers between devices  6.08 us (14%)
  loops' own time  0.66 us (2%)
    pallas_call x10, Pallas kernels, call(): pl.pallas_call(kernel, out_shape=shapes, in_specs=list(specs), out_specs=...  13.5 us
    ppermute x1, starting transfers between devices, packed(): left = lax.ppermute(xp, 'gx', ring('gx', 1))  11.4 us
    ppermute x2, waiting for transfers between devices, below(): lax.ppermute(value, 'gz', [(i, i - 1) for i in range(1, lax.axis_size('gz...  3.03 us
    ppermute x1, starting transfers between devices, packed(): north1 = lax.ppermute(ym1, 'gy', ring('gy', -1))  2.95 us
    ppermute x1, starting transfers between devices, packed(): north0 = lax.ppermute(ym0, 'gy', ring('gy', -1))  2.94 us
    ppermute x2, starting transfers between devices, below(): lax.ppermute(value, 'gz', [(i, i - 1) for i in range(1, lax.axis_size('gz...  2.56 us
    ppermute x1, waiting for transfers between devices, packed(): right = lax.ppermute(xm, 'gx', ring('gx', -1))  2.55 us
    ppermute x1, starting transfers between devices, packed(): right = lax.ppermute(xm, 'gx', ring('gx', -1))  2.18 us
  transfers between devices with their start and end apart: 8, of which 4 were waited for; matrix products, arithmetic and copies ran while one was open for 0% of the time, Pallas kernels for 23%

profile of v6, /device:TPU:6, one launch (start us, length us, event | category | flops | bytes accessed | tf_op | source)
XLA Modules:
  0.0 42.7 jit_solution(15156587762994209437)
XLA Ops:
  0.0 1.0 %shard_map.76 = (s32[1]{0:T(128)S(4)}, s32[2]{0:T(128)S(4)}, f32[8]{0:T(128)S(4)}, f32[8]{0:T(128)S(4)}) custom-call(s32[1,128]{1,0:T(1,128)} %bitcast.32, f32[8]{0:T(128)} %refs_1_.1, f32[8]{0:T(128)} %refs_2_.1), custom_call_target="tpu_custom_call" | custom-call | tf_op jit(solution)/shard_map/pallas_call | solution.py:56
  1.0 41.5 %conditional.1 = (f32[8,64,8,128]{3,2,1,0:T(8,128)}) conditional(s32[]{:T(128)} %bitcast.13, (s32[128]{0:T(128)}, f32[8,64,8,128]{3,2,1,0:T(8,128)}, s32[64,8]{0,1:T(8,128)}, f32[128,128]{1,0:T(8,128)}, f32[128,128]{1,0:T(8,128)}, /*index=5*/f32[8]{0:T(128)}, f32[8]{0:T(128)}) %tuple.16, (f32[8]{0:T(128)}, f32[8]{0:T(128)}, ...), branch_computations={%region_0.1_spmd, %region_1.2_spmd, %region_2.3_spmd} | conditional | flops 13958645760 | bytes 92374296 | solution.py:793
  1.2 1.7 %branch_2_fun.9 = (f32[4096,128]{1,0:T(8,128)S(1)}, f32[528,128]{1,0:T(8,128)S(1)}, f32[648,128]{1,0:T(8,128)S(1)}, f32[512,128]{1,0:T(8,128)S(1)}, f32[648,128]...) custom-call(f32[4096,128]{1,0:T(8,128)} %bitcast.27, ...), custom_call_target="tpu_custom_call" | custom-call | flops 1000 | bytes 4194304 | tf_op jit(solution)/shard_map/cond/branch_2_fun/pallas_call | solution.py:56
  3.0 0.0 collective-permute-start.8
  3.0 2.9 %collective-permute-start.9 = (f32[648,128]{1,0:T(8,128)S(1)}, f32[648,128]{1,0:T(8,128)S(1)}, u32[]{:S(2)}, u32[]{:S(2)}) collective-permute-start(f32[648,128]{1,0:T(8,128)S(1)} %get-tuple-element.148), channel_id=1, source_target_pairs={{0,180},{12,0},{24,12},{36,24},{48,36},{60,48},{72,60},{84,72},{96... | collective-permute-start | bytes 995336 | tf_op jit(solution)/shard_map/cond/branch_2_fun/ppermute | solution.py:614
  5.9 0.0 collective-permute-start.12
  5.9 3.0 %collective-permute-start.13 = (f32[512,128]{1,0:T(8,128)S(1)}, f32[512,128]{1,0:T(8,128)S(1)}, u32[]{:S(2)}, u32[]{:S(2)}) collective-permute-start(f32[512,128]{1,0:T(8,128)S(1)} %get-tuple-element.160), channel_id=1, source_target_pairs={{0,180},{12,0},{24,12},{36,24},{48,36},{60,48},{72,60},{84,72},{96... | collective-permute-start | bytes 786440 | tf_op jit(solution)/shard_map/cond/branch_2_fun/ppermute | solution.py:616
  8.9 0.0 copy-start.5
  8.9 0.0 copy-start.8
  8.9 1.7 %branch_2_fun.11 = (f32[4352,128]{1,0:T(8,128)S(1)}, bf16[256,256]{1,0:T(8,128)(2,1)S(1)}, bf16[256,256]{1,0:T(8,128)(2,1)S(1)}) custom-call(f32[4096,128]{1,0:T(8,128)S(1)} %get-tuple-element.145.refs_0_, f32[528,128]{1,0:T(8,128)S(1)} %get-tuple-element.146.refs_1_.refs_10_.refs_12_.refs_13_, ...), custom_call_target="tpu_custom_call", output_to_operand_aliasing={{1}: (2, {}), {2}: (3, {})} | custom-call | flops 3221225472 | bytes 8388608 | tf_op jit(solution)/shard_map/cond/branch_2_fun/pallas_call | solution.py:56
  10.6 0.1 collective-permute-done.8.refs_2_.refs_6_.refs_7_.refs_9_.refs_5_
  10.7 0.0 collective-permute-done.9.refs_3_.refs_7_.refs_8_.refs_10_.refs_6_
  10.7 0.0 copy-done.5
  10.7 0.1 broadcast_in_dim.46.refs_3_
  10.8 0.0 copy-done.8
  10.8 0.1 broadcast_in_dim.47.refs_4_
  10.9 2.3 %branch_2_fun.12 = (f32[2112,128]{1,0:T(8,128)S(1)}, f32[4224,128]{1,0:T(8,128)S(1)}, f32[1024,128]{1,0:T(8,128)S(1)}, f32[4224,128]{1,0:T(8,128)S(1)}, f32[1024...) custom-call(s32[2]{0:T(128)S(4)} %get-tuple-element.136.refs_0_, ...), custom_call_target="tpu_custom_call", output_to_operand_aliasing={{7}: (8, {}), {8}: (9, {})} | custom-call | flops 3221225472 | bytes 8388608 | tf_op jit(solution)/shard_map/cond/branch_2_fun/pallas_call | solution.py:56
  13.1 0.4 collective-permute-done.12.refs_9_
  13.5 0.0 collective-permute-done.13.refs_10_
  13.5 1.3 %collective-permute-start.14 = (f32[1104,128]{1,0:T(8,128)S(1)}, f32[1104,128]{1,0:T(8,128)S(1)}, u32[]{:S(2)}, u32[]{:S(2)}) collective-permute-start(f32[1104,128]{1,0:T(8,128)S(1)} %get-tuple-element.191), channel_id=1, source_target_pairs={{1,0},{2,1},{3,2},{4,3},{5,4},{6,5},{7,6},{8,7},{9,8},{10,9},{11,1... | collective-permute-start | bytes 1695752 | tf_op jit(solution)/shard_map/cond/branch_2_fun/ppermute | solution.py:596
  14.9 11.4 %collective-permute-start.10 = (f32[168,128]{1,0:T(8,128)S(1)}, f32[168,128]{1,0:T(8,128)S(1)}, u32[]{:S(2)}, u32[]{:S(2)}) collective-permute-start(f32[168,128]{1,0:T(8,128)S(1)} %get-tuple-element.149), channel_id=1, source_target_pairs={{0,192},{192,384},{384,576},{576,0},{1,193},{193,385},{385,577},{5... | collective-permute-start | bytes 258056 | tf_op jit(solution)/shard_map/cond/branch_2_fun/ppermute | solution.py:638
  26.3 2.2 %collective-permute-start.11 = (f32[168,128]{1,0:T(8,128)S(1)}, f32[168,128]{1,0:T(8,128)S(1)}, u32[]{:S(2)}, u32[]{:S(2)}) collective-permute-start(f32[168,128]{1,0:T(8,128)S(1)} %get-tuple-element.150), channel_id=1, source_target_pairs={{0,576},{192,0},{384,192},{576,384},{1,577},{193,1},{385,193},{577... | collective-permute-start | bytes 258056 | tf_op jit(solution)/shard_map/cond/branch_2_fun/ppermute | solution.py:639
  28.4 2.8 %branch_2_fun.13 = (f32[2112,128]{1,0:T(8,128)S(1)}, f32[4224,128]{1,0:T(8,128)S(1)}, f32[1024,128]{1,0:T(8,128)S(1)}, f32[4224,128]{1,0:T(8,128)S(1)}, f32[1024...) custom-call(s32[2]{0:T(128)S(4)} %get-tuple-element.136.refs_0_, ...), custom_call_target="tpu_custom_call", output_to_operand_aliasing={{0}: (13, {}), {1}: (14, {}), {2}: (15, {}), {3}: (16, {}),... | custom-call | flops 3221225472 | bytes 8388608 | tf_op jit(solution)/shard_map/cond/branch_2_fun/pallas_call | solution.py:56
  31.3 0.0 collective-permute-done.10.refs_5_
  31.3 2.5 %collective-permute-done.11.refs_6_ = f32[168,128]{1,0:T(8,128)S(1)} collective-permute-done((f32[168,128]{1,0:T(8,128)S(1)}, f32[168,128]{1,0:T(8,128)S(1)}, u32[]{:S(2)}, u32[]{:S(2)}) %collective-permute-start.11) | collective-permute-done | bytes 86048 | tf_op jit(solution)/shard_map/cond/branch_2_fun/ppermute | solution.py:639
  33.8 0.8 %branch_2_fun.14 = (f32[4352,128]{1,0:T(8,128)S(1)}, f32[2112,128]{1,0:T(8,128)S(1)}, f32[528,128]{1,0:T(8,128)S(1)}, f32[4224,128]{1,0:T(8,128)S(1)}, f32[1024,...) custom-call(s32[2]{0:T(128)S(4)} %get-tuple-element.136.refs_0_, ...), custom_call_target="tpu_custom_call", output_to_operand_aliasing={{0}: (11, {}), {1}: (12, {}), {2}: (13, {}), {3}: (14, {}),... | custom-call | flops 268435456 | bytes 1048576 | tf_op jit(solution)/shard_map/cond/branch_2_fun/pallas_call | solution.py:56
  34.6 1.3 %collective-permute-start.15 = (f32[72,128]{1,0:T(8,128)S(1)}, f32[72,128]{1,0:T(8,128)S(1)}, u32[]{:S(2)}, u32[]{:S(2)}) collective-permute-start(f32[72,128]{1,0:T(8,128)S(1)} %get-tuple-element.200), channel_id=1, source_target_pairs={{1,0},{2,1},{3,2},{4,3},{5,4},{6,5},{7,6},{8,7},{9,8},{10,9},{11,1... | collective-permute-start | bytes 110600 | tf_op jit(solution)/shard_map/cond/branch_2_fun/ppermute | solution.py:596
  35.9 0.4 branch_2_fun.15
  36.3 0.0 collective-permute-done.14.refs_10_
  36.3 1.8 %branch_2_fun.16 = (f32[4096,128]{1,0:T(8,128)}, f32[4224,128]{1,0:T(8,128)S(1)}, f32[1024,128]{1,0:T(8,128)S(1)}, f32[4096,128]{1,0:T(8,128)S(1)}, f32[128,128]...) custom-call(s32[2]{0:T(128)S(4)} %get-tuple-element.136.refs_0_, ...), custom_call_target="tpu_custom_call", output_to_operand_aliasing={{1}: (12, {}), {2}: (13, {}), {3}: (14, {}), {6}: (3, {}), ... | custom-call | flops 3221225472 | bytes 8388608 | tf_op jit(solution)/shard_map/cond/branch_2_fun/pallas_call | solution.py:56
  38.0 3.0 %collective-permute-done.15.refs_12_ = f32[72,128]{1,0:T(8,128)S(1)} collective-permute-done((f32[72,128]{1,0:T(8,128)S(1)}, f32[72,128]{1,0:T(8,128)S(1)}, u32[]{:S(2)}, u32[]{:S(2)}) %collective-permute-start.15) | collective-permute-done | bytes 36896 | tf_op jit(solution)/shard_map/cond/branch_2_fun/ppermute | solution.py:596
  41.1 1.1 %branch_2_fun.17 = (f32[4096,128]{1,0:T(8,128)}, f32[4224,128]{1,0:T(8,128)S(1)}, f32[1024,128]{1,0:T(8,128)S(1)}, f32[4096,128]{1,0:T(8,128)S(1)}) custom-call(s32[2]{0:T(128)S(4)} %get-tuple-element.136.refs_0_, f32[8]{0:T(128)S(4)} %get-tuple-element.137.refs_1_, ...), custom_call_target="tpu_custom_call", output_to_operand_aliasing={{0}: (13, {}), {1}: (14, {}), {2}: (15, {}), {3}: (16, {})} | custom-call | flops 268435456 | bytes 1048576 | tf_op jit(solution)/shard_map/cond/branch_2_fun/pallas_call | solution.py:56
  (1 shorter events, 0.0 us)
Async XLA Ops:
  3.0 7.8 %collective-permute-start.8 = (f32[648,128]{1,0:T(8,128)S(1)}, f32[648,128]{1,0:T(8,128)S(1)}, u32[]{:S(2)}, u32[]{:S(2)}) collective-permute-start(f32[648,128]{1,0:T(8,128)S(1)} %get-tuple-element.147), channel_id=1, source_target_pairs={{0,12},{12,24},{24,36},{36,48},{48,60},{60,72},{72,84},{84,96},{96... | collective-permute-start | bytes 995336 | tf_op jit(solution)/shard_map/cond/branch_2_fun/ppermute | solution.py:613
  3.0 7.7 %collective-permute-start.9 = (f32[648,128]{1,0:T(8,128)S(1)}, f32[648,128]{1,0:T(8,128)S(1)}, u32[]{:S(2)}, u32[]{:S(2)}) collective-permute-start(f32[648,128]{1,0:T(8,128)S(1)} %get-tuple-element.148), channel_id=1, source_target_pairs={{0,180},{12,0},{24,12},{36,24},{48,36},{60,48},{72,60},{84,72},{96... | collective-permute-start | bytes 995336 | tf_op jit(solution)/shard_map/cond/branch_2_fun/ppermute | solution.py:614
  5.9 7.6 %collective-permute-start.12 = (f32[512,128]{1,0:T(8,128)S(1)}, f32[512,128]{1,0:T(8,128)S(1)}, u32[]{:S(2)}, u32[]{:S(2)}) collective-permute-start(f32[512,128]{1,0:T(8,128)S(1)} %get-tuple-element.159), channel_id=1, source_target_pairs={{0,12},{12,24},{24,36},{36,48},{48,60},{60,72},{72,84},{84,96},{96... | collective-permute-start | bytes 786440 | tf_op jit(solution)/shard_map/cond/branch_2_fun/ppermute | solution.py:615
  5.9 7.6 %collective-permute-start.13 = (f32[512,128]{1,0:T(8,128)S(1)}, f32[512,128]{1,0:T(8,128)S(1)}, u32[]{:S(2)}, u32[]{:S(2)}) collective-permute-start(f32[512,128]{1,0:T(8,128)S(1)} %get-tuple-element.160), channel_id=1, source_target_pairs={{0,180},{12,0},{24,12},{36,24},{48,36},{60,48},{72,60},{84,72},{96... | collective-permute-start | bytes 786440 | tf_op jit(solution)/shard_map/cond/branch_2_fun/ppermute | solution.py:616
  8.9 1.8 %copy-start.5 = (f32[8]{0:T(128)S(1)}, f32[8]{0:T(128)}, u32[]{:S(2)}) copy-start(f32[8]{0:T(128)} %get-tuple-element.139) | copy-start | bytes 100 | tf_op jit(solution)/shard_map/cond
  8.9 1.9 %copy-start.8 = (f32[8]{0:T(128)S(1)}, f32[8]{0:T(128)}, u32[]{:S(2)}) copy-start(f32[8]{0:T(128)} %get-tuple-element.140) | copy-start | bytes 100 | tf_op jit(solution)/shard_map/cond
  13.5 22.7 %collective-permute-start.14 = (f32[1104,128]{1,0:T(8,128)S(1)}, f32[1104,128]{1,0:T(8,128)S(1)}, u32[]{:S(2)}, u32[]{:S(2)}) collective-permute-start(f32[1104,128]{1,0:T(8,128)S(1)} %get-tuple-element.191), channel_id=1, source_target_pairs={{1,0},{2,1},{3,2},{4,3},{5,4},{6,5},{7,6},{8,7},{9,8},{10,9},{11,1... | collective-permute-start | bytes 1695752 | tf_op jit(solution)/shard_map/cond/branch_2_fun/ppermute | solution.py:596
  14.9 16.4 %collective-permute-start.10 = (f32[168,128]{1,0:T(8,128)S(1)}, f32[168,128]{1,0:T(8,128)S(1)}, u32[]{:S(2)}, u32[]{:S(2)}) collective-permute-start(f32[168,128]{1,0:T(8,128)S(1)} %get-tuple-element.149), channel_id=1, source_target_pairs={{0,192},{192,384},{384,576},{576,0},{1,193},{193,385},{385,577},{5... | collective-permute-start | bytes 258056 | tf_op jit(solution)/shard_map/cond/branch_2_fun/ppermute | solution.py:638
  26.3 7.6 %collective-permute-start.11 = (f32[168,128]{1,0:T(8,128)S(1)}, f32[168,128]{1,0:T(8,128)S(1)}, u32[]{:S(2)}, u32[]{:S(2)}) collective-permute-start(f32[168,128]{1,0:T(8,128)S(1)} %get-tuple-element.150), channel_id=1, source_target_pairs={{0,576},{192,0},{384,192},{576,384},{1,577},{193,1},{385,193},{577... | collective-permute-start | bytes 258056 | tf_op jit(solution)/shard_map/cond/branch_2_fun/ppermute | solution.py:639
  34.6 6.5 %collective-permute-start.15 = (f32[72,128]{1,0:T(8,128)S(1)}, f32[72,128]{1,0:T(8,128)S(1)}, u32[]{:S(2)}, u32[]{:S(2)}) collective-permute-start(f32[72,128]{1,0:T(8,128)S(1)} %get-tuple-element.200), channel_id=1, source_target_pairs={{1,0},{2,1},{3,2},{4,3},{5,4},{6,5},{7,6},{8,7},{9,8},{10,9},{11,1... | collective-permute-start | bytes 110600 | tf_op jit(solution)/shard_map/cond/branch_2_fun/ppermute | solution.py:596

commit v7 on v6

--- a/solution.py
+++ b/solution.py
@@ -8,7 +8,6 @@
 from jax.sharding import PartitionSpec as P
 
 H_MAX = 2
-STEPS = 2
 Z, X, Y, B = 8, 64, 8, 128
 T = 8
 XW = X + 4
@@ -18,9 +17,7 @@
 ENDS = HALF + 2 * X
 XROWS = 2 * Z * Y
 EARLY = (X - 2) + 2 * X // T + (X - 4)
-GROUPS = 4
-SPARE = B // GROUPS
-EXTRA = -(-EARLY // GROUPS)
+SPARES = (0, 8, 24, B)
 LATE = 4 + 1 + 4
 EDGE = (0, 1, XA - 2, XA - 1)
 ENDING = (0, 1, X - 2, X - 1)
@@ -110,7 +107,7 @@
     n2 = jnp.sum((ref[...] == H_MAX).astype(jnp.int32))
     out[0] = n0
     out[1] = B - n2
-    way[0] = (n2 - n0 <= SPARE).astype(jnp.int32) + (n2 <= n0).astype(jnp.int32)
+    way[0] = sum((n2 - n0 > spare).astype(jnp.int32) for spare in SPARES[:-1])
 
 
 def edges_body(drops, cloud, k_in, t_in, own, m1, ym0, ym1, yp0, yp1, kk, tt, mask, k_ref, t_ref, sem):
@@ -149,23 +146,25 @@
             out[at : at + LOW] = own[pl.ds(start, LOW, stride=X * Y), :]
 
 
-def sides_body(own, m1, south, north, xm, xp):
-    for out, cols in ((xm, (0, 1)), (xp, (X - 1, X - 2))):
-        for d, x in enumerate(cols):
-            out[XROWS + d * Y : XROWS + (d + 1) * Y] = m1[(x + 1) * Y : (x + 2) * Y]
+def sides_body(own, m1, south, north, first, second):
+    even = lax.axis_index("gx") % 2 == 0
+    for out, to_right in ((first, even), (second, jnp.logical_not(even))):
+        edge = jnp.where(to_right, X - 1, 0)
+        inward = jnp.where(to_right, -1, 1)
+        for d in range(2):
+            x = edge + d * inward
+            out[XROWS + d * Y : XROWS + (d + 1) * Y] = m1[rows((x + 1) * Y)]
             for z in range(Z):
-                at = (z * X + x) * Y
-                out[(d * Z + z) * Y : (d * Z + z + 1) * Y] = own[at : at + Y]
-        x = cols[0]
+                out[(d * Z + z) * Y : (d * Z + z + 1) * Y] = own[rows((z * X + x) * Y)]
         at = XROWS + 2 * Y
         out[at + 2 * Z :] = jnp.zeros((T, B), F32)
         for side, ref in enumerate((south, north)):
             row = at + side * Z
-            end = ENDS + (LOW if x else 0)
-            out[row : row + LOW] = ref[pl.ds(x, LOW, stride=X), :]
-            out[row + LOW : row + Z] = ref[end : end + LOW]
+            end = ENDS + jnp.where(to_right, LOW, 0)
+            out[row : row + LOW] = ref[pl.ds(edge, LOW, stride=X), :]
+            out[row + LOW : row + Z] = ref[pl.ds(end, LOW), :]
             row = at + 2 * Z + side
-            out[row : row + 1] = ref[HALF + x : HALF + x + 1]
+            out[row : row + 1] = ref[pl.ds(HALF + edge, 1), :]
 
 
 XMESSAGE = XROWS + 2 * Y + 2 * Z + T
@@ -297,7 +296,7 @@
 
 
 def early_body(
-    extra, sc, u_ref, v_ref, ub, vb, c1, south, north, kk, tt, m1, cy, a1, a1y, c2, c2y, a2, pay
+    spare, sc, u_ref, v_ref, ub, vb, c1, south, north, kk, tt, m1, cy, a1, a1y, c2, c2y, a2, pay
 ):
     k, t = kk[...], tt[...]
     c0, cc2 = classes(sc)
@@ -329,24 +328,30 @@
         l0 = level(0)
         packed = fall(c0, cc2, pltpu.roll(l0, n2, 1), l0, level(1))
         pay[tile * T : (tile + 1) * T] = packed
-    group = lax.broadcasted_iota(jnp.int32, (T, B), 1) // SPARE
-    for j in range(extra):
+    tiles = spare_tiles(spare)
+    lane = lax.broadcasted_iota(jnp.int32, (T, B), 1)
+    for j in range(tiles):
         out = jnp.zeros((T, B), F32)
-        for g in range(GROUPS):
-            if j + g * EXTRA < EARLY:
-                l0 = falling(a1, a1y, a2, j + g * EXTRA)(0)
-                turn = (n2 - n0 + g * SPARE + B) & (B - 1)
-                out = jnp.where(group == g, pltpu.roll(l0, turn, 1), out)
+        for g in range(B // spare):
+            if j + g * tiles < EARLY:
+                l0 = falling(a1, a1y, a2, j + g * tiles)(0)
+                turn = (n2 - n0 + g * spare + B) & (B - 1)
+                here = (lane >= g * spare) & (lane < (g + 1) * spare)
+                out = jnp.where(here, pltpu.roll(l0, turn, 1), out)
         pay[(EARLY + j) * T : (EARLY + j + 1) * T] = out
 
 
 def late_body(
-    extra, sc, u_ref, v_ref, ub, vb, left, right, kk, tt, south, north,
+    spare, sc, u_ref, v_ref, ub, vb, first, second, kk, tt, south, north,
     c1_in, cy_in, m1_in, a1_in, a1y_in, c2_in, c2y_in, a2_in,
-    c1, cy, m1, a1, a1y, c2, c2y, a2, pay,
+    c1, cy, m1, a1, a1y, c2, c2y, a2, pay, sides,
 ):
     k, t = kk[...], tt[...]
     c0, cc2 = classes(sc)
+    even = lax.axis_index("gx") % 2 == 0
+    for to, a, b in ((sides.at[0], second, first), (sides.at[1], first, second)):
+        to[...] = jnp.where(even, a[...], b[...])
+    left, right = sides.at[0], sides.at[1]
     m1[0:Y] = left[XROWS : XROWS + Y]
     m1[Y + X * Y :] = right[XROWS : XROWS + Y]
     at_mask = XROWS + 2 * Y
@@ -386,9 +391,9 @@
     )
     tiles += [[a2[(z * X + x) * T : (z * X + x + 1) * T] for z in range(2)] for x in ENDING]
     for i, (l0, l1) in enumerate(tiles):
-        own = l0 if extra else pltpu.roll(l0, B - sc[1], 1)
+        own = l0 if spare else pltpu.roll(l0, B - sc[1], 1)
         pay[i * T : (i + 1) * T] = fall(c0, cc2, own, l0, l1)
-        if extra:
+        if spare:
             pay[(LATE + i) * T : (LATE + i + 1) * T] = l0
 
 
@@ -449,23 +454,27 @@
         fall_out(z, ENDING, c0, cc2, a2, res)
 
 
-def unpacking(extra, sc):
+def spare_tiles(spare):
+    return -(-EARLY // (B // spare)) if spare else 0
+
+
+def unpacking(spare, sc):
     n0, start2 = sc[0], sc[1]
     within = lax.broadcasted_iota(jnp.int32, (T, B), 1) < start2 + n0
 
     def early(ref, tile):
         m = ref[tile * T : (tile + 1) * T]
         p6 = pltpu.roll(m, start2, 1)
-        if extra:
-            g, j = divmod(tile, EXTRA)
-            spare = ref[(EARLY + j) * T : (EARLY + j + 1) * T]
-            turn = (n0 + start2 - g * SPARE + B) & (B - 1)
-            p6 = jnp.where(within, p6, pltpu.roll(spare, turn, 1))
+        if spare:
+            g, j = divmod(tile, spare_tiles(spare))
+            more = ref[(EARLY + j) * T : (EARLY + j + 1) * T]
+            turn = (n0 + start2 - g * spare + B) & (B - 1)
+            p6 = jnp.where(within, p6, pltpu.roll(more, turn, 1))
         return m, p6
 
     def late(ref, i):
         m = ref[i * T : (i + 1) * T]
-        return m, ref[(LATE + i) * T : (LATE + i + 1) * T] if extra else pltpu.roll(m, start2, 1)
+        return m, ref[(LATE + i) * T : (LATE + i + 1) * T] if spare else pltpu.roll(m, start2, 1)
 
     return early, late
 
@@ -495,14 +504,14 @@
 
 
 def upper_body(
-    extra, sc, u_ref, v_ref, kk, tt, south, north, m1, a1, a1y, early, low, c2_in, c2y_in, a2_in,
+    spare, sc, u_ref, v_ref, kk, tt, south, north, m1, a1, a1y, early, low, c2_in, c2y_in, a2_in,
     out, c2, c2y, a2, row7, row6, res, sem,
 ):
     k, t = kk[...], tt[...]
     c0, cc2 = classes(sc)
     copies = [pltpu.make_async_copy(low, out.at[pl.ds(0, 4 * X * T)], sem.at[4])]
     copies[0].start()
-    unpack, _ = unpacking(extra, sc)
+    unpack, _ = unpacking(spare, sc)
     settle_top(range(2, X), lambda i: unpack(early, i - 2), c0, cc2, a1, c2)
     for i in ROW_TILES:
         row7[i * T : (i + 1) * T], row6[i * T : (i + 1) * T] = unpack(early, X - 2 + i)
@@ -535,12 +544,12 @@
 
 
 def last_body(
-    extra, sc, u_ref, v_ref, kk, tt, south, north, m1, a1, a1y, row7_in, row6_in, late, out_in,
+    spare, sc, u_ref, v_ref, kk, tt, south, north, m1, a1, a1y, row7_in, row6_in, late, out_in,
     c2_in, c2y_in, a2_in, out, c2, c2y, a2, res, sem,
 ):
     k, t = kk[...], tt[...]
     c0, cc2 = classes(sc)
-    _, unpack = unpacking(extra, sc)
+    _, unpack = unpacking(spare, sc)
     settle_top(EDGE, lambda i: unpack(late, EDGE.index(i)), c0, cc2, a1, c2)
     p7, p6 = unpack(late, 4)
     lane_row = lax.broadcasted_iota(jnp.int32, (T, B), 0)
@@ -592,11 +601,17 @@
     return [(i, (i + step) % n) for i in range(n)]
 
 
+def swaps(axis, start):
+    n = lax.axis_size(axis)
+    pairs = [(i % n, (i + 1) % n) for i in range(start, n + start, 2)]
+    return sorted({(a, b) for i, j in pairs for a, b in ((i, j), (j, i))})
+
+
 def below(value):
     return lax.ppermute(value, "gz", [(i, i - 1) for i in range(1, lax.axis_size("gz"))])
 
 
-def packed(extra, scalars, drops, capture, transfer, courant_u, courant_v, fall_class, cloud_mask):
+def packed(spare, scalars, drops, capture, transfer, courant_u, courant_v, fall_class, cloud_mask):
     drops = drops.reshape(Z * X * Y, B)
     ub = jnp.broadcast_to(courant_u[:, None], (Z, B))
     vb = jnp.broadcast_to(courant_v[:, None], (Z, B))
@@ -619,8 +634,8 @@
     )
     shapes = [v(4 * XA * Z), v(Z * XA * T), v(2 * X * Z), v(Z * XA * T), v(Z * 2 * X), v(Z * X * T)]
     cy, a1, a1y, c2, c2y, a2, pay, kk, tt = call(
-        functools.partial(early_body, extra),
-        shapes + [v((EARLY + extra) * T)],
+        functools.partial(early_body, spare),
+        shapes + [v((EARLY + spare_tiles(spare)) * T)],
         [*scalars, ub, vb, c1, south0, north0, kk, tt, m1],
         [SMEM] * 3 + [VMEM] * 8,
         cost=(3 << 30, 8 << 20),
@@ -628,15 +643,15 @@
     )
     pay, south1, north1 = lax.optimization_barrier((pay, south1, north1))
     early = below(pay)
-    xm, xp = call(
+    first, second = call(
         sides_body,
         [v(XMESSAGE)] * 2,
         [own, m1, south0, north0],
         [VMEM] * 4,
         cost=(1000, 1 << 18),
     )
-    left = lax.ppermute(xp, "gx", ring("gx", 1))
-    right = lax.ppermute(xm, "gx", ring("gx", -1))
+    first = lax.ppermute(first, "gx", swaps("gx", 0))
+    second = lax.ppermute(second, "gx", swaps("gx", 1))
     cy, a1, a1y, c2, c2y, a2, res, kk, tt = call(
         between_body,
         shapes + [v(4 * X * T)],
@@ -647,10 +662,11 @@
         keep=(5, 6),
     )
     c1, cy, m1, a1, a1y, c2, c2y, a2, pay, kk, tt = call(
-        functools.partial(late_body, extra),
-        [v(Z * XW * Y), shapes[0], v(XA * Y)] + shapes[1:] + [v((2 if extra else 1) * LATE * T)],
-        [*scalars, ub, vb, left, right, kk, tt, south0, north0, c1, cy, m1, a1, a1y, c2, c2y, a2],
+        functools.partial(late_body, spare),
+        [v(Z * XW * Y), shapes[0], v(XA * Y)] + shapes[1:] + [v((2 if spare else 1) * LATE * T)],
+        [*scalars, ub, vb, first, second, kk, tt, south0, north0, c1, cy, m1, a1, a1y, c2, c2y, a2],
         [SMEM] * 3 + [VMEM] * 16,
+        [pltpu.VMEM((2, XMESSAGE, B), F32)],
         cost=(1 << 28, 1 << 20),
         aliases={11 + i: i for i in range(8)},
         keep=(7, 8),
@@ -666,7 +682,7 @@
         keep=(3, 4),
     )
     out, c2, c2y, a2, row7, row6, kk, tt = call(
-        functools.partial(upper_body, extra),
+        functools.partial(upper_body, spare),
         [((Z * X * Y, B), F32, False), *shapes[3:], v(2 * X), v(2 * X)],
         [*scalars, kk, tt, south0, north0, m1, a1, a1y, early, res, c2, c2y, a2],
         [SMEM] * 3 + [VMEM] * 12,
@@ -677,7 +693,7 @@
         keep=(3, 4),
     )
     out, *_ = call(
-        functools.partial(last_body, extra),
+        functools.partial(last_body, spare),
         [((Z * X * Y, B), F32, False), *shapes[3:]],
         [*scalars, kk, tt, south0, north0, m1, a1, a1y, row7, row6, late, out, c2, c2y, a2],
         [SMEM] * 3 + [VMEM] * 10 + [HBM] + [VMEM] * 3,
@@ -687,93 +703,6 @@
         aliases={13: 0, 14: 1, 15: 2, 16: 3},
     )
     return out.reshape(Z, X, Y, B)
-
-
-def passed_along(block, axis, distance):
-    devices = range(lax.axis_size(axis))
-    route = [(i - distance, i) for i in devices if i - distance in devices]
-    return lax.ppermute(block, axis, route)
-
-
-def with_halo(value, sides, width):
-    edges = {}
-    for axis, dim in sides:
-        devices, length = (lax.axis_size(axis), value.shape[dim])
-        up = [(i, (i + 1) % devices) for i in range(devices)]
-        last = lax.slice_in_dim(value, length - width, length, axis=dim)
-        leading = lax.slice_in_dim(value, 0, width, axis=dim)
-        edges[dim] = (
-            lax.ppermute(last, axis, up),
-            lax.ppermute(leading, axis, [(b, a) for a, b in up]),
-        )
-    done = []
-    for _, dim in sides:
-        low, high = edges[dim]
-        around = [(width, width) if d in done else (0, 0) for d in range(value.ndim)]
-        value = jnp.concatenate([jnp.pad(low, around), value, jnp.pad(high, around)], axis=dim)
-        done.append(dim)
-    return value
-
-
-def collide_plain(particle_distribution, capture_efficiency_matrix, transfer, cloudy):
-    merger_speed = jnp.einsum(
-        "ugcr,mr->ugcm",
-        particle_distribution,
-        capture_efficiency_matrix,
-        precision=lax.Precision.HIGHEST,
-    )
-    water_removed = particle_distribution * merger_speed
-    mass_gain = jnp.einsum(
-        "zxyi,ik->zxyk", water_removed, transfer, precision=lax.Precision.HIGHEST
-    )
-    return particle_distribution + cloudy[None, :, :, None] * (mass_gain - water_removed)
-
-
-def advect_plain(with_edges, courant_u, courant_v):
-    centre = with_edges[:, 1:-1, 1:-1]
-    west_side = with_edges[:, :-2, 1:-1]
-    east_side = with_edges[:, 2:, 1:-1]
-    south_side = with_edges[:, 1:-1, :-2]
-    north_side = with_edges[:, 1:-1, 2:]
-    x_plus = jnp.maximum(courant_u, 0.0)[:, None, None, None]
-    x_minus = jnp.minimum(courant_u, 0.0)[:, None, None, None]
-    northward_neighbor = jnp.maximum(courant_v, 0.0)[:, None, None, None]
-    y_minus = jnp.minimum(courant_v, 0.0)[:, None, None, None]
-    result = centre - x_plus * (centre - west_side) - x_minus * (east_side - centre)
-    return result - northward_neighbor * (centre - south_side) - y_minus * (north_side - centre)
-
-
-def sediment(padded, fall_class, levels):
-    result = padded[:levels]
-    for fall_depth in range(1, H_MAX + 1):
-        result = jnp.where(
-            (fall_class == fall_depth)[None, None, None, :],
-            padded[fall_depth : fall_depth + levels],
-            result,
-        )
-    return result
-
-
-def plain(
-    drops, capture_efficiency_matrix, transfer, courant_u, courant_v, fall_class, cloud_mask
-):
-    cloudy = cloud_mask.astype(jnp.float32)
-    reach = STEPS * H_MAX
-    from_above, upper_u, upper_v = passed_along(
-        (drops[:reach], courant_u[:reach], courant_v[:reach]), "gz", -1
-    )
-    particle_distribution = jnp.concatenate([drops, from_above], axis=0)
-    column_u = jnp.concatenate([courant_u, upper_u], axis=0)
-    column_v = jnp.concatenate([courant_v, upper_v], axis=0)
-    for repeat in range(STEPS):
-        current = particle_distribution.shape[0]
-        coalesced_drops = collide_plain(
-            particle_distribution, capture_efficiency_matrix, transfer, cloudy
-        )
-        with_edges = with_halo(coalesced_drops, (("gx", 1), ("gy", 2)), 1)
-        advected = advect_plain(with_edges, column_u[:current], column_v[:current])
-        particle_distribution = sediment(advected, fall_class, current - H_MAX)
-    return particle_distribution
 
 
 def on_device(*args):
@@ -785,11 +714,7 @@
         [pltpu.VMEM((1, B), jnp.int32), pltpu.SemaphoreType.DMA((3,))],
         out_specs=[SMEM] * 4,
     )
-    ways = (
-        lambda s, *a: plain(*a),
-        lambda s, *a: packed(EXTRA, s, *a),
-        lambda s, *a: packed(0, s, *a),
-    )
+    ways = [functools.partial(packed, spare) for spare in SPARES]
     return lax.switch(way.reshape(()), ways, scalars, *args)
 
 

time: 42.9 us -> 42.1 us (0.981)
  the two profiles are of different devices: /device:TPU:6 before, /device:TPU:64 now
where the time goes in v7:
time: 42.1 us; the launch traced here: 41.9 us
  starting transfers between devices  22.2 us (53%)
  Pallas kernels  13.5 us (32%)
  waiting for transfers between devices  5.07 us (12%)
  loops' own time  0.66 us (2%)
    pallas_call x10, Pallas kernels, call(): pl.pallas_call(kernel, out_shape=shapes, in_specs=list(specs), out_specs=...  13.5 us
    ppermute x2, starting transfers between devices, below(): lax.ppermute(value, 'gz', [(i, i - 1) for i in range(1, lax.axis_size('gz...  12.5 us
    ppermute x1, starting transfers between devices, packed(): north1 = lax.ppermute(ym1, 'gy', ring('gy', -1))  2.95 us
    ppermute x1, starting transfers between devices, packed(): north0 = lax.ppermute(ym0, 'gy', ring('gy', -1))  2.94 us
    ppermute x1, waiting for transfers between devices, packed(): second = lax.ppermute(second, 'gx', swaps('gx', 1))  2.83 us
    ppermute x1, starting transfers between devices, packed(): first = lax.ppermute(first, 'gx', swaps('gx', 0))  1.92 us
    ppermute x1, starting transfers between devices, packed(): second = lax.ppermute(second, 'gx', swaps('gx', 1))  1.92 us
    ppermute x2, waiting for transfers between devices, below(): lax.ppermute(value, 'gz', [(i, i - 1) for i in range(1, lax.axis_size('gz...  1.75 us
  transfers between devices with their start and end apart: 8, of which 4 were waited for; matrix products, arithmetic and copies ran while one was open for 0% of the time, Pallas kernels for 23%

profile of v7, /device:TPU:64, one launch (start us, length us, event | category | flops | bytes accessed | tf_op | source)
XLA Modules:
  0.0 41.9 jit_solution(15126788155321673702)
XLA Ops:
  0.0 1.0 %shard_map.77 = (s32[1]{0:T(128)S(4)}, s32[2]{0:T(128)S(4)}, f32[8]{0:T(128)S(4)}, f32[8]{0:T(128)S(4)}) custom-call(s32[1,128]{1,0:T(1,128)} %bitcast.26, f32[8]{0:T(128)} %refs_1_.1, f32[8]{0:T(128)} %refs_2_.1), custom_call_target="tpu_custom_call" | custom-call | tf_op jit(solution)/shard_map/pallas_call | solution.py:53
  1.0 40.7 %conditional.1 = (f32[8,64,8,128]{3,2,1,0:T(8,128)}) conditional(s32[]{:T(128)} %bitcast.13, (f32[8]{0:T(128)}, f32[8]{0:T(128)}, f32[8,64,8,128]{3,2,1,0:T(8,128)}, s32[64,8]{0,1:T(8,128)}, f32[128,128]{1,0:T(8,128)}, /*index=5*/f32[128,128]{1,0:T(8,128)}, s32[2]{0:T(128)S(4)}, f32[8]{0:T(128)S(4)}, ...), branch_computations={%region_0.0_spmd, %region_1.0_spmd, %region_2.0_spmd, %region_3.0_... | conditional | flops 13958645760 | bytes 51421888 | solution.py:718
  1.0 1.7 %branch_0_fun.9 = (f32[4096,128]{1,0:T(8,128)S(1)}, f32[528,128]{1,0:T(8,128)S(1)}, f32[648,128]{1,0:T(8,128)S(1)}, f32[512,128]{1,0:T(8,128)S(1)}, f32[648,128]...) custom-call(f32[4096,128]{1,0:T(8,128)} %bitcast.18, ...), custom_call_target="tpu_custom_call" | custom-call | flops 1000 | bytes 4194304 | tf_op jit(solution)/shard_map/cond/branch_0_fun/pallas_call | solution.py:53
  2.7 0.0 collective-permute-start
  2.7 2.9 %collective-permute-start.1 = (f32[648,128]{1,0:T(8,128)S(1)}, f32[648,128]{1,0:T(8,128)S(1)}, u32[]{:S(2)}, u32[]{:S(2)}) collective-permute-start(f32[648,128]{1,0:T(8,128)S(1)} %get-tuple-element.94), channel_id=1, source_target_pairs={{0,180},{12,0},{24,12},{36,24},{48,36},{60,48},{72,60},{84,72},{96... | collective-permute-start | bytes 995336 | tf_op jit(solution)/shard_map/cond/branch_0_fun/ppermute | solution.py:629
  5.7 0.0 collective-permute-start.4
  5.7 3.0 %collective-permute-start.5 = (f32[512,128]{1,0:T(8,128)S(1)}, f32[512,128]{1,0:T(8,128)S(1)}, u32[]{:S(2)}, u32[]{:S(2)}) collective-permute-start(f32[512,128]{1,0:T(8,128)S(1)} %get-tuple-element.106), channel_id=1, source_target_pairs={{0,180},{12,0},{24,12},{36,24},{48,36},{60,48},{72,60},{84,72},{96... | collective-permute-start | bytes 786440 | tf_op jit(solution)/shard_map/cond/branch_0_fun/ppermute | solution.py:631
  8.6 0.0 copy-start
  8.7 1.7 %branch_0_fun.11 = (f32[4352,128]{1,0:T(8,128)S(1)}, bf16[256,256]{1,0:T(8,128)(2,1)S(1)}, bf16[256,256]{1,0:T(8,128)(2,1)S(1)}) custom-call(f32[4096,128]{1,0:T(8,128)S(1)} %get-tuple-element.91.refs_0_, f32[528,128]{1,0:T(8,128)S(1)} %get-tuple-element.92.refs_1_.refs_10_.refs_12_.refs_13_, ...), custom_call_target="tpu_custom_call", output_to_operand_aliasing={{1}: (2, {}), {2}: (3, {})} | custom-call | flops 3221225472 | bytes 8388608 | tf_op jit(solution)/shard_map/cond/branch_0_fun/pallas_call | solution.py:53
  10.4 0.1 collective-permute-done.refs_2_.refs_6_.refs_7_.refs_9_.refs_5_
  10.5 0.0 collective-permute-done.1.refs_3_.refs_7_.refs_8_.refs_10_.refs_6_
  10.5 0.0 copy-done
  10.5 0.1 broadcast_in_dim.16.refs_3_
  10.6 0.0 copy-done.4
  10.6 0.1 broadcast_in_dim.17.refs_4_
  10.6 2.3 %branch_0_fun.12 = (f32[2112,128]{1,0:T(8,128)S(1)}, f32[4224,128]{1,0:T(8,128)S(1)}, f32[1024,128]{1,0:T(8,128)S(1)}, f32[4224,128]{1,0:T(8,128)S(1)}, f32[1024...) custom-call(s32[2]{0:T(128)S(4)} %get-tuple-element.80.refs_0_, ...), custom_call_target="tpu_custom_call", output_to_operand_aliasing={{7}: (8, {}), {8}: (9, {})} | custom-call | flops 3221225472 | bytes 8388608 | tf_op jit(solution)/shard_map/cond/branch_0_fun/pallas_call | solution.py:53
  12.9 0.4 collective-permute-done.4.refs_9_
  13.3 0.0 collective-permute-done.5.refs_10_
  13.3 10.6 %collective-permute-start.6 = (f32[1104,128]{1,0:T(8,128)S(1)}, f32[1104,128]{1,0:T(8,128)S(1)}, u32[]{:S(2)}, u32[]{:S(2)}) collective-permute-start(f32[1104,128]{1,0:T(8,128)S(1)} %get-tuple-element.137), channel_id=1, source_target_pairs={{1,0},{2,1},{3,2},{4,3},{5,4},{6,5},{7,6},{8,7},{9,8},{10,9},{11,1... | collective-permute-start | bytes 1695752 | tf_op jit(solution)/shard_map/cond/branch_0_fun/ppermute | solution.py:611
  23.9 0.1 branch_0_fun.10
  23.9 1.9 %collective-permute-start.2 = (f32[168,128]{1,0:T(8,128)S(1)}, f32[168,128]{1,0:T(8,128)S(1)}, u32[]{:S(2)}, u32[]{:S(2)}) collective-permute-start(f32[168,128]{1,0:T(8,128)S(1)} %get-tuple-element.95), channel_id=1, source_target_pairs={{0,192},{192,0},{384,576},{576,384},{1,193},{193,1},{385,577},{577... | collective-permute-start | bytes 258056 | tf_op jit(solution)/shard_map/cond/branch_0_fun/ppermute | solution.py:653
  25.9 1.9 %collective-permute-start.3 = (f32[168,128]{1,0:T(8,128)S(1)}, f32[168,128]{1,0:T(8,128)S(1)}, u32[]{:S(2)}, u32[]{:S(2)}) collective-permute-start(f32[168,128]{1,0:T(8,128)S(1)} %get-tuple-element.96), channel_id=1, source_target_pairs={{0,576},{192,384},{384,192},{576,0},{1,577},{193,385},{385,193},{5... | collective-permute-start | bytes 258056 | tf_op jit(solution)/shard_map/cond/branch_0_fun/ppermute | solution.py:654
  27.8 2.8 %branch_0_fun.13 = (f32[2112,128]{1,0:T(8,128)S(1)}, f32[4224,128]{1,0:T(8,128)S(1)}, f32[1024,128]{1,0:T(8,128)S(1)}, f32[4224,128]{1,0:T(8,128)S(1)}, f32[1024...) custom-call(s32[2]{0:T(128)S(4)} %get-tuple-element.80.refs_0_, ...), custom_call_target="tpu_custom_call", output_to_operand_aliasing={{0}: (13, {}), {1}: (14, {}), {2}: (15, {}), {3}: (16, {}),... | custom-call | flops 3221225472 | bytes 8388608 | tf_op jit(solution)/shard_map/cond/branch_0_fun/pallas_call | solution.py:53
  30.6 0.0 collective-permute-done.2.refs_5_
  30.6 2.8 %collective-permute-done.3.refs_6_ = f32[168,128]{1,0:T(8,128)S(1)} collective-permute-done((f32[168,128]{1,0:T(8,128)S(1)}, f32[168,128]{1,0:T(8,128)S(1)}, u32[]{:S(2)}, u32[]{:S(2)}) %collective-permute-start.3) | collective-permute-done | bytes 86048 | tf_op jit(solution)/shard_map/cond/branch_0_fun/ppermute | solution.py:654
  33.4 0.8 %branch_0_fun.14 = (f32[4352,128]{1,0:T(8,128)S(1)}, f32[2112,128]{1,0:T(8,128)S(1)}, f32[528,128]{1,0:T(8,128)S(1)}, f32[4224,128]{1,0:T(8,128)S(1)}, f32[1024,...) custom-call(s32[2]{0:T(128)S(4)} %get-tuple-element.80.refs_0_, ...), custom_call_target="tpu_custom_call", output_to_operand_aliasing={{0}: (11, {}), {1}: (12, {}), {2}: (13, {}), {3}: (14, {}),... | custom-call | flops 268435456 | bytes 1048576 | tf_op jit(solution)/shard_map/cond/branch_0_fun/pallas_call | solution.py:53
  34.2 1.9 %collective-permute-start.7 = (f32[72,128]{1,0:T(8,128)S(1)}, f32[72,128]{1,0:T(8,128)S(1)}, u32[]{:S(2)}, u32[]{:S(2)}) collective-permute-start(f32[72,128]{1,0:T(8,128)S(1)} %get-tuple-element.146), channel_id=1, source_target_pairs={{1,0},{2,1},{3,2},{4,3},{5,4},{6,5},{7,6},{8,7},{9,8},{10,9},{11,1... | collective-permute-start | bytes 110600 | tf_op jit(solution)/shard_map/cond/branch_0_fun/ppermute | solution.py:611
  36.1 0.4 branch_0_fun.15
  36.5 0.0 collective-permute-done.6.refs_10_
  36.5 1.8 %branch_0_fun.16 = (f32[4096,128]{1,0:T(8,128)}, f32[4224,128]{1,0:T(8,128)S(1)}, f32[1024,128]{1,0:T(8,128)S(1)}, f32[4096,128]{1,0:T(8,128)S(1)}, f32[128,128]...) custom-call(s32[2]{0:T(128)S(4)} %get-tuple-element.80.refs_0_, ...), custom_call_target="tpu_custom_call", output_to_operand_aliasing={{1}: (12, {}), {2}: (13, {}), {3}: (14, {}), {6}: (3, {}), ... | custom-call | flops 3221225472 | bytes 8388608 | tf_op jit(solution)/shard_map/cond/branch_0_fun/pallas_call | solution.py:53
  38.3 1.7 %collective-permute-done.7.refs_12_ = f32[72,128]{1,0:T(8,128)S(1)} collective-permute-done((f32[72,128]{1,0:T(8,128)S(1)}, f32[72,128]{1,0:T(8,128)S(1)}, u32[]{:S(2)}, u32[]{:S(2)}) %collective-permute-start.7) | collective-permute-done | bytes 36896 | tf_op jit(solution)/shard_map/cond/branch_0_fun/ppermute | solution.py:611
  40.1 1.1 %branch_0_fun.17 = (f32[4096,128]{1,0:T(8,128)}, f32[4224,128]{1,0:T(8,128)S(1)}, f32[1024,128]{1,0:T(8,128)S(1)}, f32[4096,128]{1,0:T(8,128)S(1)}) custom-call(s32[2]{0:T(128)S(4)} %get-tuple-element.80.refs_0_, f32[8]{0:T(128)S(4)} %get-tuple-element.82.refs_1_, ...), custom_call_target="tpu_custom_call", output_to_operand_aliasing={{0}: (13, {}), {1}: (14, {}), {2}: (15, {}), {3}: (16, {})} | custom-call | flops 268435456 | bytes 1048576 | tf_op jit(solution)/shard_map/cond/branch_0_fun/pallas_call | solution.py:53
  (1 shorter events, 0.0 us)
Async XLA Ops:
  2.7 7.8 %collective-permute-start = (f32[648,128]{1,0:T(8,128)S(1)}, f32[648,128]{1,0:T(8,128)S(1)}, u32[]{:S(2)}, u32[]{:S(2)}) collective-permute-start(f32[648,128]{1,0:T(8,128)S(1)} %get-tuple-element.93), channel_id=1, source_target_pairs={{0,12},{12,24},{24,36},{36,48},{48,60},{60,72},{72,84},{84,96},{96... | collective-permute-start | bytes 995336 | tf_op jit(solution)/shard_map/cond/branch_0_fun/ppermute | solution.py:628
  2.7 7.7 %collective-permute-start.1 = (f32[648,128]{1,0:T(8,128)S(1)}, f32[648,128]{1,0:T(8,128)S(1)}, u32[]{:S(2)}, u32[]{:S(2)}) collective-permute-start(f32[648,128]{1,0:T(8,128)S(1)} %get-tuple-element.94), channel_id=1, source_target_pairs={{0,180},{12,0},{24,12},{36,24},{48,36},{60,48},{72,60},{84,72},{96... | collective-permute-start | bytes 995336 | tf_op jit(solution)/shard_map/cond/branch_0_fun/ppermute | solution.py:629
  5.7 7.6 %collective-permute-start.4 = (f32[512,128]{1,0:T(8,128)S(1)}, f32[512,128]{1,0:T(8,128)S(1)}, u32[]{:S(2)}, u32[]{:S(2)}) collective-permute-start(f32[512,128]{1,0:T(8,128)S(1)} %get-tuple-element.105), channel_id=1, source_target_pairs={{0,12},{12,24},{24,36},{36,48},{48,60},{60,72},{72,84},{84,96},{96... | collective-permute-start | bytes 786440 | tf_op jit(solution)/shard_map/cond/branch_0_fun/ppermute | solution.py:630
  5.7 7.6 %collective-permute-start.5 = (f32[512,128]{1,0:T(8,128)S(1)}, f32[512,128]{1,0:T(8,128)S(1)}, u32[]{:S(2)}, u32[]{:S(2)}) collective-permute-start(f32[512,128]{1,0:T(8,128)S(1)} %get-tuple-element.106), channel_id=1, source_target_pairs={{0,180},{12,0},{24,12},{36,24},{48,36},{60,48},{72,60},{84,72},{96... | collective-permute-start | bytes 786440 | tf_op jit(solution)/shard_map/cond/branch_0_fun/ppermute | solution.py:631
  8.6 1.8 %copy-start = (f32[8]{0:T(128)S(1)}, f32[8]{0:T(128)}, u32[]{:S(2)}) copy-start(f32[8]{0:T(128)} %get-tuple-element.85) | copy-start | bytes 100 | tf_op jit(solution)/shard_map/cond
  8.6 1.9 %copy-start.4 = (f32[8]{0:T(128)S(1)}, f32[8]{0:T(128)}, u32[]{:S(2)}) copy-start(f32[8]{0:T(128)} %get-tuple-element.86) | copy-start | bytes 100 | tf_op jit(solution)/shard_map/cond
  13.3 23.2 %collective-permute-start.6 = (f32[1104,128]{1,0:T(8,128)S(1)}, f32[1104,128]{1,0:T(8,128)S(1)}, u32[]{:S(2)}, u32[]{:S(2)}) collective-permute-start(f32[1104,128]{1,0:T(8,128)S(1)} %get-tuple-element.137), channel_id=1, source_target_pairs={{1,0},{2,1},{3,2},{4,3},{5,4},{6,5},{7,6},{8,7},{9,8},{10,9},{11,1... | collective-permute-start | bytes 1695752 | tf_op jit(solution)/shard_map/cond/branch_0_fun/ppermute | solution.py:611
  23.9 6.7 %collective-permute-start.2 = (f32[168,128]{1,0:T(8,128)S(1)}, f32[168,128]{1,0:T(8,128)S(1)}, u32[]{:S(2)}, u32[]{:S(2)}) collective-permute-start(f32[168,128]{1,0:T(8,128)S(1)} %get-tuple-element.95), channel_id=1, source_target_pairs={{0,192},{192,0},{384,576},{576,384},{1,193},{193,1},{385,577},{577... | collective-permute-start | bytes 258056 | tf_op jit(solution)/shard_map/cond/branch_0_fun/ppermute | solution.py:653
  25.9 7.6 %collective-permute-start.3 = (f32[168,128]{1,0:T(8,128)S(1)}, f32[168,128]{1,0:T(8,128)S(1)}, u32[]{:S(2)}, u32[]{:S(2)}) collective-permute-start(f32[168,128]{1,0:T(8,128)S(1)} %get-tuple-element.96), channel_id=1, source_target_pairs={{0,576},{192,384},{384,192},{576,0},{1,577},{193,385},{385,193},{5... | collective-permute-start | bytes 258056 | tf_op jit(solution)/shard_map/cond/branch_0_fun/ppermute | solution.py:654
  34.2 5.8 %collective-permute-start.7 = (f32[72,128]{1,0:T(8,128)S(1)}, f32[72,128]{1,0:T(8,128)S(1)}, u32[]{:S(2)}, u32[]{:S(2)}) collective-permute-start(f32[72,128]{1,0:T(8,128)S(1)} %get-tuple-element.146), channel_id=1, source_target_pairs={{1,0},{2,1},{3,2},{4,3},{5,4},{6,5},{7,6},{8,7},{9,8},{10,9},{11,1... | collective-permute-start | bytes 110600 | tf_op jit(solution)/shard_map/cond/branch_0_fun/ppermute | solution.py:611

commit v8 on v7

--- a/solution.py
+++ b/solution.py
@@ -14,7 +14,7 @@
 XA = X + 2
 LOW = Z // 2
 HALF = 2 * LOW * X
-ENDS = HALF + 2 * X
+ENDS = HALF + T
 XROWS = 2 * Z * Y
 EARLY = (X - 2) + 2 * X // T + (X - 4)
 SPARES = (0, 8, 24, B)
@@ -123,6 +123,7 @@
         copy.start()
     copies[Z].wait()
     columns = mask[...].astype(F32)
+    wide = jnp.concatenate([columns, jnp.zeros((Y, B - X), F32)], axis=1)
     for x in range(X):
         m1[(x + 1) * Y : (x + 2) * Y] = jnp.broadcast_to(columns[:, x : x + 1], (Y, B))
     for i, (ref, out, turned) in enumerate(((k_ref, kk, True), (t_ref, tt, False))):
@@ -132,8 +133,8 @@
         half = jnp.concatenate([high, low], axis=1)
         out[...] = jnp.concatenate([half, half], axis=0)
     for out, ys in ((ym0, (0, 1)), (yp0, (Y - 1, Y - 2))):
-        for d, y in enumerate(ys):
-            out[HALF + d * X : HALF + (d + 1) * X] = m1[pl.ds(Y + y, X, stride=Y), :]
+        picked = [wide[y : y + 1] for y in ys] + [jnp.zeros((T - 2, B), F32)]
+        out[HALF : HALF + T] = jnp.concatenate(picked, axis=0)
     for z in range(Z):
         copies[z].wait()
         for outs, ys in (((ym0, ym1), (0, 1)), ((yp0, yp1), (Y - 1, Y - 2))):
@@ -146,7 +147,7 @@
             out[at : at + LOW] = own[pl.ds(start, LOW, stride=X * Y), :]
 
 
-def sides_body(own, m1, south, north, first, second):
+def sides_body(own, m1, south, north, south_mask, north_mask, first, second):
     even = lax.axis_index("gx") % 2 == 0
     for out, to_right in ((first, even), (second, jnp.logical_not(even))):
         edge = jnp.where(to_right, X - 1, 0)
@@ -158,13 +159,13 @@
                 out[(d * Z + z) * Y : (d * Z + z + 1) * Y] = own[rows((z * X + x) * Y)]
         at = XROWS + 2 * Y
         out[at + 2 * Z :] = jnp.zeros((T, B), F32)
-        for side, ref in enumerate((south, north)):
+        for side, (ref, mask_ref) in enumerate(((south, south_mask), (north, north_mask))):
             row = at + side * Z
             end = ENDS + jnp.where(to_right, LOW, 0)
             out[row : row + LOW] = ref[pl.ds(edge, LOW, stride=X), :]
             out[row + LOW : row + Z] = ref[pl.ds(end, LOW), :]
             row = at + 2 * Z + side
-            out[row : row + 1] = ref[pl.ds(HALF + edge, 1), :]
+            out[row : row + 1] = mask_ref[pl.ds(edge, 1), :]
 
 
 XMESSAGE = XROWS + 2 * Y + 2 * Z + T
@@ -187,10 +188,19 @@
 def collide_rows(part, south, north, masks, cy, k, t):
     for side, (ref, mask_ref) in enumerate(zip((south, north), masks)):
         for d in range(2):
-            mask = jnp.concatenate([mask_ref[HALF + d * X : HALF + (d + 1) * X]] * LOW, axis=0)
+            mask = jnp.concatenate([mask_ref[d * X : (d + 1) * X]] * LOW, axis=0)
             c = collide(ref[d * LOW * X : (d + 1) * LOW * X], mask, k, t)
             for z in range(LOW):
                 cy[pl.ds(cy_at(side, d, 0) + part * LOW + z, X, stride=Z), :] = c[z * X : (z + 1) * X]
+
+
+def widen(ref, out):
+    row, lane = (lax.broadcasted_iota(jnp.int32, (X, B), i) for i in range(2))
+    ones = jnp.ones((B, B), BF16)
+    for d in range(2):
+        values = jnp.concatenate([eightfold(ref, HALF + d)] * (X // T), axis=0)
+        picked = jnp.where(row == lane, values, 0.0).astype(BF16)
+        out[d * X : (d + 1) * X] = jnp.dot(picked, ones, preferred_element_type=F32)
 
 
 def upwind(z, u_ref, v_ref):
@@ -263,7 +273,7 @@
             a = [a1y[pl.ds(i * T * Z + z + j, T, stride=Z), :] for j in range(H_MAX + 1)]
             pieces.append(fall(c0, cc2, *a))
             side, first = divmod(i * T, X)
-            cloudy.append(masks[side][HALF + first : HALF + first + T])
+            cloudy.append(masks[side][first : first + T])
             where.append(z * 2 * X + i * T)
     c = collide(jnp.concatenate(pieces, axis=0), jnp.concatenate(cloudy, axis=0), k, t)
     for i, to in enumerate(where):
@@ -296,11 +306,13 @@
 
 
 def early_body(
-    spare, sc, u_ref, v_ref, ub, vb, c1, south, north, kk, tt, m1, cy, a1, a1y, c2, c2y, a2, pay
+    spare, sc, u_ref, v_ref, ub, vb, c1, south, north, kk, tt, m1, cy, a1, a1y, c2, c2y, a2, pay, sm, nm
 ):
     k, t = kk[...], tt[...]
     c0, cc2 = classes(sc)
-    collide_rows(0, south, north, (south, north), cy, k, t)
+    widen(south, sm)
+    widen(north, nm)
+    collide_rows(0, south, north, (sm, nm), cy, k, t)
 
     def first(z, _):
         advect_first(z, range(2, X), c1, a1, cy, u_ref, v_ref)
@@ -314,7 +326,7 @@
         return 0
 
     lax.fori_loop(0, 2, second, 0, unroll=2)
-    settle_rows(range(2), ROW_TILES, c0, cc2, a1y, (south, north), c2y, k, t)
+    settle_rows(range(2), ROW_TILES, c0, cc2, a1y, (sm, nm), c2y, k, t)
 
     def third(z, _):
         advect_second(z, range(2, X - 2), c2, a2, c2y, u_ref, v_ref)
@@ -516,7 +528,7 @@
     for i in ROW_TILES:
         row7[i * T : (i + 1) * T], row6[i * T : (i + 1) * T] = unpack(early, X - 2 + i)
     settle_top_rows(ROW_TILES, row7, row6, c0, cc2, a1y, c2y)
-    mask = jnp.concatenate([south[HALF : HALF + X], north[HALF : HALF + X]] * 2, axis=0)
+    mask = jnp.concatenate([south[0:X], north[0:X]] * 2, axis=0)
     at = slice(12 * X, 16 * X)
     c2y[at] = collide(c2y[at], mask, k, t)
     for z in (6, 7):
@@ -569,7 +581,7 @@
     for tile in ROW_EDGES:
         x6, x7 = (a1y[pl.ds(tile * T * Z + z, T, stride=Z), :] for z in (6, 7))
         side, first = divmod(tile * T, X)
-        mask = (south, north)[side][HALF + first : HALF + first + T]
+        mask = (south, north)[side][first : first + T]
         for z, value in ((6, fall(c0, cc2, x6, x7, fixed[tile][1])), (7, jnp.where(c0, x7, fixed[tile][0]))):
             where.append((c2y, z * 2 * X + tile * T))
             pieces.append(value)
@@ -630,12 +642,12 @@
     south1 = lax.ppermute(yp1, "gy", ring("gy", 1))
     north1 = lax.ppermute(ym1, "gy", ring("gy", -1))
     c1, kk, tt = call(
-        own_body, [v(Z * XW * Y)], [own, m1, kk, tt], [VMEM] * 4, cost=(3 << 30, 8 << 20), keep=(2, 3)
+        own_body, [v(Z * XW * Y)], [own, m1, kk, tt], [VMEM] * 4, cost=(1 << 30, 2 << 20), keep=(2, 3)
     )
     shapes = [v(4 * XA * Z), v(Z * XA * T), v(2 * X * Z), v(Z * XA * T), v(Z * 2 * X), v(Z * X * T)]
-    cy, a1, a1y, c2, c2y, a2, pay, kk, tt = call(
+    cy, a1, a1y, c2, c2y, a2, pay, south_mask, north_mask, kk, tt = call(
         functools.partial(early_body, spare),
-        shapes + [v((EARLY + spare_tiles(spare)) * T)],
+        shapes + [v((EARLY + spare_tiles(spare)) * T), v(2 * X), v(2 * X)],
         [*scalars, ub, vb, c1, south0, north0, kk, tt, m1],
         [SMEM] * 3 + [VMEM] * 8,
         cost=(3 << 30, 8 << 20),
@@ -646,8 +658,8 @@
     first, second = call(
         sides_body,
         [v(XMESSAGE)] * 2,
-        [own, m1, south0, north0],
-        [VMEM] * 4,
+        [own, m1, south0, north0, south_mask, north_mask],
+        [VMEM] * 6,
         cost=(1000, 1 << 18),
     )
     first = lax.ppermute(first, "gx", swaps("gx", 0))
@@ -655,7 +667,7 @@
     cy, a1, a1y, c2, c2y, a2, res, kk, tt = call(
         between_body,
         shapes + [v(4 * X * T)],
-        [*scalars, ub, vb, kk, tt, south0, north0, south1, north1, c1, m1, cy, a1, a1y, c2, c2y, a2],
+        [*scalars, ub, vb, kk, tt, south_mask, north_mask, south1, north1, c1, m1, cy, a1, a1y, c2, c2y, a2],
         [SMEM] * 3 + [VMEM] * 16,
         cost=(3 << 30, 8 << 20),
         aliases={13 + i: i for i in range(6)},
@@ -664,7 +676,7 @@
     c1, cy, m1, a1, a1y, c2, c2y, a2, pay, kk, tt = call(
         functools.partial(late_body, spare),
         [v(Z * XW * Y), shapes[0], v(XA * Y)] + shapes[1:] + [v((2 if spare else 1) * LATE * T)],
-        [*scalars, ub, vb, first, second, kk, tt, south0, north0, c1, cy, m1, a1, a1y, c2, c2y, a2],
+        [*scalars, ub, vb, first, second, kk, tt, south_mask, north_mask, c1, cy, m1, a1, a1y, c2, c2y, a2],
         [SMEM] * 3 + [VMEM] * 16,
         [pltpu.VMEM((2, XMESSAGE, B), F32)],
         cost=(1 << 28, 1 << 20),
@@ -675,7 +687,7 @@
     a1, c2, c2y, a2, res, kk, tt = call(
         rest_body,
         [shapes[1], *shapes[3:], v(4 * X * T)],
-        [*scalars, kk, tt, south0, north0, c1, m1, cy, a1y, a1, c2, c2y, a2, res],
+        [*scalars, kk, tt, south_mask, north_mask, c1, m1, cy, a1y, a1, c2, c2y, a2, res],
         [SMEM] * 3 + [VMEM] * 13,
         cost=(1 << 29, 1 << 20),
         aliases={11 + i: i for i in range(5)},
@@ -684,7 +696,7 @@
     out, c2, c2y, a2, row7, row6, kk, tt = call(
         functools.partial(upper_body, spare),
         [((Z * X * Y, B), F32, False), *shapes[3:], v(2 * X), v(2 * X)],
-        [*scalars, kk, tt, south0, north0, m1, a1, a1y, early, res, c2, c2y, a2],
+        [*scalars, kk, tt, south_mask, north_mask, m1, a1, a1y, early, res, c2, c2y, a2],
         [SMEM] * 3 + [VMEM] * 12,
         [pltpu.VMEM((4 * X * T, B), F32), pltpu.SemaphoreType.DMA((5,))],
         cost=(3 << 30, 8 << 20),
@@ -695,7 +707,7 @@
     out, *_ = call(
         functools.partial(last_body, spare),
         [((Z * X * Y, B), F32, False), *shapes[3:]],
-        [*scalars, kk, tt, south0, north0, m1, a1, a1y, row7, row6, late, out, c2, c2y, a2],
+        [*scalars, kk, tt, south_mask, north_mask, m1, a1, a1y, row7, row6, late, out, c2, c2y, a2],
         [SMEM] * 3 + [VMEM] * 10 + [HBM] + [VMEM] * 3,
         [pltpu.VMEM((4 * len(ENDING) * T, B), F32), pltpu.SemaphoreType.DMA((8,))],
         cost=(1 << 28, 1 << 20),

time: 42.1 us -> 41.7 us (level)
  transfers between devices with their start and end apart: 8 -> 8, of which waited for: 4 -> 2; matrix products, arithmetic and copies ran while one was open for 0% -> 0% of each run, Pallas kernels for 23% -> 23%
where the time goes in v8:
time: 41.7 us; the launch traced here: 41.4 us
  starting transfers between devices  22.2 us (53%)
  Pallas kernels  13.4 us (32%)
  waiting for transfers between devices  4.74 us (11%)
  loops' own time  0.72 us (2%)
    pallas_call x10, Pallas kernels, call(): pl.pallas_call(kernel, out_shape=shapes, in_specs=list(specs), out_specs=...  13.4 us
    ppermute x2, starting transfers between devices, below(): lax.ppermute(value, 'gz', [(i, i - 1) for i in range(1, lax.axis_size('gz...  12.5 us
    ppermute x1, waiting for transfers between devices, packed(): second = lax.ppermute(second, 'gx', swaps('gx', 1))  2.97 us
    ppermute x1, starting transfers between devices, packed(): north1 = lax.ppermute(ym1, 'gy', ring('gy', -1))  2.95 us
    ppermute x1, starting transfers between devices, packed(): north0 = lax.ppermute(ym0, 'gy', ring('gy', -1))  2.94 us
    ppermute x1, starting transfers between devices, packed(): first = lax.ppermute(first, 'gx', swaps('gx', 0))  1.92 us
    ppermute x1, starting transfers between devices, packed(): second = lax.ppermute(second, 'gx', swaps('gx', 1))  1.92 us
    ppermute x2, waiting for transfers between devices, below(): lax.ppermute(value, 'gz', [(i, i - 1) for i in range(1, lax.axis_size('gz...  1.75 us
  transfers between devices with their start and end apart: 8, of which 2 were waited for; matrix products, arithmetic and copies ran while one was open for 0% of the time, Pallas kernels for 23%

profile of v8, /device:TPU:64, one launch (start us, length us, event | category | flops | bytes accessed | tf_op | source)
XLA Modules:
  0.0 41.4 jit_solution(12098945305347697907)
XLA Ops:
  0.0 1.0 %shard_map.77 = (s32[1]{0:T(128)S(4)}, s32[2]{0:T(128)S(4)}, f32[8]{0:T(128)S(4)}, f32[8]{0:T(128)S(4)}) custom-call(s32[1,128]{1,0:T(1,128)} %bitcast.26, f32[8]{0:T(128)} %refs_1_.1, f32[8]{0:T(128)} %refs_2_.1), custom_call_target="tpu_custom_call" | custom-call | tf_op jit(solution)/shard_map/pallas_call | solution.py:53
  1.0 40.2 %conditional.1 = (f32[8,64,8,128]{3,2,1,0:T(8,128)}) conditional(s32[]{:T(128)} %bitcast.13, (f32[8]{0:T(128)}, f32[8]{0:T(128)}, f32[8,64,8,128]{3,2,1,0:T(8,128)}, s32[64,8]{0,1:T(8,128)}, f32[128,128]{1,0:T(8,128)}, /*index=5*/f32[128,128]{1,0:T(8,128)}, s32[2]{0:T(128)S(4)}, f32[8]{0:T(128)S(4)}, ...), branch_computations={%region_0.0_spmd, %region_1.0_spmd, %region_2.0_spmd, %region_3.0_... | conditional | flops 11811162112 | bytes 44638912 | solution.py:730
  1.0 1.7 %branch_0_fun.9 = (f32[4096,128]{1,0:T(8,128)S(1)}, f32[528,128]{1,0:T(8,128)S(1)}, f32[528,128]{1,0:T(8,128)S(1)}, f32[512,128]{1,0:T(8,128)S(1)}, f32[528,128]...) custom-call(f32[4096,128]{1,0:T(8,128)} %bitcast.14, ...), custom_call_target="tpu_custom_call" | custom-call | flops 1000 | bytes 4194304 | tf_op jit(solution)/shard_map/cond/branch_0_fun/pallas_call | solution.py:53
  2.7 0.0 copy-start
  2.7 0.0 copy-start.4
  2.7 0.0 collective-permute-start
  2.8 2.9 %collective-permute-start.1 = (f32[528,128]{1,0:T(8,128)S(1)}, f32[528,128]{1,0:T(8,128)S(1)}, u32[]{:S(2)}, u32[]{:S(2)}) collective-permute-start(f32[528,128]{1,0:T(8,128)S(1)} %get-tuple-element.94), channel_id=1, source_target_pairs={{0,180},{12,0},{24,12},{36,24},{48,36},{60,48},{72,60},{84,72},{96... | collective-permute-start | bytes 811016 | tf_op jit(solution)/shard_map/cond/branch_0_fun/ppermute | solution.py:641
  5.7 0.0 collective-permute-start.4
  5.7 3.0 %collective-permute-start.5 = (f32[512,128]{1,0:T(8,128)S(1)}, f32[512,128]{1,0:T(8,128)S(1)}, u32[]{:S(2)}, u32[]{:S(2)}) collective-permute-start(f32[512,128]{1,0:T(8,128)S(1)} %get-tuple-element.108), channel_id=1, source_target_pairs={{0,180},{12,0},{24,12},{36,24},{48,36},{60,48},{72,60},{84,72},{96... | collective-permute-start | bytes 786440 | tf_op jit(solution)/shard_map/cond/branch_0_fun/ppermute | solution.py:643
  8.7 1.7 %branch_0_fun.10 = (f32[4352,128]{1,0:T(8,128)S(1)}, bf16[256,256]{1,0:T(8,128)(2,1)S(1)}, bf16[256,256]{1,0:T(8,128)(2,1)S(1)}) custom-call(f32[4096,128]{1,0:T(8,128)S(1)} %get-tuple-element.91.refs_0_, f32[528,128]{1,0:T(8,128)S(1)} %get-tuple-element.92.refs_1_.refs_10_.refs_12_.refs_13_, ...), custom_call_target="tpu_custom_call", output_to_operand_aliasing={{1}: (2, {}), {2}: (3, {})} | custom-call | flops 1073741824 | bytes 2097152 | tf_op jit(solution)/shard_map/cond/branch_0_fun/pallas_call | solution.py:53
  10.4 0.0 collective-permute-done.refs_6_.refs_2_
  10.4 0.0 collective-permute-done.1.refs_7_.refs_3_
  10.4 0.0 copy-done
  10.4 0.1 broadcast_in_dim.16.refs_3_
  10.5 0.1 broadcast_in_dim.17.refs_4_
  10.6 2.2 %branch_0_fun.11 = (f32[2112,128]{1,0:T(8,128)S(1)}, f32[4224,128]{1,0:T(8,128)S(1)}, f32[1024,128]{1,0:T(8,128)S(1)}, f32[4224,128]{1,0:T(8,128)S(1)}, f32[1024...) custom-call(s32[2]{0:T(128)S(4)} %get-tuple-element.80.refs_0_, ...), custom_call_target="tpu_custom_call", output_to_operand_aliasing={{9}: (8, {}), {10}: (9, {})} | custom-call | flops 3221225472 | bytes 8388608 | tf_op jit(solution)/shard_map/cond/branch_0_fun/pallas_call | solution.py:53
  12.8 0.0 collective-permute-done.4.refs_9_
  12.9 0.0 collective-permute-done.5.refs_10_
  12.9 10.6 %collective-permute-start.6 = (f32[1104,128]{1,0:T(8,128)S(1)}, f32[1104,128]{1,0:T(8,128)S(1)}, u32[]{:S(2)}, u32[]{:S(2)}) collective-permute-start(f32[1104,128]{1,0:T(8,128)S(1)} %get-tuple-element.139), channel_id=1, source_target_pairs={{1,0},{2,1},{3,2},{4,3},{5,4},{6,5},{7,6},{8,7},{9,8},{10,9},{11,1... | collective-permute-start | bytes 1695752 | tf_op jit(solution)/shard_map/cond/branch_0_fun/ppermute | solution.py:623
  23.4 0.1 branch_0_fun.12
  23.5 1.9 %collective-permute-start.2 = (f32[168,128]{1,0:T(8,128)S(1)}, f32[168,128]{1,0:T(8,128)S(1)}, u32[]{:S(2)}, u32[]{:S(2)}) collective-permute-start(f32[168,128]{1,0:T(8,128)S(1)} %get-tuple-element.102), channel_id=1, source_target_pairs={{0,192},{192,0},{384,576},{576,384},{1,193},{193,1},{385,577},{577... | collective-permute-start | bytes 258056 | tf_op jit(solution)/shard_map/cond/branch_0_fun/ppermute | solution.py:665
  25.4 1.9 %collective-permute-start.3 = (f32[168,128]{1,0:T(8,128)S(1)}, f32[168,128]{1,0:T(8,128)S(1)}, u32[]{:S(2)}, u32[]{:S(2)}) collective-permute-start(f32[168,128]{1,0:T(8,128)S(1)} %get-tuple-element.103), channel_id=1, source_target_pairs={{0,576},{192,384},{384,192},{576,0},{1,577},{193,385},{385,193},{5... | collective-permute-start | bytes 258056 | tf_op jit(solution)/shard_map/cond/branch_0_fun/ppermute | solution.py:666
  27.3 2.7 %branch_0_fun.13 = (f32[2112,128]{1,0:T(8,128)S(1)}, f32[4224,128]{1,0:T(8,128)S(1)}, f32[1024,128]{1,0:T(8,128)S(1)}, f32[4224,128]{1,0:T(8,128)S(1)}, f32[1024...) custom-call(s32[2]{0:T(128)S(4)} %get-tuple-element.80.refs_0_, ...), custom_call_target="tpu_custom_call", output_to_operand_aliasing={{0}: (13, {}), {1}: (14, {}), {2}: (15, {}), {3}: (16, {}),... | custom-call | flops 3221225472 | bytes 8388608 | tf_op jit(solution)/shard_map/cond/branch_0_fun/pallas_call | solution.py:53
  30.0 0.0 collective-permute-done.2.refs_5_
  30.0 3.0 %collective-permute-done.3.refs_6_ = f32[168,128]{1,0:T(8,128)S(1)} collective-permute-done((f32[168,128]{1,0:T(8,128)S(1)}, f32[168,128]{1,0:T(8,128)S(1)}, u32[]{:S(2)}, u32[]{:S(2)}) %collective-permute-start.3) | collective-permute-done | bytes 86048 | tf_op jit(solution)/shard_map/cond/branch_0_fun/ppermute | solution.py:666
  33.0 0.8 %branch_0_fun.14 = (f32[4352,128]{1,0:T(8,128)S(1)}, f32[2112,128]{1,0:T(8,128)S(1)}, f32[528,128]{1,0:T(8,128)S(1)}, f32[4224,128]{1,0:T(8,128)S(1)}, f32[1024,...) custom-call(s32[2]{0:T(128)S(4)} %get-tuple-element.80.refs_0_, ...), custom_call_target="tpu_custom_call", output_to_operand_aliasing={{0}: (11, {}), {1}: (12, {}), {2}: (13, {}), {3}: (14, {}),... | custom-call | flops 268435456 | bytes 1048576 | tf_op jit(solution)/shard_map/cond/branch_0_fun/pallas_call | solution.py:53
  33.8 1.9 %collective-permute-start.7 = (f32[72,128]{1,0:T(8,128)S(1)}, f32[72,128]{1,0:T(8,128)S(1)}, u32[]{:S(2)}, u32[]{:S(2)}) collective-permute-start(f32[72,128]{1,0:T(8,128)S(1)} %get-tuple-element.148), channel_id=1, source_target_pairs={{1,0},{2,1},{3,2},{4,3},{5,4},{6,5},{7,6},{8,7},{9,8},{10,9},{11,1... | collective-permute-start | bytes 110600 | tf_op jit(solution)/shard_map/cond/branch_0_fun/ppermute | solution.py:623
  35.7 0.4 branch_0_fun.15
  36.1 0.0 collective-permute-done.6.refs_10_
  36.1 1.8 %branch_0_fun.16 = (f32[4096,128]{1,0:T(8,128)}, f32[4224,128]{1,0:T(8,128)S(1)}, f32[1024,128]{1,0:T(8,128)S(1)}, f32[4096,128]{1,0:T(8,128)S(1)}, f32[128,128]...) custom-call(s32[2]{0:T(128)S(4)} %get-tuple-element.80.refs_0_, ...), custom_call_target="tpu_custom_call", output_to_operand_aliasing={{1}: (12, {}), {2}: (13, {}), {3}: (14, {}), {6}: (3, {}), ... | custom-call | flops 3221225472 | bytes 8388608 | tf_op jit(solution)/shard_map/cond/branch_0_fun/pallas_call | solution.py:53
  37.9 1.8 %collective-permute-done.7.refs_12_ = f32[72,128]{1,0:T(8,128)S(1)} collective-permute-done((f32[72,128]{1,0:T(8,128)S(1)}, f32[72,128]{1,0:T(8,128)S(1)}, u32[]{:S(2)}, u32[]{:S(2)}) %collective-permute-start.7) | collective-permute-done | bytes 36896 | tf_op jit(solution)/shard_map/cond/branch_0_fun/ppermute | solution.py:623
  39.6 1.1 %branch_0_fun.17 = (f32[4096,128]{1,0:T(8,128)}, f32[4224,128]{1,0:T(8,128)S(1)}, f32[1024,128]{1,0:T(8,128)S(1)}, f32[4096,128]{1,0:T(8,128)S(1)}) custom-call(s32[2]{0:T(128)S(4)} %get-tuple-element.80.refs_0_, f32[8]{0:T(128)S(4)} %get-tuple-element.82.refs_1_, ...), custom_call_target="tpu_custom_call", output_to_operand_aliasing={{0}: (13, {}), {1}: (14, {}), {2}: (15, {}), {3}: (16, {})} | custom-call | flops 268435456 | bytes 1048576 | tf_op jit(solution)/shard_map/cond/branch_0_fun/pallas_call | solution.py:53
  (1 shorter events, 0.0 us)
Async XLA Ops:
  2.7 7.7 %copy-start = (f32[8]{0:T(128)S(1)}, f32[8]{0:T(128)}, u32[]{:S(2)}) copy-start(f32[8]{0:T(128)} %get-tuple-element.85) | copy-start | bytes 100 | tf_op jit(solution)/shard_map/cond
  2.7 7.8 %copy-start.4 = (f32[8]{0:T(128)S(1)}, f32[8]{0:T(128)}, u32[]{:S(2)}) copy-start(f32[8]{0:T(128)} %get-tuple-element.86) | copy-start | bytes 100 | tf_op jit(solution)/shard_map/cond
  2.7 7.7 %collective-permute-start = (f32[528,128]{1,0:T(8,128)S(1)}, f32[528,128]{1,0:T(8,128)S(1)}, u32[]{:S(2)}, u32[]{:S(2)}) collective-permute-start(f32[528,128]{1,0:T(8,128)S(1)} %get-tuple-element.93), channel_id=1, source_target_pairs={{0,12},{12,24},{24,36},{36,48},{48,60},{60,72},{72,84},{84,96},{96... | collective-permute-start | bytes 811016 | tf_op jit(solution)/shard_map/cond/branch_0_fun/ppermute | solution.py:640
  2.8 7.7 %collective-permute-start.1 = (f32[528,128]{1,0:T(8,128)S(1)}, f32[528,128]{1,0:T(8,128)S(1)}, u32[]{:S(2)}, u32[]{:S(2)}) collective-permute-start(f32[528,128]{1,0:T(8,128)S(1)} %get-tuple-element.94), channel_id=1, source_target_pairs={{0,180},{12,0},{24,12},{36,24},{48,36},{60,48},{72,60},{84,72},{96... | collective-permute-start | bytes 811016 | tf_op jit(solution)/shard_map/cond/branch_0_fun/ppermute | solution.py:641
  5.7 7.1 %collective-permute-start.4 = (f32[512,128]{1,0:T(8,128)S(1)}, f32[512,128]{1,0:T(8,128)S(1)}, u32[]{:S(2)}, u32[]{:S(2)}) collective-permute-start(f32[512,128]{1,0:T(8,128)S(1)} %get-tuple-element.107), channel_id=1, source_target_pairs={{0,12},{12,24},{24,36},{36,48},{48,60},{60,72},{72,84},{84,96},{96... | collective-permute-start | bytes 786440 | tf_op jit(solution)/shard_map/cond/branch_0_fun/ppermute | solution.py:642
  5.7 7.1 %collective-permute-start.5 = (f32[512,128]{1,0:T(8,128)S(1)}, f32[512,128]{1,0:T(8,128)S(1)}, u32[]{:S(2)}, u32[]{:S(2)}) collective-permute-start(f32[512,128]{1,0:T(8,128)S(1)} %get-tuple-element.108), channel_id=1, source_target_pairs={{0,180},{12,0},{24,12},{36,24},{48,36},{60,48},{72,60},{84,72},{96... | collective-permute-start | bytes 786440 | tf_op jit(solution)/shard_map/cond/branch_0_fun/ppermute | solution.py:643
  12.9 23.2 %collective-permute-start.6 = (f32[1104,128]{1,0:T(8,128)S(1)}, f32[1104,128]{1,0:T(8,128)S(1)}, u32[]{:S(2)}, u32[]{:S(2)}) collective-permute-start(f32[1104,128]{1,0:T(8,128)S(1)} %get-tuple-element.139), channel_id=1, source_target_pairs={{1,0},{2,1},{3,2},{4,3},{5,4},{6,5},{7,6},{8,7},{9,8},{10,9},{11,1... | collective-permute-start | bytes 1695752 | tf_op jit(solution)/shard_map/cond/branch_0_fun/ppermute | solution.py:623
  23.5 6.5 %collective-permute-start.2 = (f32[168,128]{1,0:T(8,128)S(1)}, f32[168,128]{1,0:T(8,128)S(1)}, u32[]{:S(2)}, u32[]{:S(2)}) collective-permute-start(f32[168,128]{1,0:T(8,128)S(1)} %get-tuple-element.102), channel_id=1, source_target_pairs={{0,192},{192,0},{384,576},{576,384},{1,193},{193,1},{385,577},{577... | collective-permute-start | bytes 258056 | tf_op jit(solution)/shard_map/cond/branch_0_fun/ppermute | solution.py:665
  25.4 7.6 %collective-permute-start.3 = (f32[168,128]{1,0:T(8,128)S(1)}, f32[168,128]{1,0:T(8,128)S(1)}, u32[]{:S(2)}, u32[]{:S(2)}) collective-permute-start(f32[168,128]{1,0:T(8,128)S(1)} %get-tuple-element.103), channel_id=1, source_target_pairs={{0,576},{192,384},{384,192},{576,0},{1,577},{193,385},{385,193},{5... | collective-permute-start | bytes 258056 | tf_op jit(solution)/shard_map/cond/branch_0_fun/ppermute | solution.py:666
  33.8 5.8 %collective-permute-start.7 = (f32[72,128]{1,0:T(8,128)S(1)}, f32[72,128]{1,0:T(8,128)S(1)}, u32[]{:S(2)}, u32[]{:S(2)}) collective-permute-start(f32[72,128]{1,0:T(8,128)S(1)} %get-tuple-element.148), channel_id=1, source_target_pairs={{1,0},{2,1},{3,2},{4,3},{5,4},{6,5},{7,6},{8,7},{9,8},{10,9},{11,1... | collective-permute-start | bytes 110600 | tf_op jit(solution)/shard_map/cond/branch_0_fun/ppermute | solution.py:623
